TPU v7x, 32 devices: a whole 2x2x4 slice. The times are simulated.
32 devices in a mesh: groups: 2 (over x), pen: 16 (over z, y, core).
Axes of the slice: x: 2, y: 2, z: 4, core: 2. Of those that a mesh axis runs over, the one named last changes fastest.
Arguments:
- point_feat: bfloat16 [64, 65536], P(None, ('groups', 'pen')), parts along dimension 1, may hold values from -6 to 6
- pair_kernel: bfloat16 [2048, 128, 128], P(('groups', 'pen')), parts along dimension 0, may hold values from -0.5 to 0.5
- pair_owner: int32 [2048, 1], P(('groups', 'pen')), parts along dimension 0, may hold values from 0 to 15; in each aligned block of 64 rows (0 to 63, 64 to 127, ...) at most 8 rows name the same one
- pair_block: int32 [2048], P(('groups', 'pen')), parts along dimension 0, may hold values from 0 to 255
- spec_weight: bfloat16 [2, 256, 16, 64, 128], P(None, 'pen'), may hold values from -3 to 3
- mlp_up: bfloat16 [2, 256, 64], replicated, may hold values from -0.75 to 0.75
- mlp_down: bfloat16 [2, 64, 256], replicated, may hold values from -0.375 to 0.375
Outputs:
- point_out: float32 [64, 65536], P(None, ('groups', 'pen')), parts along dimension 1
There are 2 independent parts, one for each index of `groups`. A program takes and returns all parts, laid end to end along the dimension named above; an argument that names none is the same for every part. Nothing has to cross between parts.
Inputs may be any that keep to these rules, and one draw needn't show every extreme that they name: `pair_owner`: among the pairs of one device, no device is named more than 8 times.
All inputs are finite; a program needn't handle non-finite values.
Results may differ from a plain program's by a relative error of at most 0.0055.
Values may be sent and summed in bfloat16 or wider, within the bound.
No kernel may reach another device: no remote copies, remote signals or barrier semaphores. Data moves between devices by JAX's collectives and lax.ppermute only.
A program may use at most 128 MiB of HBM per device.

v0:
```python
import math

import jax
import jax.numpy as jnp
from jax import lax
from jax.sharding import PartitionSpec as P

NX = 128
NY = 64
NZ = 64
MX = 16
MY = 16
MZ = 16
LAYERS = 2
NBR = 4


HIGHEST = lax.Precision.HIGHEST


def yz_tables():
    mode_index = jnp.arange(MY * MZ, dtype=jnp.int32)
    wave_y = mode_index // MZ - MY // 2
    wave_z = mode_index % MZ
    cell_index = jnp.arange(NY * NZ, dtype=jnp.int32)
    row_y = cell_index // NZ
    row_z = cell_index % NZ
    phase_turns = (
        jnp.mod(row_y[:, None] * wave_y[None, :], NY).astype(jnp.float32) / NY
        + jnp.mod(row_z[:, None] * wave_z[None, :], NZ).astype(jnp.float32) / NZ
    )
    angle = 2.0 * math.pi * phase_turns
    forward_table = jnp.stack([jnp.cos(angle), -jnp.sin(angle)], axis=2).reshape(
        NY * NZ, 2 * MY * MZ
    )
    scaling = jnp.where(wave_z == 0, 1.0, 2.0).astype(jnp.float32) / (NX * NY * NZ)
    inverse_table = forward_table * jnp.repeat(scaling, 2)[None, :]
    return (forward_table, inverse_table)


def along_tables(positions):
    wave_number = jnp.arange(MX, dtype=jnp.int32) - MX // 2
    angle = (
        2.0
        * math.pi
        * jnp.mod(wave_number[:, None] * positions[None, :], NX).astype(jnp.float32)
        / NX
    )
    return (jnp.cos(angle), jnp.sin(angle))


def mix_modes(modes_real, modes_imag, weight_real, weight_imag):
    mixed_real = jnp.einsum(
        "mjc,mjco->mjo", modes_real, weight_real, precision=HIGHEST
    ) - jnp.einsum("mjc,mjco->mjo", modes_imag, weight_imag, precision=HIGHEST)
    mixed_imag = jnp.einsum(
        "mjc,mjco->mjo", modes_real, weight_imag, precision=HIGHEST
    ) + jnp.einsum("mjc,mjco->mjo", modes_imag, weight_real, precision=HIGHEST)
    return (mixed_real, mixed_imag)


def unfold_modes(mixed_real, mixed_imag, cosine_table, sine_table):
    back_real = jnp.einsum("jx,mjo->oxm", cosine_table, mixed_real, precision=HIGHEST) - jnp.einsum(
        "jx,mjo->oxm", sine_table, mixed_imag, precision=HIGHEST
    )
    back_imag = jnp.einsum("jx,mjo->oxm", sine_table, mixed_real, precision=HIGHEST) + jnp.einsum(
        "jx,mjo->oxm", cosine_table, mixed_imag, precision=HIGHEST
    )
    stacked = jnp.stack([back_real, back_imag], axis=3)
    return stacked.reshape(stacked.shape[0], stacked.shape[1], 2 * stacked.shape[2])


def spectral_part(grid_field, weights_now, forward_table, inverse_table, planes):
    channels = grid_field.shape[0]
    modes_all = forward_table.shape[1] // 2
    modes_here = weights_now.shape[0]
    planar = jnp.dot(
        grid_field.reshape(channels * planes, NY * NZ), forward_table, precision=HIGHEST
    ).reshape(channels, planes, 2 * modes_all)
    weight_real = weights_now[..., :channels].astype(jnp.float32)
    weight_imag = weights_now[..., channels:].astype(jnp.float32)
    across = lax.all_to_all(planar, "pen", split_axis=2, concat_axis=1, tiled=True).reshape(
        channels, NX, modes_here, 2
    )
    cosine_table, sine_table = along_tables(jnp.arange(NX, dtype=jnp.int32))
    part_real = across[..., 0]
    part_imag = across[..., 1]
    modes_real = jnp.einsum("jx,cxm->mjc", cosine_table, part_real, precision=HIGHEST) + jnp.einsum(
        "jx,cxm->mjc", sine_table, part_imag, precision=HIGHEST
    )
    modes_imag = jnp.einsum("jx,cxm->mjc", cosine_table, part_imag, precision=HIGHEST) - jnp.einsum(
        "jx,cxm->mjc", sine_table, part_real, precision=HIGHEST
    )
    mixed_real, mixed_imag = mix_modes(modes_real, modes_imag, weight_real, weight_imag)
    joined = unfold_modes(mixed_real, mixed_imag, cosine_table, sine_table)
    result = lax.all_to_all(joined, "pen", split_axis=1, concat_axis=2, tiled=True)
    flat_result = result.reshape(channels * planes, 2 * modes_all)
    return jnp.dot(flat_result, inverse_table.T, precision=HIGHEST).reshape(
        channels, planes * NY * NZ
    )


def channel_mlp(summed, weight_up, weight_down):
    rounded = summed.astype(jnp.bfloat16)
    hidden = jnp.dot(weight_up, rounded, preferred_element_type=jnp.float32)
    active = jax.nn.gelu(hidden, approximate=True).astype(jnp.bfloat16)
    return summed + jnp.dot(weight_down, active, preferred_element_type=jnp.float32)


def per_device(point_feat, pair_kernel, pair_owner, pair_block, spec_weight, mlp_up, mlp_down):
    devices = lax.axis_size("pen")
    pair_count = pair_kernel.shape[0]
    block_size = pair_kernel.shape[1]
    channels = point_feat.shape[0]
    capacity = 2 * pair_count // devices
    slots_total = devices * capacity
    planes = NX // devices
    local_cells = planes * NY * NZ
    grid_count = local_cells // block_size
    owners = pair_owner[:, 0]
    member = (owners[:, None] == jnp.arange(devices, dtype=jnp.int32)[None, :]).astype(jnp.int32)
    earlier = jnp.sum((jnp.cumsum(member, axis=0) - member) * member, axis=1)
    slot_index = owners * capacity + earlier
    slot_target = (
        jnp.zeros((slots_total,), jnp.int32)
        .at[slot_index]
        .set(pair_block)
        .reshape(devices, capacity)
    )
    feature_blocks = point_feat.reshape(channels, pair_count // NBR, block_size).transpose(1, 0, 2)
    pair_features = jnp.repeat(feature_blocks, NBR, axis=0)
    contrib_pairs = jnp.einsum(
        "pci,pij->pcj", pair_features, pair_kernel, preferred_element_type=jnp.float32
    )
    send_sums = (
        jnp.zeros((slots_total, channels, block_size), jnp.float32)
        .at[slot_index]
        .set(contrib_pairs)
    )
    got_sums, got_targets = (
        lax.all_to_all(
            send_sums.reshape(devices, capacity, channels, block_size),
            "pen",
            split_axis=0,
            concat_axis=0,
            tiled=True,
        ),
        lax.all_to_all(slot_target, "pen", split_axis=0, concat_axis=0, tiled=True),
    )
    flat_targets = got_targets.reshape(slots_total)
    contrib = got_sums.reshape(slots_total, channels, block_size)
    grid_blocks = jax.ops.segment_sum(contrib, flat_targets, num_segments=grid_count)
    grid_field = grid_blocks.transpose(1, 0, 2).reshape(channels, local_cells)
    forward_table, inverse_table = yz_tables()
    for number in range(LAYERS):
        spectral = spectral_part(
            grid_field, spec_weight[number], forward_table, inverse_table, planes
        )
        summed = grid_field + spectral
        grid_field = channel_mlp(summed, mlp_up[number], mlp_down[number])
    grid_out = (
        grid_field.astype(jnp.bfloat16).reshape(channels, grid_count, block_size).transpose(1, 0, 2)
    )
    fetched = lax.all_to_all(
        grid_out[lax.all_to_all(slot_target, "pen", split_axis=0, concat_axis=0, tiled=True)],
        "pen",
        split_axis=0,
        concat_axis=0,
        tiled=True,
    )
    pair_rows = fetched.reshape(slots_total, channels, block_size)[slot_index]
    pair_results = jnp.einsum(
        "pcj,pij->pci", pair_rows, pair_kernel, preferred_element_type=jnp.float32
    )
    summed_back = pair_results.reshape(pair_count // NBR, NBR, channels, block_size).sum(axis=1)
    return summed_back.transpose(1, 0, 2).reshape(channels, pair_count // NBR * block_size)


def solution(mesh):
    in_specs = (
        P(None, ("groups", "pen")),
        P(("groups", "pen"), None, None),
        P(("groups", "pen"), None),
        P(("groups", "pen")),
        P(None, "pen", None, None, None),
        P(),
        P(),
    )
    out_specs = P(None, ("groups", "pen"))
    return jax.shard_map(
        per_device, mesh=mesh, in_specs=in_specs, out_specs=out_specs, check_vma=False
    )
```

profile of v0, /device:TPU:1, one launch (start us, length us, event | category | flops | bytes accessed | tf_op | source)
XLA Modules:
  0.0 649.2 jit_solution(12362412406866547493)
XLA Ops:
  4.1 7.3 %all-to-all-start = ((s32[16,1,8]{2,1,0:T(1,128)}), s32[16,1,8]{2,1,0:T(1,128)S(1)}, u32[]{:S(2)}, u32[]{:S(2)}) async-start(s32[16,1,8]{2,1,0:T(1,128)} %bitcast.3), calls=%async_computation | async-start | bytes 16384 | tf_op jit(solution)/shard_map/all_to_all | solution.py:148
  14.8 2.5 broadcast_in_dim.18
  17.3 10.1 %scatter_fusion = f32[128,64,128]{2,1,0:T(8,128)} fusion(f32[128,64,128]{2,1,0:T(8,128)} %broadcast_in_dim.18, s32[64]{0:T(128)S(1)} %fusion.155, f32[64,64,128]{2,1,0:T(8,128)} %fusion.232), kind=kCustom, calls=%fused_computation.3 | custom fusion | bytes 6291712 | tf_op jit(solution)/shard_map/scatter | solution.py:138
  27.4 6.4 all-to-all-start.1
  33.8 18.7 %fusion.58 = (f32[4096,256,1]{1,0,2:T(8,128)S(1)}, f32[4096,256,1]{1,0,2:T(8,128)S(1)}) fusion(s32[256]{0:T(256)S(1)} %get-tuple-element.17, s32[4096]{0:T(1024)S(1)} %get-tuple-element.15, s32[256]{0:T(256)S(1)} %get-tuple-element.18, s32[4096]{0:T(1024)S(1)} %get-tuple-element.16), kind=kLoop, calls=%fused_computation.82 | loop fusion | flops 30408704 | bytes 8423424 | tf_op jit(solution)/shard_map/cos | solution.py:33
  52.5 6.5 broadcast_multiply_fusion
  59.0 13.4 %copy.142 = f32[4096,256,2]{0,2,1:T(2,128)} copy(f32[4096,256,2]{1,0,2:T(8,128)} %get-tuple-element.8) | data formatting | bytes 16777216 | tf_op jit(solution)/shard_map/stack | solution.py:33
  72.4 11.1 %reshape.465 = f32[4096,512]{0,1:T(8,128)} reshape(f32[4096,256,2]{0,2,1:T(2,128)} %copy.142) | data formatting | bytes 16777216 | tf_op jit(solution)/shard_map/reshape | solution.py:33
  84.7 27.0 %all-to-all-done.1 = f32[16,8,64,128]{3,2,1,0:T(8,128)} async-done(((f32[16,8,64,128]{3,2,1,0:T(8,128)}), f32[16,8,64,128]{3,2,1,0:T(8,128)}, u32[]{:S(2)}, u32[]{:S(2)}) %all-to-all-start.1) | async-done | bytes 4194336 | tf_op jit(solution)/shard_map/all_to_all | solution.py:141
  111.7 4.3 broadcast_in_dim.16
  116.0 22.3 %scatter_fusion.1 = f32[256,64,128]{2,1,0:T(8,128)} fusion(f32[256,64,128]{2,1,0:T(8,128)} %broadcast_in_dim.16, s32[128]{0:T(128)S(1)} %reshape.513, f32[128,64,128]{2,1,0:T(8,128)} %bitcast.7), kind=kCustom, calls=%fused_computation.4 | custom fusion | flops 1048576 | bytes 12583424 | tf_op jit(solution)/shard_map/scatter-add | solution.py:152
  138.4 11.5 %copy.140 = f32[64,256,128]{2,1,0:T(8,128)} copy(f32[64,256,128]{2,0,1:T(8,128)} %bitcast.268) | data formatting | bytes 16777216 | tf_op jit(solution)/shard_map/transpose | solution.py:153
  149.8 9.3 %dot_general.115 = f32[64,8,4096]{2,1,0:T(8,128)} reshape(f32[64,256,128]{2,1,0:T(8,128)} %copy.140) | data formatting | bytes 16777216 | tf_op jit(solution)/shard_map/dot_general | solution.py:77
  159.2 16.4 %fusion.21 = f32[64,8,512]{2,1,0:T(8,128)S(1)} fusion(f32[64,8,4096]{2,1,0:T(8,128)} %dot_general.115, f32[4096,512]{0,1:T(8,128)} %reshape.465), kind=kOutput, calls=%fused_computation.34 | convolution fusion | flops 12884901888 | bytes 17825792 | tf_op jit(solution)/shard_map/dot_general | solution.py:77
  175.5 2.3 copy.144
  177.9 3.8 reshape.548
  181.7 19.5 %all-to-all-start.2 = ((f32[16,1,16384]{2,1,0:T(1,128)}), f32[16,1,16384]{2,1,0:T(1,128)S(1)}, u32[]{:S(2)}, u32[]{:S(2)}) async-start(f32[16,1,16384]{2,1,0:T(1,128)} %reshape.548), calls=%async_computation.2 | async-start | bytes 2097152 | tf_op jit(solution)/shard_map/all_to_all | solution.py:82
  201.2 6.9 %slice_bitcast_fusion = (bf16[16,16,64,128]{3,2,1,0:T(8,128)(2,1)}, bf16[16,16,64,128]{3,2,1,0:T(8,128)(2,1)}) fusion(bf16[2,16,16,64,128]{4,3,2,1,0:T(8,128)(2,1)} %param.11), kind=kLoop, calls=%fused_computation.60 | loop fusion | bytes 16777216 | tf_op jit(solution)/shard_map/squeeze | solution.py:157
  208.1 16.2 %all-to-all-done.2 = f32[16,1,16384]{2,1,0:T(1,128)S(1)} async-done(((f32[16,1,16384]{2,1,0:T(1,128)}), f32[16,1,16384]{2,1,0:T(1,128)S(1)}, u32[]{:S(2)}, u32[]{:S(2)}) %all-to-all-start.2) | async-done | bytes 1048608 | tf_op jit(solution)/shard_map/all_to_all | solution.py:82
  225.9 4.3 reduce.4
  230.2 2.2 reshape.549
  243.8 5.5 fusion.51
  249.3 3.6 fusion.49
  253.8 5.8 fusion.47
  259.7 3.4 fusion.53
  267.4 2.8 copy.150
  270.2 3.4 reshape.550
  273.7 7.1 %all-to-all-start.3 = ((f32[16,1,16384]{2,1,0:T(1,128)}), f32[16,1,16384]{2,1,0:T(1,128)}, u32[]{:S(2)}, u32[]{:S(2)}) async-start(f32[16,1,16384]{2,1,0:T(1,128)} %reshape.550), calls=%async_computation.3 | async-start | bytes 2097152 | tf_op jit(solution)/shard_map/all_to_all | solution.py:96
  280.7 13.4 %copy.152 = f32[4096,256,2]{0,2,1:T(2,128)} copy(f32[4096,256,2]{1,0,2:T(8,128)} %get-tuple-element.7) | data formatting | bytes 16777216 | tf_op jit(solution)/shard_map/mul | solution.py:37
  294.2 10.9 %mul.262 = f32[4096,512]{0,1:T(8,128)} reshape(f32[4096,256,2]{0,2,1:T(2,128)} %copy.152) | data formatting | bytes 16777216 | tf_op jit(solution)/shard_map/mul | solution.py:37
  305.0 4.3 reduce.5
  311.5 5.7 copy.151
  317.2 3.5 reshape.468
  320.7 17.3 %fusion.233 = f32[512,4096]{1,0:T(8,128)} fusion(f32[512,512]{1,0:T(8,128)S(1)} %reshape.468, f32[4096,512]{0,1:T(8,128)} %mul.262), kind=kOutput, calls=%fused_computation.269 | convolution fusion | flops 12884901888 | bytes 17825792 | tf_op jit(solution)/shard_map/dot_general | solution.py:98
  338.0 9.3 %reshape.470 = f32[64,256,128]{2,1,0:T(8,128)} reshape(f32[512,4096]{1,0:T(8,128)} %fusion.233) | data formatting | bytes 16777216 | tf_op jit(solution)/shard_map/reshape | solution.py:98
  347.3 9.4 %reshape.469 = f32[64,32768]{1,0:T(8,128)} reshape(f32[512,4096]{1,0:T(8,128)} %fusion.233) | data formatting | bytes 16777216 | tf_op jit(solution)/shard_map/reshape | solution.py:98
  356.7 30.0 %fusion = f32[64,32768]{1,0:T(8,128)} fusion(f32[64,32768]{1,0:T(8,128)} %reshape.469, bf16[2,64,256]{2,1,0:T(8,128)(2,1)S(1)} %copy-done.10, bf16[2,256,64]{1,2,0:T(8,128)(2,1)S(1)} %copy-done.11, f32[256,64,128]{2,1,0:T(8,128)} %scatter_fusion.1, f32[64,256,128]{2,1,0:T(8,128)} %reshape.470), kind=kOutput, calls=%fused_computation.11 | convolution fusion | flops 2231369728 | bytes 42008576 | tf_op jit(solution)/shard_map/dot_general | solution.py:107
  386.7 8.1 %copy.195 = f32[8,8,8,4096]{3,2,1,0:T(8,128)S(1)} copy(f32[8,8,8,4096]{3,1,2,0:T(8,128)} %bitcast.278) | data formatting | bytes 16777216
  394.8 16.0 %fusion.19 = f32[64,8,512]{2,1,0:T(8,128)S(1)} fusion(f32[64,8,4096]{2,1,0:T(8,128)S(1)} %bitcast.269, f32[4096,512]{0,1:T(8,128)} %reshape.465), kind=kOutput, calls=%fused_computation.32 | convolution fusion | flops 12884901888 | bytes 17825792 | tf_op jit(solution)/shard_map/dot_general | solution.py:77
  410.8 2.3 copy.156
  413.2 2.6 reshape.552
  415.8 31.4 %all_to_all.83 = f32[16,1,16384]{2,1,0:T(1,128)} all-to-all(f32[16,1,16384]{2,1,0:T(1,128)S(1)} %reshape.552), channel_id=1, replica_groups=mesh['groups'=2,'pen'=16] {'pen'}, dimensions={0} | all-to-all | bytes 2097152 | tf_op jit(solution)/shard_map/all_to_all | solution.py:82
  447.3 4.3 reduce.6
  451.6 2.2 reshape.553
  465.2 5.8 fusion.43
  471.0 3.6 fusion.41
  475.6 5.8 fusion.39
  481.4 3.4 fusion.45
  489.1 2.8 copy.162
  492.0 3.4 reshape.554
  495.4 4.8 all-to-all-start.5
  500.5 22.9 %all-to-all-done.5 = f32[16,1,16384]{2,1,0:T(1,128)} async-done(((f32[16,1,16384]{2,1,0:T(1,128)}), f32[16,1,16384]{2,1,0:T(1,128)}, u32[]{:S(2)}, u32[]{:S(2)}) %all-to-all-start.5) | async-done | bytes 1048608 | tf_op jit(solution)/shard_map/all_to_all | solution.py:96
  523.4 4.3 reduce.7
  527.7 2.2 reshape.555
  529.9 5.7 copy.163
  535.5 3.5 reshape.473
  539.1 17.3 %fusion.234 = f32[512,4096]{1,0:T(8,128)} fusion(f32[512,512]{1,0:T(8,128)S(1)} %reshape.473, f32[4096,512]{0,1:T(8,128)} %mul.262), kind=kOutput, calls=%fused_computation.270 | convolution fusion | flops 12884901888 | bytes 17825792 | tf_op jit(solution)/shard_map/dot_general | solution.py:98
  556.4 9.4 %reshape.474 = f32[64,32768]{1,0:T(8,128)} reshape(f32[512,4096]{1,0:T(8,128)} %fusion.234) | data formatting | bytes 16777216 | tf_op jit(solution)/shard_map/reshape | solution.py:98
  565.8 20.8 %fusion.55 = bf16[8,256,8,128]{3,2,1,0:T(8,128)(2,1)} fusion(f32[64,32768]{1,0:T(8,128)} %fusion, f32[64,32768]{1,0:T(8,128)} %reshape.474, bf16[2,64,256]{2,1,0:T(8,128)(2,1)S(1)} %copy-done.10, bf16[2,256,64]{1,2,0:T(8,128)(2,1)S(1)} %copy-done.11), kind=kOutput, calls=%fused_computation.80 | convolution fusion | flops 2233466880 | bytes 37814272 | tf_op jit(solution)/shard_map/dot_general | solution.py:107
  586.5 5.3 copy.212
  591.9 4.3 gather_fusion
  596.2 6.5 %all-to-all-start.6 = ((bf16[16,8,64,128]{3,2,1,0:T(8,128)(2,1)}), bf16[16,8,64,128]{3,2,1,0:T(8,128)(2,1)}, u32[]{:S(2)}, u32[]{:S(2)}) async-start(bf16[16,8,64,128]{3,2,1,0:T(8,128)(2,1)} %bitcast.279), calls=%async_computation.6 | async-start | bytes 4194304 | tf_op jit(solution)/shard_map/all_to_all | solution.py:164
  602.7 41.6 %all-to-all-done.6 = bf16[16,8,64,128]{3,2,1,0:T(8,128)(2,1)} async-done(((bf16[16,8,64,128]{3,2,1,0:T(8,128)(2,1)}), bf16[16,8,64,128]{3,2,1,0:T(8,128)(2,1)}, u32[]{:S(2)}, u32[]{:S(2)}) %all-to-all-start.6) | async-done | bytes 2097184 | tf_op jit(solution)/shard_map/all_to_all | solution.py:164
  644.3 2.3 gather_fusion.1
  (85 shorter events, 48.3 us)
Async XLA Ops:
  0.0 12.7 %copy-start = (bf16[64,128,128]{2,1,0:T(8,128)(2,1)S(1)}, bf16[64,128,128]{2,1,0:T(8,128)(2,1)}, u32[]{:S(2)}) copy-start(bf16[64,128,128]{2,1,0:T(8,128)(2,1)} %param.8) | copy-start | bytes 6291460
  2.5 14.8 %copy-start.8 = (s32[64]{0:T(128)}, s32[64]{0:T(128)S(1)}, u32[]{:S(2)}) copy-start(s32[64]{0:T(128)S(1)} %fusion.155) | copy-start | bytes 772
  4.1 23.3 %all-to-all-start = ((s32[16,1,8]{2,1,0:T(1,128)}), s32[16,1,8]{2,1,0:T(1,128)S(1)}, u32[]{:S(2)}, u32[]{:S(2)}) async-start(s32[16,1,8]{2,1,0:T(1,128)} %bitcast.3), calls=%async_computation | async-start | bytes 16384 | tf_op jit(solution)/shard_map/all_to_all | solution.py:148
  27.4 84.3 %all-to-all-start.1 = ((f32[16,8,64,128]{3,2,1,0:T(8,128)}), f32[16,8,64,128]{3,2,1,0:T(8,128)}, u32[]{:S(2)}, u32[]{:S(2)}) async-start(f32[16,8,64,128]{3,2,1,0:T(8,128)} %bitcast.270), calls=%async_computation.1 | async-start | bytes 8388608 | tf_op jit(solution)/shard_map/all_to_all | solution.py:141
  181.7 42.7 %all-to-all-start.2 = ((f32[16,1,16384]{2,1,0:T(1,128)}), f32[16,1,16384]{2,1,0:T(1,128)S(1)}, u32[]{:S(2)}, u32[]{:S(2)}) async-start(f32[16,1,16384]{2,1,0:T(1,128)} %reshape.548), calls=%async_computation.2 | async-start | bytes 2097152 | tf_op jit(solution)/shard_map/all_to_all | solution.py:82
  224.4 1.0 copy-start.1
  243.8 5.5 copy-start.4
  243.8 9.1 %copy-start.7 = (f32[64,16,16]{2,1,0:T(8,128)S(1)}, f32[64,16,16]{2,1,0:T(8,128)}, u32[]{:S(2)}) copy-start(f32[64,16,16]{2,1,0:T(8,128)} %fusion.77) | copy-start | bytes 196612
  253.8 5.8 copy-start.5
  273.7 31.4 %all-to-all-start.3 = ((f32[16,1,16384]{2,1,0:T(1,128)}), f32[16,1,16384]{2,1,0:T(1,128)}, u32[]{:S(2)}, u32[]{:S(2)}) async-start(f32[16,1,16384]{2,1,0:T(1,128)} %reshape.550), calls=%async_computation.3 | async-start | bytes 2097152 | tf_op jit(solution)/shard_map/all_to_all | solution.py:96
  347.3 9.4 %copy-start.10 = (bf16[2,64,256]{2,1,0:T(8,128)(2,1)S(1)}, bf16[2,64,256]{2,1,0:T(8,128)(2,1)}, u32[]{:S(2)}) copy-start(bf16[2,64,256]{2,1,0:T(8,128)(2,1)} %param.13) | copy-start | bytes 196612
  347.3 9.4 %copy-start.11 = (bf16[2,256,64]{1,2,0:T(8,128)(2,1)S(1)}, bf16[2,256,64]{1,2,0:T(8,128)(2,1)}, u32[]{:S(2)}) copy-start(bf16[2,256,64]{1,2,0:T(8,128)(2,1)} %param.12) | copy-start | bytes 196612
  465.2 5.8 copy-start.2
  465.2 9.4 %copy-start.6 = (f32[64,16,16]{2,1,0:T(8,128)S(1)}, f32[64,16,16]{2,1,0:T(8,128)}, u32[]{:S(2)}) copy-start(f32[64,16,16]{2,1,0:T(8,128)} %fusion.71) | copy-start | bytes 196612
  475.6 5.8 copy-start.3
  495.4 28.0 %all-to-all-start.5 = ((f32[16,1,16384]{2,1,0:T(1,128)}), f32[16,1,16384]{2,1,0:T(1,128)}, u32[]{:S(2)}, u32[]{:S(2)}) async-start(f32[16,1,16384]{2,1,0:T(1,128)} %reshape.554), calls=%async_computation.5 | async-start | bytes 2097152 | tf_op jit(solution)/shard_map/all_to_all | solution.py:96
  591.9 10.8 %copy-start.9 = (s32[64]{0:T(128)S(1)}, s32[64]{0:T(128)}, u32[]{:S(2)}) copy-start(s32[64]{0:T(128)} %copy-done.8) | copy-start | bytes 772
  596.2 48.1 %all-to-all-start.6 = ((bf16[16,8,64,128]{3,2,1,0:T(8,128)(2,1)}), bf16[16,8,64,128]{3,2,1,0:T(8,128)(2,1)}, u32[]{:S(2)}, u32[]{:S(2)}) async-start(bf16[16,8,64,128]{3,2,1,0:T(8,128)(2,1)} %bitcast.279), calls=%async_computation.6 | async-start | bytes 4194304 | tf_op jit(solution)/shard_map/all_to_all | solution.py:164
where the time goes:
time: 660 us; the launch traced here: 649 us
  local copies, waits for them, and re-layouts  215 us (33%)
  matrix products  175 us (27%)
  waiting for transfers between devices  108 us (16%)
  other arithmetic  68.2 us (10%)
  starting transfers between devices  51.5 us (8%)
  blocking collectives  31.4 us (5%)
    dot_general x2, matrix products, channel_mlp(): jnp.dot(weight_down, active, preferred_element_type=jnp.float32)  50.8 us
    all_to_all x1, waiting for transfers between devices, per_device(): lax.all_to_all(grid_out[lax.all_to_all(slot_target, 'pen', split_axis=0,...  41.6 us
    unnamed x38, local copies, waits for them, and re-layouts  38.6 us
    dot_general x2, matrix products, spectral_part(): jnp.dot(flat_result, inverse_table.T, precision=HIGHEST)  34.6 us
    dot_general x2, matrix products, spectral_part(): jnp.dot(grid_field.reshape(channels * planes, NY * NZ), forward_table, pr...  32.4 us
    all_to_all x1, blocking collectives, spectral_part(): lax.all_to_all(planar, 'pen', split_axis=2, concat_axis=1, tiled=True)  31.4 us
    reshape x3, local copies, waits for them, and re-layouts, spectral_part(): jnp.dot(flat_result, inverse_table.T, precision=HIGHEST)  28.1 us
    all_to_all x1, waiting for transfers between devices, per_device(): lax.all_to_all(send_sums.reshape(devices, capacity, channels, block_size)...  27 us
  transfers between devices with their start and end apart: 6, of which 4 were waited for; matrix products, arithmetic and copies ran while one was open for 15% of the time, Pallas kernels for 0%

commit v1 on v0

v1 whole, which is shorter than its diff:
```python
import functools
import math

import jax
import jax.numpy as jnp
import numpy as np
from jax import lax
from jax.experimental import pallas as pl
from jax.experimental.pallas import tpu as pltpu
from jax.sharding import PartitionSpec as P

NX = 128
NY = 64
NZ = 64
MX = 16
MY = 16
MZ = 16
LAYERS = 2
NBR = 4
GELU_K = math.sqrt(2.0 / math.pi)
SCALE = 1.66575

F32 = jnp.float32
BF16 = jnp.bfloat16


def vmem_spec():
    return pl.BlockSpec(memory_space=pltpu.VMEM)


def cost(flops, size, transcendentals=0):
    return pl.CostEstimate(
        flops=int(flops), bytes_accessed=int(size), transcendentals=int(transcendentals)
    )


def dot(left, right):
    return jnp.dot(left, right, preferred_element_type=F32)


def column_waves(devices, modes_here):
    column = np.arange(devices * 2 * MX)
    wave_y = (column // (2 * MX) * modes_here) // MZ - MY // 2
    return wave_y, column // MX % 2, column % MX - MX // 2


def line_tables(devices, modes_here):
    wave_y, part, wave_x = column_waves(devices, modes_here)
    x_angle = 2.0 * np.pi / NX * (np.arange(NX)[:, None] * wave_x % NX)
    y_angle = 2.0 * np.pi / NY * (np.arange(NY)[:, None] * wave_y % NY)
    x_cos, x_sin = SCALE * np.cos(x_angle), SCALE * np.sin(x_angle)
    first = np.where(part == 0, x_cos, -x_sin)
    second = np.where(part == 0, -x_sin, -x_cos)
    return [
        jnp.asarray(each.astype(np.float32))
        for each in (first, second, np.cos(y_angle), np.sin(y_angle))
    ]


def split(values):
    high = values.astype(BF16)
    return high, (values - high.astype(F32)).astype(BF16)


def depth_tables(devices, modes_here):
    local = NZ // devices
    wave_z = np.arange(MZ).reshape(MZ // modes_here, modes_here)
    z_of = np.arange(devices)[None, :] * local + np.arange(local)[:, None]
    angle = 2.0 * np.pi / NZ * (z_of[None, :, :, None] * wave_z[:, None, None, :] % NZ)
    cosine, sine = np.cos(angle), np.sin(angle)
    to_real = np.stack([cosine, sine], axis=-1)
    to_imag = np.stack([-sine, cosine], axis=-1)
    forward = np.stack([to_real, to_imag], axis=-2) / SCALE
    forward = forward.transpose(0, 1, 3, 4, 2, 5).reshape(
        -1, local * modes_here * 2, devices * 2
    )
    scale = np.where(wave_z == 0, 1.0, 2.0)[:, None, None, :] / (NX * NY * NZ * SCALE)
    cosine, sine = cosine * scale, sine * scale
    low = np.stack(
        [np.stack([cosine, -sine], axis=-1), np.stack([sine, cosine], axis=-1)], axis=3
    ).reshape(-1, local * devices * 2, modes_here * 2)
    high = np.stack(
        [np.stack([-sine, -cosine], axis=-1), np.stack([cosine, -sine], axis=-1)], axis=3
    ).reshape(-1, local * devices * 2, modes_here * 2)
    inverse = np.concatenate([low, high], axis=2)
    which = lax.axis_index("pen") * modes_here % MZ // modes_here
    chosen = []
    for table in (forward, inverse):
        table = jnp.asarray(table.astype(np.float32))
        chosen.append(table[0] if table.shape[0] == 1 else table[which])
    forward, inverse = chosen
    return jnp.concatenate(split(forward), axis=1), jnp.concatenate(split(inverse), axis=1)


def table_kernel(first_ref, second_ref, cos_ref, sin_ref, table_ref, flipped_ref):
    pieces = []
    for line in range(first_ref.shape[0]):
        piece = (
            first_ref[line : line + 1, :] * cos_ref[...]
            + second_ref[line : line + 1, :] * sin_ref[...]
        )
        pieces.append(piece.astype(BF16))
    whole = jnp.concatenate(pieces, axis=0)
    table_ref[...] = whole
    flipped_ref[...] = whole.T


def grid_tables(devices, modes_here):
    first, second, y_cos, y_sin = line_tables(devices, modes_here)
    columns = first.shape[1]
    lines = 8
    rows = lines * NY
    const = lambda i: (0, 0)
    return pl.pallas_call(
        table_kernel,
        out_shape=(
            jax.ShapeDtypeStruct((NX * NY, columns), BF16),
            jax.ShapeDtypeStruct((columns, NX * NY), BF16),
        ),
        grid=(NX // lines,),
        in_specs=[
            pl.BlockSpec((lines, columns), lambda i: (i, 0)),
            pl.BlockSpec((lines, columns), lambda i: (i, 0)),
            pl.BlockSpec((NY, columns), const),
            pl.BlockSpec((NY, columns), const),
        ],
        out_specs=(
            pl.BlockSpec((rows, columns), lambda i: (i, 0)),
            pl.BlockSpec((columns, rows), lambda i: (0, i)),
        ),
        cost_estimate=cost(4 * NX * NY * columns, 4 * NX * NY * columns),
        name="tables",
    )(first, second, y_cos, y_sin)


def encode_kernel(feature_ref, weight_ref, spot_ref, out_ref, wide_ref, turned_ref):
    devices = out_ref.shape[0]
    pairs, block = weight_ref.shape[0], weight_ref.shape[1]
    lines = block // NZ
    local = NZ // devices
    tiles = local // 2
    rows = tiles * pairs * lines
    lane = lax.broadcasted_iota(jnp.int32, (lines * devices, 128), 1)

    def one(point, carry):
        features = feature_ref[:, pl.ds(pl.multiple_of(point * block, block), block)]
        features = jnp.concatenate([features, features], axis=0)
        for near in range(NBR):
            pair = point * NBR + near
            turned_ref[near] = lax.dot_general(
                weight_ref[pair], features, (((0,), (1,)), ((), ())), preferred_element_type=F32
            )
            for tile in range(tiles):
                even = turned_ref[near, pl.ds(2 * tile, lines * devices, stride=local), :]
                odd = turned_ref[near, pl.ds(2 * tile + 1, lines * devices, stride=local), :]
                both = jnp.where(lane < 64, even, odd)
                for line in range(lines):
                    wide_ref[
                        pl.ds(tile * pairs * lines + pair * lines + line, devices, stride=rows), :
                    ] = both[line * devices : (line + 1) * devices, :]
        return carry

    lax.fori_loop(0, pairs // NBR, one, 0)
    for device in range(devices):
        out_ref[device, 0:rows, :] = wide_ref[device * rows : (device + 1) * rows, :].astype(BF16)
        out_ref[device, rows : rows + 8, :] = spot_ref[...].astype(BF16)


def encode(features, weights, spots, devices):
    pairs, block = weights.shape[0], weights.shape[1]
    rows = NZ // devices // 2 * pairs * (block // NZ)
    return pl.pallas_call(
        encode_kernel,
        out_shape=jax.ShapeDtypeStruct((devices, rows + 8, 128), BF16),
        in_specs=[vmem_spec()] * 3,
        out_specs=vmem_spec(),
        scratch_shapes=[
            pltpu.VMEM((devices * rows, 128), F32),
            pltpu.VMEM((NBR, block, 128), F32),
        ],
        cost_estimate=cost(4 * pairs * block * block * 64, pairs * block * block * 2),
        name="encode",
    )(features, weights, spots)


def decode_kernel(got_ref, weight_ref, out_ref, wide_ref, turned_ref):
    devices, rows, _ = got_ref.shape
    pairs, block = weight_ref.shape[0], weight_ref.shape[1]
    lines = block // NZ
    local = NZ // devices
    tiles = local // 2
    lane = lax.broadcasted_iota(jnp.int32, (block, 128), 1)
    row = lax.broadcasted_iota(jnp.int32, (block, 128), 0)
    keep = lane // 64 == row % 2
    for device in range(devices):
        wide_ref[device * rows : (device + 1) * rows, :] = got_ref[device].astype(F32)

    def one(point, carry):
        total = None
        for near in range(NBR):
            pair = point * NBR + near
            for tile in range(tiles):
                for line in range(lines):
                    values = wide_ref[
                        pl.ds(tile * pairs * lines + pair * lines + line, devices, stride=rows), :
                    ]
                    for side in range(2):
                        turned_ref[
                            near, pl.ds(line * NZ + tile * 2 + side, devices, stride=local), :
                        ] = values
            left = jnp.where(keep, turned_ref[near], 0.0).astype(BF16)
            part = lax.dot_general(
                left, weight_ref[pair], (((0,), (1,)), ((), ())), preferred_element_type=F32
            )
            total = part if total is None else total + part
        out_ref[:, pl.ds(pl.multiple_of(point * block, block), block)] = (
            total[0:64, :] + total[64:128, :]
        )
        return carry

    lax.fori_loop(0, pairs // NBR, one, 0)


def decode(got, weights, channels):
    devices, rows, _ = got.shape
    pairs, block = weights.shape[0], weights.shape[1]
    return pl.pallas_call(
        decode_kernel,
        out_shape=jax.ShapeDtypeStruct((channels, pairs // NBR * block), F32),
        in_specs=[vmem_spec()] * 2,
        out_specs=vmem_spec(),
        scratch_shapes=[
            pltpu.VMEM((devices * rows, 128), F32),
            pltpu.VMEM((NBR, block, 128), F32),
        ],
        cost_estimate=cost(4 * pairs * block * block * 64, pairs * block * block * 2),
        name="decode",
    )(got, weights)


def pair_spectrum_kernel(modes_here, got_ref, out_ref, phase_ref):
    devices = got_ref.shape[0]
    rows = got_ref.shape[1] - 8
    tiles = out_ref.shape[1] // 128
    lanes = rows // tiles
    wave_x = lax.broadcasted_iota(jnp.int32, (MX, lanes), 0) - MX // 2
    wave_y = lax.broadcasted_iota(jnp.int32, (MY, lanes), 0) - MY // 2
    for source in range(devices):
        spot = got_ref[source, rows : rows + 8, :].astype(F32)
        x_at = spot[0:1, :].astype(jnp.int32)
        y_at = spot[1:2, :].astype(jnp.int32)
        x_angle = (2.0 * math.pi / NX) * ((wave_x * x_at) & (NX - 1)).astype(F32)
        y_angle = (2.0 * math.pi / NY) * ((wave_y * y_at) & (NY - 1)).astype(F32)
        x_cos, x_sin = SCALE * jnp.cos(x_angle), SCALE * jnp.sin(x_angle)
        y_cos, y_sin = jnp.cos(y_angle), jnp.sin(y_angle)
        place = slice(source * lanes, (source + 1) * lanes)
        for device in range(devices):
            row = (device * modes_here) // MZ
            cos_now, sin_now = y_cos[row : row + 1, :], y_sin[row : row + 1, :]
            base = device * 2 * MX
            phase_ref[base : base + MX, place] = (x_cos * cos_now - x_sin * sin_now).astype(BF16)
            phase_ref[base + MX : base + 2 * MX, place] = (
                -x_sin * cos_now - x_cos * sin_now
            ).astype(BF16)
    values = jnp.concatenate(
        [
            jnp.concatenate(
                [
                    got_ref[source, tile * lanes : (tile + 1) * lanes, :]
                    for source in range(devices)
                ],
                axis=0,
            )
            for tile in range(tiles)
        ],
        axis=1,
    )
    out_ref[...] = dot(phase_ref[...], values).astype(BF16)


def pair_spectrum(got, modes_here, lanes):
    devices, rows, _ = got.shape
    count = devices * (rows - 8) // (lanes // 128)
    columns = devices * 2 * MX
    return pl.pallas_call(
        functools.partial(pair_spectrum_kernel, modes_here),
        out_shape=(
            jax.ShapeDtypeStruct((columns, lanes), BF16),
            jax.ShapeDtypeStruct((columns, count), BF16),
        ),
        in_specs=[vmem_spec()],
        out_specs=(vmem_spec(), vmem_spec()),
        cost_estimate=cost(2 * columns * count * lanes, got.size * 2 + columns * count * 2),
        name="pair_spectrum",
    )(got)


def mix_kernel(
    devices, number, got_ref, forward_ref, inverse_ref, all_ref, out_ref, wide_ref, back_ref,
    weight_ref, sem_ref
):
    modes_here, _, channels, _ = weight_ref.shape
    pieces_at = [slice(first, first + 4) for first in range(0, MX, 4)]
    copies = [
        pltpu.make_async_copy(
            all_ref.at[number, :, place], weight_ref.at[:, place], sem_ref.at[index]
        )
        for index, place in enumerate(pieces_at)
    ]
    for copy in copies:
        copy.start()
    local = got_ref.shape[1] // channels
    tiles = got_ref.shape[1] // 128
    group = 8
    for tile in range(tiles):
        wide_ref[tile] = got_ref[:, tile * 128 : (tile + 1) * 128].astype(F32)
    lane = lax.broadcasted_iota(jnp.int32, (2 * modes_here, 128), 1)
    row = lax.broadcasted_iota(jnp.int32, (2 * group, 128), 0)
    lane_small = lax.broadcasted_iota(jnp.int32, (2 * group, 128), 1)
    lane_back = lax.broadcasted_iota(jnp.int32, (2 * devices, 128), 1)
    forward = forward_ref[...]
    inverse = inverse_ref[...]
    spread = []
    for wave in range(MX):
        planes = jnp.concatenate(
            [wide_ref[tile, pl.ds(wave, 2 * devices, stride=MX), :] for tile in range(tiles)],
            axis=1,
        ).astype(BF16)
        turned = dot(forward, jnp.concatenate([planes, planes], axis=0))
        total = None
        for tile in range(tiles):
            part = slice(tile * 128, (tile + 1) * 128)
            size = 2 * modes_here
            even = turned[2 * tile * size : (2 * tile + 1) * size, part]
            odd = turned[(2 * tile + 1) * size : (2 * tile + 2) * size, part]
            both = even + pltpu.roll(odd, 64, 1)
            total = both if total is None else total + both
        spread.append(jnp.where(lane < 64, total, pltpu.roll(total, 64, 1)))
    mixed = []
    for wave in range(MX):
        pieces = []
        if wave % 4 == 0:
            copies[wave // 4].wait()
        for first in range(0, modes_here, group):
            now = spread[wave][2 * first : 2 * (first + group), :]
            left = jnp.concatenate(
                [
                    jnp.where(row // 2 == 2 * step + lane_small // 64, now, 0.0)
                    for step in range(group // 2)
                ],
                axis=1,
            )
            left = jnp.concatenate(split(left), axis=0)
            right = weight_ref[first : first + group, wave, :, :].reshape(
                group * channels, 2 * channels
            )
            both = dot(left, right)
            pieces.append(both[0 : 2 * group] + both[2 * group :])
        mixed.append(pieces[0] if len(pieces) == 1 else jnp.concatenate(pieces, axis=0))
    for wave in range(MX):
        stacked = jnp.concatenate([mixed[wave], pltpu.roll(mixed[wave], 64, 1)], axis=0)
        upper, lower = split(stacked)
        count = upper.shape[0]
        planes = dot(inverse, jnp.concatenate([upper, upper], axis=0)) + dot(
            inverse[:, 0:count], lower
        )
        size = 2 * devices
        for tile in range(tiles):
            even = planes[2 * tile * size : (2 * tile + 1) * size, :]
            odd = planes[(2 * tile + 1) * size : (2 * tile + 2) * size, :]
            back_ref[tile, pl.ds(wave, size, stride=MX), :] = jnp.where(
                lane_back < 64, even, pltpu.roll(odd, 64, 1)
            )
    for tile in range(tiles):
        out_ref[:, tile * 128 : (tile + 1) * 128] = back_ref[tile].astype(BF16)


def mix(got, forward, inverse, weights, number, devices):
    rows, lanes = got.shape
    return pl.pallas_call(
        functools.partial(mix_kernel, devices, number),
        out_shape=jax.ShapeDtypeStruct((rows, lanes), BF16),
        in_specs=[vmem_spec()] * 3 + [pl.BlockSpec(memory_space=pl.ANY)],
        out_specs=vmem_spec(),
        scratch_shapes=[pltpu.VMEM((lanes // 128, rows, 128), F32)] * 2
        + [pltpu.VMEM(weights.shape[1:], BF16), pltpu.SemaphoreType.DMA((4,))],
        cost_estimate=cost(6e8, weights.size + rows * lanes * 4),
        name="mix",
    )(got, forward, inverse, weights)


def spread_weights(up_ref, down_ref, up_wide_ref, down_wide_ref):
    hidden, channels = up_ref.shape[1:]
    up = up_ref[0].T
    down = (down_ref[0].astype(F32) * 0.5).astype(BF16).T
    up_wide_ref[...] = jnp.zeros_like(up_wide_ref)
    down_wide_ref[...] = jnp.zeros_like(down_wide_ref)
    for cell in range(2):
        here = slice(cell * channels, (cell + 1) * channels)
        there = slice(cell * hidden, (cell + 1) * hidden)
        up_wide_ref[here, there] = up
        down_wide_ref[there, here] = down


def mlp(summed, up_ref, down_ref):
    rounded = summed.astype(BF16)
    total = summed
    width = 256
    for first in range(0, up_ref.shape[1], width):
        hidden = dot(rounded, up_ref[:, first : first + width])
        slope = hidden * (GELU_K + (GELU_K * 0.044715) * (hidden * hidden))
        active = (hidden * jnp.tanh(slope) + hidden).astype(BF16)
        total = total + dot(active, down_ref[first : first + width, :])
    return total


def scatter_kernel(spot_ref, got_ref, out_ref, wide_ref):
    devices, rows, _ = got_ref.shape
    rows = rows - 8
    pairs = spot_ref.shape[0] // devices
    size = rows // pairs
    lines = size // TILES(out_ref)
    tiles = TILES(out_ref)
    out_ref[...] = jnp.zeros_like(out_ref)
    for source in range(devices):
        for tile in range(tiles):
            wide_ref[pl.ds(source * rows + tile, pairs * lines, stride=tiles), :] = got_ref[
                source, tile * pairs * lines : (tile + 1) * pairs * lines, :
            ].astype(F32)

    @pl.loop(0, devices)
    def _(source):
        for pair in range(pairs):
            base = pl.multiple_of(spot_ref[source * pairs + pair], size)
            here = pl.multiple_of(source * rows + pair * size, size)
            out_ref[pl.ds(base, size), :] = (
                out_ref[pl.ds(base, size), :] + wide_ref[pl.ds(here, size), :]
            )


def TILES(ref):
    return ref.shape[0] // (NX * NY)


def scatter(spots, got, tiles):
    devices, rows, _ = got.shape
    return pl.pallas_call(
        scatter_kernel,
        out_shape=jax.ShapeDtypeStruct((NX * NY * tiles, 128), F32),
        grid_spec=pltpu.PrefetchScalarGridSpec(
            num_scalar_prefetch=1,
            grid=(1,),
            in_specs=[pl.BlockSpec(got.shape, lambda i, s: (0, 0, 0))],
            out_specs=pl.BlockSpec((NX * NY * tiles, 128), lambda i, s: (0, 0)),
            scratch_shapes=[pltpu.VMEM((devices * (rows - 8), 128), F32)],
        ),
        compiler_params=pltpu.CompilerParams(vmem_limit_bytes=48 * 1024 * 1024),
        cost_estimate=cost(1e6, NX * NY * tiles * 128 * 16),
        name="scatter",
    )(spots, got)


def gather_kernel(size, devices, spot_ref, grid_ref, out_ref):
    pairs = spot_ref.shape[0] // devices

    @pl.loop(0, devices)
    def _(source):
        for pair in range(pairs):
            base = pl.multiple_of(spot_ref[source * pairs + pair], size)
            here = pl.multiple_of(source * (pairs * size) + pair * size, size)
            out_ref[pl.ds(here, size), :] = grid_ref[pl.ds(base, size), :]


def gather(spots, grid, size, devices):
    count = spots.shape[0]
    return pl.pallas_call(
        functools.partial(gather_kernel, size, devices),
        out_shape=jax.ShapeDtypeStruct((count * size, 128), F32),
        grid_spec=pltpu.PrefetchScalarGridSpec(
            num_scalar_prefetch=1,
            grid=(1,),
            in_specs=[pl.BlockSpec(grid.shape, lambda i, s: (0, 0))],
            out_specs=pl.BlockSpec((count * size, 128), lambda i, s: (0, 0)),
        ),
        compiler_params=pltpu.CompilerParams(vmem_limit_bytes=48 * 1024 * 1024),
        cost_estimate=cost(1e6, grid.size * 8),
        name="gather",
    )(spots, grid)


def layer_kernel(
    table_ref, flipped_ref, modes_ref, grid_ref, up_ref, down_ref, out_ref, spec_ref, total_ref,
    up_wide_ref, down_wide_ref
):
    step = pl.program_id(0)
    rows = table_ref.shape[0]
    tiles = modes_ref.shape[1] // 128

    @pl.when(step == 0)
    def _():
        total_ref[...] = jnp.zeros_like(total_ref)
        spread_weights(up_ref, down_ref, up_wide_ref, down_wide_ref)

    spectral = dot(table_ref[...], modes_ref[...])
    results = []
    for tile in range(tiles):
        place = pl.ds(tile, rows, stride=tiles)
        summed = grid_ref[place, :] + spectral[:, tile * 128 : (tile + 1) * 128]
        result = mlp(summed, up_wide_ref, down_wide_ref)
        out_ref[place, :] = result
        results.append(result.astype(BF16))
    total_ref[...] += dot(flipped_ref[...], jnp.concatenate(results, axis=1))

    @pl.when(step == pl.num_programs(0) - 1)
    def _():
        spec_ref[...] = total_ref[...].astype(BF16)


def weight_specs(up, down, number):
    return [
        pl.BlockSpec((1,) + up.shape[1:], lambda i: (number, 0, 0)),
        pl.BlockSpec((1,) + down.shape[1:], lambda i: (number, 0, 0)),
    ]


def wide_weights(up):
    hidden, channels = up.shape[1:]
    return [
        pltpu.VMEM((2 * channels, 2 * hidden), BF16),
        pltpu.VMEM((2 * hidden, 2 * channels), BF16),
    ]


def layer(table, flipped, modes, grid, up, down, number):
    cells, columns = table.shape
    lanes = modes.shape[1]
    tiles = lanes // 128
    rows = 512
    const = lambda i: (0, 0)
    return pl.pallas_call(
        layer_kernel,
        out_shape=(
            jax.ShapeDtypeStruct((cells * tiles, 128), F32),
            jax.ShapeDtypeStruct((columns, lanes), BF16),
        ),
        grid=(cells // rows,),
        in_specs=[
            pl.BlockSpec((rows, columns), lambda i: (i, 0)),
            pl.BlockSpec((columns, rows), lambda i: (0, i)),
            pl.BlockSpec((columns, lanes), const),
            pl.BlockSpec((rows * tiles, 128), lambda i: (i, 0)),
        ]
        + weight_specs(up, down, number),
        out_specs=(
            pl.BlockSpec((rows * tiles, 128), lambda i: (i, 0)),
            pl.BlockSpec((columns, lanes), const),
        ),
        scratch_shapes=[pltpu.VMEM((columns, lanes), F32)] + wide_weights(up),
        cost_estimate=cost(
            4 * cells * columns * lanes + 16 * cells * lanes * up.shape[1],
            cells * (columns * 4 + lanes * 8),
        ),
        name="layer",
    )(table, flipped, modes, grid, up, down)


def last_kernel(phase_ref, modes_ref, grid_ref, up_ref, down_ref, out_ref, up_wide_ref, down_wide_ref):
    group, rows, _ = out_ref.shape
    tiles = modes_ref.shape[1] // 128
    rows = rows // tiles

    @pl.when(pl.program_id(0) == 0)
    def _():
        spread_weights(up_ref, down_ref, up_wide_ref, down_wide_ref)

    spectral = lax.dot_general(
        phase_ref[...], modes_ref[...], (((0,), (0,)), ((), ())), preferred_element_type=F32
    )
    for tile in range(tiles):
        summed = (
            grid_ref[pl.ds(tile, group * rows, stride=tiles), :]
            + spectral[:, tile * 128 : (tile + 1) * 128]
        )
        result = mlp(summed, up_wide_ref, down_wide_ref).astype(BF16)
        for source in range(group):
            out_ref[source, tile * rows : (tile + 1) * rows, :] = result[
                source * rows : (source + 1) * rows, :
            ]


def last_layer(phases, modes, grid, up, down, number, devices):
    columns, count = phases.shape
    lanes = modes.shape[1]
    tiles = lanes // 128
    group = 4
    rows = count // devices
    return pl.pallas_call(
        last_kernel,
        out_shape=jax.ShapeDtypeStruct((devices, rows * tiles, 128), BF16),
        grid=(devices // group,),
        in_specs=[
            pl.BlockSpec((columns, group * rows), lambda i: (0, i)),
            pl.BlockSpec((columns, lanes), lambda i: (0, 0)),
            pl.BlockSpec((group * rows * tiles, 128), lambda i: (i, 0)),
        ]
        + weight_specs(up, down, number),
        out_specs=pl.BlockSpec((group, rows * tiles, 128), lambda i: (i, 0, 0)),
        scratch_shapes=wide_weights(up),
        cost_estimate=cost(
            2 * count * columns * lanes + 16 * count * lanes * up.shape[1],
            count * (columns * 2 + lanes * 6),
        ),
        name="last_layer",
    )(phases, modes, grid, up, down)


def exchange(values):
    return lax.all_to_all(values, "pen", split_axis=0, concat_axis=0, tiled=True)


def per_device(point_feat, pair_kernel, pair_owner, pair_block, spec_weight, mlp_up, mlp_down):
    devices = lax.axis_size("pen")
    pairs, block = pair_kernel.shape[0], pair_kernel.shape[1]
    channels = point_feat.shape[0]
    modes_here = spec_weight.shape[1]
    lines = block // NZ
    lanes = NZ // devices * channels
    tiles = lanes // 128
    columns = devices * 2 * MX

    target = pair_owner[:, 0] * (NX * NY // lines // devices) + pair_block
    x_at = jnp.repeat(target // (NY // lines), lines)
    y_at = (target % (NY // lines))[:, None] * lines + jnp.arange(lines, dtype=jnp.int32)
    spots = jnp.stack([x_at, y_at.reshape(-1)] + [jnp.zeros_like(x_at)] * 6).astype(F32)

    got = exchange(encode(point_feat, pair_kernel, spots, devices))

    table, flipped = grid_tables(devices, modes_here)
    forward, inverse = depth_tables(devices, modes_here)
    here = got[:, -8:-6, 0 : pairs * lines : lines].astype(jnp.int32)
    rows = ((here[:, 0, :] * NY + here[:, 1, :]) * tiles).reshape(devices * pairs)

    spectrum, phases = pair_spectrum(got, modes_here, lanes)
    grid = scatter(rows, got, tiles)
    modes = exchange(spectrum.reshape(devices, 2 * MX, lanes)).reshape(columns, lanes)
    modes = mix(modes, forward, inverse, spec_weight, 0, devices)
    modes = exchange(modes.reshape(devices, 2 * MX, lanes)).reshape(columns, lanes)
    grid, spectrum = layer(table, flipped, modes, grid, mlp_up, mlp_down, 0)
    listed = gather(rows, grid, lines * tiles, devices)
    modes = exchange(spectrum.reshape(devices, 2 * MX, lanes)).reshape(columns, lanes)
    modes = mix(modes, forward, inverse, spec_weight, 1, devices)
    modes = exchange(modes.reshape(devices, 2 * MX, lanes)).reshape(columns, lanes)
    result = last_layer(phases, modes, listed, mlp_up, mlp_down, 1, devices)
    return decode(exchange(result), pair_kernel, channels)


def solution(mesh):
    in_specs = (
        P(None, ("groups", "pen")),
        P(("groups", "pen"), None, None),
        P(("groups", "pen"), None),
        P(("groups", "pen")),
        P(None, "pen", None, None, None),
        P(),
        P(),
    )
    out_specs = P(None, ("groups", "pen"))
    return jax.shard_map(
        per_device, mesh=mesh, in_specs=in_specs, out_specs=out_specs, check_vma=False
    )
```

time: 660 us -> 203 us (0.31); the launches traced: 649 us -> 201 us
  local copies, waits for them, and re-layouts: 215 us -> 4.46 us
  matrix products: 175 us -> 0 us
  waiting for transfers between devices: 108 us -> 3.38 us
  Pallas kernels: 0 us -> 89.1 us
  other arithmetic: 68.2 us -> 1.48 us
  blocking collectives: 31.4 us -> 94.8 us
  starting transfers between devices: 51.5 us -> 7.9 us
    dot_general x32 -> x0, matrix products: 175 us -> none  [the longest x2 50.8 us: channel_mlp(): jnp.dot(weight_down, active, preferred_element_type=jnp.float32)]
    all_to_all x6 -> x2, waiting for transfers between devices: 108 us -> 3.38 us  [exchange(): lax.all_to_all(values, 'pen', split_axis=0, concat_axis=0, tiled=True)]
    pallas_call x0 -> x10, Pallas kernels: none -> 89.1 us  [the longest x1 28.7 us: layer(): pl.pallas_call(layer_kernel, out_shape=(jax.ShapeDtypeStruct((cells * til...]
    all_to_all x1 -> x4, blocking collectives: 31.4 us -> 94.8 us  [exchange(): lax.all_to_all(values, 'pen', split_axis=0, concat_axis=0, tiled=True)]
    reshape x10 -> x0, local copies, waits for them, and re-layouts: 58.1 us -> none  [the longest x3 28.1 us: spectral_part(): jnp.dot(flat_result, inverse_table.T, precision=HIGHEST)]
    all_to_all x6 -> x2, starting transfers between devices: 51.5 us -> 7.9 us  [exchange(): lax.all_to_all(values, 'pen', split_axis=0, concat_axis=0, tiled=True)]
    unnamed x38 -> x11, local copies, waits for them, and re-layouts: 38.6 us -> 3.5 us
    mul x2 -> x1, local copies, waits for them, and re-layouts: 24.3 us -> 0.07 us  [per_device(): (here[:, 0, :] * NY + here[:, 1, :]) * tiles]
  transfers between devices with their start and end apart: 6 -> 2, of which waited for: 4 -> 1; matrix products, arithmetic and copies ran while one was open for 15% -> 1% of each run, Pallas kernels for 0% -> 12%
where the time goes in v1:
time: 203 us; the launch traced here: 201 us
  blocking collectives  94.8 us (47%)
  Pallas kernels  89.1 us (44%)
  starting transfers between devices  7.9 us (4%)
  local copies, waits for them, and re-layouts  4.46 us (2%)
  waiting for transfers between devices  3.38 us (2%)
    all_to_all x4, blocking collectives, exchange(): lax.all_to_all(values, 'pen', split_axis=0, concat_axis=0, tiled=True)  94.8 us
    pallas_call x1, Pallas kernels, layer(): pl.pallas_call(layer_kernel, out_shape=(jax.ShapeDtypeStruct((cells * til...  28.7 us
    pallas_call x1, Pallas kernels, grid_tables(): pl.pallas_call(table_kernel, out_shape=(jax.ShapeDtypeStruct((NX * NY, co...  11.9 us
    pallas_call x2, Pallas kernels, mix(): pl.pallas_call(functools.partial(mix_kernel, devices, number), out_shape=...  9.14 us
    all_to_all x2, starting transfers between devices, exchange(): lax.all_to_all(values, 'pen', split_axis=0, concat_axis=0, tiled=True)  7.9 us
    pallas_call x1, Pallas kernels, decode(): pl.pallas_call(decode_kernel, out_shape=jax.ShapeDtypeStruct((channels, p...  7.83 us
    pallas_call x1, Pallas kernels, last_layer(): pl.pallas_call(last_kernel, out_shape=jax.ShapeDtypeStruct((devices, rows...  7.67 us
    pallas_call x1, Pallas kernels, encode(): pl.pallas_call(encode_kernel, out_shape=jax.ShapeDtypeStruct((devices, ro...  7.57 us
  transfers between devices with their start and end apart: 2, of which 1 were waited for; matrix products, arithmetic and copies ran while one was open for 1% of the time, Pallas kernels for 12%

profile of v1, /device:TPU:1, one launch (start us, length us, event | category | flops | bytes accessed | tf_op | source)
XLA Modules:
  0.0 201.2 jit_solution(3247751422847086666)
XLA Ops:
  0.0 0.1 pad.3.clone
  0.1 0.1 pad.2.clone
  0.2 0.7 and_select_fusion.1
  0.8 0.1 iota_add_fusion
  0.9 0.1 add.43
  1.1 0.1 broadcast_in_dim.2
  1.1 0.1 stack_reshape.4
  1.3 0.7 add_convert_fusion.spot_ref
  2.0 0.0 copy-start.4
  2.0 7.6 %encode.1 = bf16[16,264,128]{2,1,0:T(8,128)(2,1)} custom-call(bf16[64,2048]{1,0:T(8,128)(2,1)} %feature_ref.1, bf16[64,128,128]{2,1,0:T(8,128)(2,1)} %weight_ref.3, f32[8,128]{1,0:T(8,128)} %add_convert_fusion.spot_ref), custom_call_target="tpu_custom_call" | custom-call | flops 268435456 | bytes 2097152 | tf_op jit(solution)/shard_map/encode/pallas_call | solution.py:172
  9.5 35.1 %all_to_all.30.got_ref = bf16[16,264,128]{2,1,0:T(8,128)(2,1)} all-to-all(bf16[16,264,128]{2,1,0:T(8,128)(2,1)} %encode.1), channel_id=1, replica_groups=mesh['groups'=2,'pen'=16] {'pen'}, dimensions={0} | all-to-all | bytes 2162688 | tf_op jit(solution)/shard_map/all_to_all | solution.py:618
  44.6 0.0 copy-start
  44.6 4.7 %pair_spectrum.1 = (bf16[512,256]{1,0:T(8,128)(2,1)}, bf16[512,2048]{1,0:T(8,128)(2,1)}) custom-call(bf16[16,264,128]{2,1,0:T(8,128)(2,1)} %all_to_all.30.got_ref), custom_call_target="tpu_custom_call" | custom-call | flops 536870912 | bytes 3178496 | tf_op jit(solution)/shard_map/pair_spectrum/pallas_call | solution.py:285
  49.3 14.0 %all_to_all.31 = bf16[16,32,256]{2,1,0:T(8,128)(2,1)} all-to-all(bf16[16,32,256]{2,1,0:T(8,128)(2,1)} %bitcast.22), channel_id=1, replica_groups=mesh['groups'=2,'pen'=16] {'pen'}, dimensions={0} | all-to-all | bytes 524288 | tf_op jit(solution)/shard_map/all_to_all | solution.py:618
  63.3 4.6 %mix.2 = bf16[512,256]{1,0:T(8,128)(2,1)} custom-call(bf16[512,256]{1,0:T(8,128)(2,1)} %bitcast.18, bf16[128,64]{1,0:T(8,128)(2,1)} %constant.60.forward_ref, bf16[128,128]{1,0:T(8,128)(2,1)} %constant.66.inverse_ref, bf16[2,16,16,64,128]{4,3,2,1,0:T(8,128)(2,1)} %all_ref.3), custom_call_target="tpu_custom_call" | custom-call | flops 600000000 | bytes 4718592 | tf_op jit(solution)/shard_map/mix/pallas_call | solution.py:380
  67.9 4.0 %all-to-all-start.2 = ((bf16[16,32,256]{2,1,0:T(8,128)(2,1)}), bf16[16,32,256]{2,1,0:T(8,128)(2,1)S(1)}, u32[]{:S(2)}, u32[]{:S(2)}) async-start(bf16[16,32,256]{2,1,0:T(8,128)(2,1)} %bitcast.15), calls=%async_computation.2 | async-start | bytes 524288 | tf_op jit(solution)/shard_map/all_to_all | solution.py:618
  71.8 0.0 copy-done.4
  71.8 0.8 copy.16.up_ref
  72.6 11.9 %tables.1 = (bf16[8192,512]{1,0:T(8,128)(2,1)}, bf16[512,8192]{1,0:T(8,128)(2,1)}) custom-call(f32[128,512]{1,0:T(8,128)} %constant.49.clone.first_ref, f32[128,512]{1,0:T(8,128)} %constant.50.clone.second_ref, f32[64,512]{1,0:T(8,128)} %constant.51.clone.cos_ref, f32[64,512]{1,0:T(8,128)} %constant.52.clone.sin_ref), custom_call_target="tpu_custom_call" | custom-call | flops 16777216 | bytes 16777216 | tf_op jit(solution)/shard_map/tables/pallas_call | solution.py:114
  84.5 0.0 copy-done
  84.5 0.4 slice.9
  84.9 0.1 mul.43.spot_ref
  85.0 6.8 %scatter.1.grid_ref = f32[16384,128]{1,0:T(8,128)} custom-call(s32[1024]{0:T(1024)S(1)} %mul.43.spot_ref, bf16[16,264,128]{2,1,0:T(8,128)(2,1)S(1)} %copy-done), custom_call_target="tpu_custom_call" | custom-call | flops 1000000 | bytes 33554432 | tf_op jit(solution)/shard_map/scatter/pallas_call | solution.py:447
  91.7 0.0 all-to-all-done.2
  91.7 0.0 copy-start.2
  91.7 0.7 copy-done.2
  92.4 28.7 %layer.1 = (f32[16384,128]{1,0:T(8,128)}, bf16[512,256]{1,0:T(8,128)(2,1)}) custom-call(bf16[8192,512]{1,0:T(8,128)(2,1)} %get-tuple-element.12.table_ref, bf16[512,8192]{1,0:T(8,128)(2,1)} %get-tuple-element.13.flipped_ref, bf16[512,256]{1,0:T(8,128)(2,1)} %bitcast.19, f32[16384,128]{1,0:T(8,128)} %scatter.1.grid_ref, bf16[2,256,64]{2,1,0:T(8,128)(2,1)} %copy.16.up_ref, ...), custom_call_target="tpu_custom_call" | custom-call | flops 12884901888 | bytes 33554432 | tf_op jit(solution)/shard_map/layer/pallas_call | solution.py:540
  121.1 15.7 %all_to_all.32 = bf16[16,32,256]{2,1,0:T(8,128)(2,1)} all-to-all(bf16[16,32,256]{2,1,0:T(8,128)(2,1)} %bitcast.21), channel_id=1, replica_groups=mesh['groups'=2,'pen'=16] {'pen'}, dimensions={0} | all-to-all | bytes 524288 | tf_op jit(solution)/shard_map/all_to_all | solution.py:618
  136.8 4.6 %mix.3 = bf16[512,256]{1,0:T(8,128)(2,1)} custom-call(bf16[512,256]{1,0:T(8,128)(2,1)} %bitcast.17, bf16[128,64]{1,0:T(8,128)(2,1)} %constant.60.forward_ref, bf16[128,128]{1,0:T(8,128)(2,1)} %constant.66.inverse_ref, bf16[2,16,16,64,128]{4,3,2,1,0:T(8,128)(2,1)} %all_ref.3), custom_call_target="tpu_custom_call" | custom-call | flops 600000000 | bytes 4718592 | tf_op jit(solution)/shard_map/mix/pallas_call | solution.py:380
  141.4 3.9 %all-to-all-start.4 = ((bf16[16,32,256]{2,1,0:T(8,128)(2,1)}), bf16[16,32,256]{2,1,0:T(8,128)(2,1)S(1)}, u32[]{:S(2)}, u32[]{:S(2)}) async-start(bf16[16,32,256]{2,1,0:T(8,128)(2,1)} %bitcast.16), calls=%async_computation.4 | async-start | bytes 524288 | tf_op jit(solution)/shard_map/all_to_all | solution.py:618
  145.4 4.9 %gather.1.grid_ref = f32[4096,128]{1,0:T(8,128)S(1)} custom-call(s32[1024]{0:T(1024)S(1)} %mul.43.spot_ref, f32[16384,128]{1,0:T(8,128)} %get-tuple-element.16.grid_ref), custom_call_target="tpu_custom_call" | custom-call | flops 1000000 | bytes 16777216 | tf_op jit(solution)/shard_map/gather/pallas_call | solution.py:476
  150.2 0.0 copy-start.1
  150.2 1.3 copy-done.1
  151.6 3.4 %all-to-all-done.4 = bf16[16,32,256]{2,1,0:T(8,128)(2,1)S(1)} async-done(((bf16[16,32,256]{2,1,0:T(8,128)(2,1)}), bf16[16,32,256]{2,1,0:T(8,128)(2,1)S(1)}, u32[]{:S(2)}, u32[]{:S(2)}) %all-to-all-start.4) | async-done | bytes 262176 | tf_op jit(solution)/shard_map/all_to_all | solution.py:618
  154.9 0.0 copy-start.3
  154.9 0.7 copy-done.3
  155.6 7.7 %last_layer.1 = bf16[16,256,128]{2,1,0:T(8,128)(2,1)} custom-call(bf16[512,2048]{1,0:T(8,128)(2,1)} %get-tuple-element.11.phase_ref, bf16[512,256]{1,0:T(8,128)(2,1)} %bitcast.20, f32[4096,128]{1,0:T(8,128)} %copy-done.1, bf16[2,256,64]{2,1,0:T(8,128)(2,1)} %copy.16.up_ref, bf16[2,64,256]{2,1,0:T(8,128)(2,1)} %down_ref.3), custom_call_target="tpu_custom_call" | custom-call | flops 2684354560 | bytes 5242880 | tf_op jit(solution)/shard_map/last_layer/pallas_call | solution.py:597
  163.3 30.1 %all_to_all.33.got_ref = bf16[16,256,128]{2,1,0:T(8,128)(2,1)} all-to-all(bf16[16,256,128]{2,1,0:T(8,128)(2,1)} %last_layer.1), channel_id=1, replica_groups=mesh['groups'=2,'pen'=16] {'pen'}, dimensions={0} | all-to-all | bytes 2097152 | tf_op jit(solution)/shard_map/all_to_all | solution.py:618
  193.4 7.8 %decode.1 = f32[64,2048]{1,0:T(8,128)} custom-call(bf16[16,256,128]{2,1,0:T(8,128)(2,1)} %all_to_all.33.got_ref, bf16[64,128,128]{2,1,0:T(8,128)(2,1)} %weight_ref.3), custom_call_target="tpu_custom_call" | custom-call | flops 268435456 | bytes 2097152 | tf_op jit(solution)/shard_map/decode/pallas_call | solution.py:227
  (5 shorter events, 0.1 us)
Async XLA Ops:
  2.0 69.9 %copy-start.4 = (bf16[2,256,64]{1,2,0:T(8,128)(2,1)S(1)}, bf16[2,256,64]{1,2,0:T(8,128)(2,1)}, u32[]{:S(2)}) copy-start(bf16[2,256,64]{1,2,0:T(8,128)(2,1)} %param.18) | copy-start | bytes 196612
  44.6 39.9 %copy-start = (bf16[16,264,128]{2,1,0:T(8,128)(2,1)S(1)}, bf16[16,264,128]{2,1,0:T(8,128)(2,1)}, u32[]{:S(2)}) copy-start(bf16[16,264,128]{2,1,0:T(8,128)(2,1)} %all_to_all.30.got_ref) | copy-start | bytes 3244036
  67.9 23.9 %all-to-all-start.2 = ((bf16[16,32,256]{2,1,0:T(8,128)(2,1)}), bf16[16,32,256]{2,1,0:T(8,128)(2,1)S(1)}, u32[]{:S(2)}, u32[]{:S(2)}) async-start(bf16[16,32,256]{2,1,0:T(8,128)(2,1)} %bitcast.15), calls=%async_computation.2 | async-start | bytes 524288 | tf_op jit(solution)/shard_map/all_to_all | solution.py:618
  91.7 0.7 copy-start.2
  141.4 13.5 %all-to-all-start.4 = ((bf16[16,32,256]{2,1,0:T(8,128)(2,1)}), bf16[16,32,256]{2,1,0:T(8,128)(2,1)S(1)}, u32[]{:S(2)}, u32[]{:S(2)}) async-start(bf16[16,32,256]{2,1,0:T(8,128)(2,1)} %bitcast.16), calls=%async_computation.4 | async-start | bytes 524288 | tf_op jit(solution)/shard_map/all_to_all | solution.py:618
  150.2 1.3 copy-start.1
  154.9 0.7 copy-start.3

commit v2 on v1

--- a/solution.py
+++ b/solution.py
@@ -19,6 +19,7 @@
 NBR = 4
 GELU_K = math.sqrt(2.0 / math.pi)
 SCALE = 1.66575
+PAD = 8
 
 F32 = jnp.float32
 BF16 = jnp.bfloat16
@@ -38,16 +39,28 @@
     return jnp.dot(left, right, preferred_element_type=F32)
 
 
-def column_waves(devices, modes_here):
-    column = np.arange(devices * 2 * MX)
-    wave_y = (column // (2 * MX) * modes_here) // MZ - MY // 2
-    return wave_y, column // MX % 2, column % MX - MX // 2
+def x_waves():
+    wave = np.arange(MX) - MX // 2
+    return np.concatenate([wave[wave % 2 == 0], wave[wave % 2 == 1]])
+
+
+def y_waves(devices, modes_here):
+    return (np.arange(devices) * modes_here) // MZ - MY // 2
+
+
+def turn(wave, count):
+    return 2.0 * np.pi / count * (np.arange(count)[:, None] * wave[None, :] % count)
 
 
 def line_tables(devices, modes_here):
-    wave_y, part, wave_x = column_waves(devices, modes_here)
-    x_angle = 2.0 * np.pi / NX * (np.arange(NX)[:, None] * wave_x % NX)
-    y_angle = 2.0 * np.pi / NY * (np.arange(NY)[:, None] * wave_y % NY)
+    size = 2 * MX * devices
+    column = np.arange(size)
+    half = MX // 2
+    wave_x = x_waves()[column // (size // 2) * half + column % half]
+    wave_y = y_waves(devices, modes_here)[column // MX % devices]
+    part = column // half % 2
+    x_angle = turn(wave_x, NX)[: NX // 2]
+    y_angle = turn(wave_y, NY)
     x_cos, x_sin = SCALE * np.cos(x_angle), SCALE * np.sin(x_angle)
     first = np.where(part == 0, x_cos, -x_sin)
     second = np.where(part == 0, -x_sin, -x_cos)
@@ -57,6 +70,15 @@
     ]
 
 
+def lookup_tables():
+    result = []
+    for wave, count, scale in ((x_waves(), NX, SCALE), (np.arange(MY) - MY // 2, NY, 1.0)):
+        angle = turn(wave, count).T
+        values = scale * np.concatenate([np.cos(angle), -np.sin(angle)])
+        result.append(jnp.concatenate(split(jnp.asarray(values.astype(np.float32))), axis=0))
+    return result
+
+
 def split(values):
     high = values.astype(BF16)
     return high, (values - high.astype(F32)).astype(BF16)
@@ -65,22 +87,22 @@
 def depth_tables(devices, modes_here):
     local = NZ // devices
     wave_z = np.arange(MZ).reshape(MZ // modes_here, modes_here)
-    z_of = np.arange(devices)[None, :] * local + np.arange(local)[:, None]
+    z_of = np.arange(devices)[None, :] + devices * np.arange(local)[:, None]
     angle = 2.0 * np.pi / NZ * (z_of[None, :, :, None] * wave_z[:, None, None, :] % NZ)
     cosine, sine = np.cos(angle), np.sin(angle)
     to_real = np.stack([cosine, sine], axis=-1)
     to_imag = np.stack([-sine, cosine], axis=-1)
     forward = np.stack([to_real, to_imag], axis=-2) / SCALE
-    forward = forward.transpose(0, 1, 3, 4, 2, 5).reshape(
+    forward = forward.transpose(0, 1, 3, 4, 5, 2).reshape(
         -1, local * modes_here * 2, devices * 2
     )
     scale = np.where(wave_z == 0, 1.0, 2.0)[:, None, None, :] / (NX * NY * NZ * SCALE)
     cosine, sine = cosine * scale, sine * scale
     low = np.stack(
-        [np.stack([cosine, -sine], axis=-1), np.stack([sine, cosine], axis=-1)], axis=3
+        [np.stack([cosine, -sine], axis=-1), np.stack([sine, cosine], axis=-1)], axis=2
     ).reshape(-1, local * devices * 2, modes_here * 2)
     high = np.stack(
-        [np.stack([-sine, -cosine], axis=-1), np.stack([cosine, -sine], axis=-1)], axis=3
+        [np.stack([-sine, -cosine], axis=-1), np.stack([cosine, -sine], axis=-1)], axis=2
     ).reshape(-1, local * devices * 2, modes_here * 2)
     inverse = np.concatenate([low, high], axis=2)
     which = lax.axis_index("pen") * modes_here % MZ // modes_here
@@ -114,10 +136,10 @@
     return pl.pallas_call(
         table_kernel,
         out_shape=(
-            jax.ShapeDtypeStruct((NX * NY, columns), BF16),
-            jax.ShapeDtypeStruct((columns, NX * NY), BF16),
-        ),
-        grid=(NX // lines,),
+            jax.ShapeDtypeStruct((NX // 2 * NY, columns), BF16),
+            jax.ShapeDtypeStruct((columns, NX // 2 * NY), BF16),
+        ),
+        grid=(NX // 2 // lines,),
         in_specs=[
             pl.BlockSpec((lines, columns), lambda i: (i, 0)),
             pl.BlockSpec((lines, columns), lambda i: (i, 0)),
@@ -128,41 +150,43 @@
             pl.BlockSpec((rows, columns), lambda i: (i, 0)),
             pl.BlockSpec((columns, rows), lambda i: (0, i)),
         ),
-        cost_estimate=cost(4 * NX * NY * columns, 4 * NX * NY * columns),
+        cost_estimate=cost(4 * NX // 2 * NY * columns, 4 * NX // 2 * NY * columns),
         name="tables",
     )(first, second, y_cos, y_sin)
 
 
-def encode_kernel(feature_ref, weight_ref, spot_ref, out_ref, wide_ref, turned_ref):
+def encode_kernel(feature_ref, weight_ref, spot_ref, out_ref, wide_ref):
     devices = out_ref.shape[0]
     pairs, block = weight_ref.shape[0], weight_ref.shape[1]
     lines = block // NZ
-    local = NZ // devices
-    tiles = local // 2
+    tiles = NZ // devices // 2
     rows = tiles * pairs * lines
-    lane = lax.broadcasted_iota(jnp.int32, (lines * devices, 128), 1)
+    lane = lax.broadcasted_iota(jnp.int32, (devices, 128), 1)
 
     def one(point, carry):
         features = feature_ref[:, pl.ds(pl.multiple_of(point * block, block), block)]
         features = jnp.concatenate([features, features], axis=0)
         for near in range(NBR):
             pair = point * NBR + near
-            turned_ref[near] = lax.dot_general(
+            turned = lax.dot_general(
                 weight_ref[pair], features, (((0,), (1,)), ((), ())), preferred_element_type=F32
             )
-            for tile in range(tiles):
-                even = turned_ref[near, pl.ds(2 * tile, lines * devices, stride=local), :]
-                odd = turned_ref[near, pl.ds(2 * tile + 1, lines * devices, stride=local), :]
-                both = jnp.where(lane < 64, even, odd)
-                for line in range(lines):
+            for line in range(lines):
+                for tile in range(tiles):
+                    first = line * NZ + 2 * tile * devices
                     wide_ref[
-                        pl.ds(tile * pairs * lines + pair * lines + line, devices, stride=rows), :
-                    ] = both[line * devices : (line + 1) * devices, :]
+                        pl.ds((tile * pairs + pair) * lines + line, devices, stride=rows + PAD), :
+                    ] = jnp.where(
+                        lane < 64,
+                        turned[first : first + devices],
+                        turned[first + devices : first + 2 * devices],
+                    )
         return carry
 
     lax.fori_loop(0, pairs // NBR, one, 0)
     for device in range(devices):
-        out_ref[device, 0:rows, :] = wide_ref[device * rows : (device + 1) * rows, :].astype(BF16)
+        base = device * (rows + PAD)
+        out_ref[device, 0:rows, :] = wide_ref[base : base + rows, :].astype(BF16)
         out_ref[device, rows : rows + 8, :] = spot_ref[...].astype(BF16)
 
 
@@ -174,43 +198,39 @@
         out_shape=jax.ShapeDtypeStruct((devices, rows + 8, 128), BF16),
         in_specs=[vmem_spec()] * 3,
         out_specs=vmem_spec(),
-        scratch_shapes=[
-            pltpu.VMEM((devices * rows, 128), F32),
-            pltpu.VMEM((NBR, block, 128), F32),
-        ],
+        scratch_shapes=[pltpu.VMEM((devices * (rows + PAD), 128), F32)],
         cost_estimate=cost(4 * pairs * block * block * 64, pairs * block * block * 2),
         name="encode",
     )(features, weights, spots)
 
 
-def decode_kernel(got_ref, weight_ref, out_ref, wide_ref, turned_ref):
+def decode_kernel(got_ref, weight_ref, out_ref, wide_ref):
     devices, rows, _ = got_ref.shape
     pairs, block = weight_ref.shape[0], weight_ref.shape[1]
     lines = block // NZ
-    local = NZ // devices
-    tiles = local // 2
-    lane = lax.broadcasted_iota(jnp.int32, (block, 128), 1)
-    row = lax.broadcasted_iota(jnp.int32, (block, 128), 0)
-    keep = lane // 64 == row % 2
+    tiles = NZ // devices // 2
+    lane = lax.broadcasted_iota(jnp.int32, (devices, 128), 1)
     for device in range(devices):
-        wide_ref[device * rows : (device + 1) * rows, :] = got_ref[device].astype(F32)
+        base = device * (rows + PAD)
+        wide_ref[base : base + rows, :] = got_ref[device].astype(F32)
 
     def one(point, carry):
         total = None
         for near in range(NBR):
             pair = point * NBR + near
-            for tile in range(tiles):
-                for line in range(lines):
+            pieces = []
+            for line in range(lines):
+                for tile in range(tiles):
                     values = wide_ref[
-                        pl.ds(tile * pairs * lines + pair * lines + line, devices, stride=rows), :
+                        pl.ds((tile * pairs + pair) * lines + line, devices, stride=rows + PAD), :
                     ]
-                    for side in range(2):
-                        turned_ref[
-                            near, pl.ds(line * NZ + tile * 2 + side, devices, stride=local), :
-                        ] = values
-            left = jnp.where(keep, turned_ref[near], 0.0).astype(BF16)
+                    pieces.append(jnp.where(lane < 64, values, 0.0))
+                    pieces.append(jnp.where(lane < 64, 0.0, values))
             part = lax.dot_general(
-                left, weight_ref[pair], (((0,), (1,)), ((), ())), preferred_element_type=F32
+                jnp.concatenate(pieces, axis=0).astype(BF16),
+                weight_ref[pair],
+                (((0,), (1,)), ((), ())),
+                preferred_element_type=F32,
             )
             total = part if total is None else total + part
         out_ref[:, pl.ds(pl.multiple_of(point * block, block), block)] = (
@@ -229,39 +249,42 @@
         out_shape=jax.ShapeDtypeStruct((channels, pairs // NBR * block), F32),
         in_specs=[vmem_spec()] * 2,
         out_specs=vmem_spec(),
-        scratch_shapes=[
-            pltpu.VMEM((devices * rows, 128), F32),
-            pltpu.VMEM((NBR, block, 128), F32),
-        ],
+        scratch_shapes=[pltpu.VMEM((devices * (rows + PAD), 128), F32)],
         cost_estimate=cost(4 * pairs * block * block * 64, pairs * block * block * 2),
         name="decode",
     )(got, weights)
 
 
-def pair_spectrum_kernel(modes_here, got_ref, out_ref, phase_ref):
+def pair_spectrum_kernel(modes_here, got_ref, x_ref, y_ref, out_ref, phase_ref):
     devices = got_ref.shape[0]
     rows = got_ref.shape[1] - 8
     tiles = out_ref.shape[1] // 128
     lanes = rows // tiles
-    wave_x = lax.broadcasted_iota(jnp.int32, (MX, lanes), 0) - MX // 2
-    wave_y = lax.broadcasted_iota(jnp.int32, (MY, lanes), 0) - MY // 2
+    half = MX // 2
+    x_all = lax.broadcasted_iota(jnp.int32, (NX, lanes), 0)
+    y_all = lax.broadcasted_iota(jnp.int32, (NY, lanes), 0)
+
+    def look_up(table_ref, chosen):
+        values = dot(table_ref[...], chosen.astype(F32).astype(BF16))
+        count = values.shape[0] // 2
+        return values[0:count] + values[count:]
+
     for source in range(devices):
         spot = got_ref[source, rows : rows + 8, :].astype(F32)
-        x_at = spot[0:1, :].astype(jnp.int32)
-        y_at = spot[1:2, :].astype(jnp.int32)
-        x_angle = (2.0 * math.pi / NX) * ((wave_x * x_at) & (NX - 1)).astype(F32)
-        y_angle = (2.0 * math.pi / NY) * ((wave_y * y_at) & (NY - 1)).astype(F32)
-        x_cos, x_sin = SCALE * jnp.cos(x_angle), SCALE * jnp.sin(x_angle)
-        y_cos, y_sin = jnp.cos(y_angle), jnp.sin(y_angle)
+        x_turn = look_up(x_ref, x_all == spot[0:1, :].astype(jnp.int32))
+        y_turn = look_up(y_ref, y_all == spot[1:2, :].astype(jnp.int32))
         place = slice(source * lanes, (source + 1) * lanes)
         for device in range(devices):
             row = (device * modes_here) // MZ
-            cos_now, sin_now = y_cos[row : row + 1, :], y_sin[row : row + 1, :]
-            base = device * 2 * MX
-            phase_ref[base : base + MX, place] = (x_cos * cos_now - x_sin * sin_now).astype(BF16)
-            phase_ref[base + MX : base + 2 * MX, place] = (
-                -x_sin * cos_now - x_cos * sin_now
-            ).astype(BF16)
+            y_cos, y_less = y_turn[row : row + 1, :], y_turn[MY + row : MY + row + 1, :]
+            for parity in range(2):
+                first = parity * half
+                x_cos, x_less = x_turn[first : first + half], x_turn[MX + first : MX + first + half]
+                both = jnp.concatenate(
+                    [x_cos * y_cos - x_less * y_less, x_less * y_cos + x_cos * y_less], axis=0
+                )
+                base = (2 * device + parity) * MX
+                phase_ref[base : base + MX, place] = both.astype(BF16)
     values = jnp.concatenate(
         [
             jnp.concatenate(
@@ -288,11 +311,17 @@
             jax.ShapeDtypeStruct((columns, lanes), BF16),
             jax.ShapeDtypeStruct((columns, count), BF16),
         ),
-        in_specs=[vmem_spec()],
+        in_specs=[vmem_spec()] * 3,
         out_specs=(vmem_spec(), vmem_spec()),
         cost_estimate=cost(2 * columns * count * lanes, got.size * 2 + columns * count * 2),
         name="pair_spectrum",
-    )(got)
+    )(got, *lookup_tables())
+
+
+def row_of(wave, part):
+    half = MX // 2
+    order = list(x_waves() + half).index(wave)
+    return order // half * MX + part * half + order % half
 
 
 def mix_kernel(
@@ -323,7 +352,16 @@
     spread = []
     for wave in range(MX):
         planes = jnp.concatenate(
-            [wide_ref[tile, pl.ds(wave, 2 * devices, stride=MX), :] for tile in range(tiles)],
+            [
+                jnp.concatenate(
+                    [
+                        wide_ref[tile, pl.ds(row_of(wave, part), devices, stride=2 * MX), :]
+                        for part in range(2)
+                    ],
+                    axis=0,
+                )
+                for tile in range(tiles)
+            ],
             axis=1,
         ).astype(BF16)
         turned = dot(forward, jnp.concatenate([planes, planes], axis=0))
@@ -368,9 +406,11 @@
         for tile in range(tiles):
             even = planes[2 * tile * size : (2 * tile + 1) * size, :]
             odd = planes[(2 * tile + 1) * size : (2 * tile + 2) * size, :]
-            back_ref[tile, pl.ds(wave, size, stride=MX), :] = jnp.where(
-                lane_back < 64, even, pltpu.roll(odd, 64, 1)
-            )
+            both = jnp.where(lane_back < 64, even, pltpu.roll(odd, 64, 1))
+            for part in range(2):
+                back_ref[tile, pl.ds(row_of(wave, part), devices, stride=2 * MX), :] = both[
+                    part * devices : (part + 1) * devices
+                ]
     for tile in range(tiles):
         out_ref[:, tile * 128 : (tile + 1) * 128] = back_ref[tile].astype(BF16)
 
@@ -402,16 +442,23 @@
         down_wide_ref[there, here] = down
 
 
+def gelu_twice(hidden):
+    hidden = hidden.astype(BF16)
+    first = jnp.asarray(GELU_K, BF16)
+    third = jnp.asarray(GELU_K * 0.044715, BF16)
+    return hidden * jnp.tanh(hidden * (first + third * (hidden * hidden))) + hidden
+
+
 def mlp(summed, up_ref, down_ref):
-    rounded = summed.astype(BF16)
-    total = summed
     width = 256
+    rounded = [each.astype(BF16) for each in summed]
+    totals = list(summed)
     for first in range(0, up_ref.shape[1], width):
-        hidden = dot(rounded, up_ref[:, first : first + width])
-        slope = hidden * (GELU_K + (GELU_K * 0.044715) * (hidden * hidden))
-        active = (hidden * jnp.tanh(slope) + hidden).astype(BF16)
-        total = total + dot(active, down_ref[first : first + width, :])
-    return total
+        hidden = [dot(each, up_ref[:, first : first + width]) for each in rounded]
+        active = [gelu_twice(each) for each in hidden]
+        for n, each in enumerate(active):
+            totals[n] = totals[n] + dot(each, down_ref[first : first + width, :])
+    return totals
 
 
 def scatter_kernel(spot_ref, got_ref, out_ref, wide_ref):
@@ -490,30 +537,49 @@
 
 def layer_kernel(
     table_ref, flipped_ref, modes_ref, grid_ref, up_ref, down_ref, out_ref, spec_ref, total_ref,
-    up_wide_ref, down_wide_ref
+    up_wide_ref, down_wide_ref, folded_ref
 ):
     step = pl.program_id(0)
     rows = table_ref.shape[0]
     tiles = modes_ref.shape[1] // 128
+    count = table_ref.shape[1] // 2
+    blocks = count // MX
 
     @pl.when(step == 0)
     def _():
         total_ref[...] = jnp.zeros_like(total_ref)
         spread_weights(up_ref, down_ref, up_wide_ref, down_wide_ref)
-
-    spectral = dot(table_ref[...], modes_ref[...])
-    results = []
-    for tile in range(tiles):
-        place = pl.ds(tile, rows, stride=tiles)
-        summed = grid_ref[place, :] + spectral[:, tile * 128 : (tile + 1) * 128]
-        result = mlp(summed, up_wide_ref, down_wide_ref)
-        out_ref[place, :] = result
-        results.append(result.astype(BF16))
-    total_ref[...] += dot(flipped_ref[...], jnp.concatenate(results, axis=1))
+        for parity in range(2):
+            for block in range(blocks):
+                base = (2 * block + parity) * MX
+                folded_ref[parity, block * MX : (block + 1) * MX, :] = modes_ref[base : base + MX]
+
+    even = dot(table_ref[:, 0:count], folded_ref[0])
+    odd = dot(table_ref[:, count:], folded_ref[1])
+    halves = (even + odd, even - odd)
+    places = [(side, tile) for side in range(2) for tile in range(tiles)]
+    summed = [
+        grid_ref[side, pl.ds(tile, rows, stride=tiles), :]
+        + halves[side][:, tile * 128 : (tile + 1) * 128]
+        for side, tile in places
+    ]
+    results = mlp(summed, up_wide_ref, down_wide_ref)
+    for (side, tile), result in zip(places, results):
+        out_ref[side, pl.ds(tile, rows, stride=tiles), :] = result
+    low, high = results[0:tiles], results[tiles:]
+    plus = jnp.concatenate([(a + b).astype(BF16) for a, b in zip(low, high)], axis=1)
+    minus = jnp.concatenate([(a - b).astype(BF16) for a, b in zip(low, high)], axis=1)
+    total_ref[0] += dot(flipped_ref[0:count, :], plus)
+    total_ref[1] += dot(flipped_ref[count:, :], minus)
 
     @pl.when(step == pl.num_programs(0) - 1)
     def _():
-        spec_ref[...] = total_ref[...].astype(BF16)
+        for parity in range(2):
+            for block in range(blocks):
+                base = (2 * block + parity) * MX
+                spec_ref[base : base + MX, :] = total_ref[
+                    parity, block * MX : (block + 1) * MX, :
+                ].astype(BF16)
 
 
 def weight_specs(up, down, number):
@@ -540,7 +606,7 @@
     return pl.pallas_call(
         layer_kernel,
         out_shape=(
-            jax.ShapeDtypeStruct((cells * tiles, 128), F32),
+            jax.ShapeDtypeStruct((2, cells * tiles, 128), F32),
             jax.ShapeDtypeStruct((columns, lanes), BF16),
         ),
         grid=(cells // rows,),
@@ -548,20 +614,22 @@
             pl.BlockSpec((rows, columns), lambda i: (i, 0)),
             pl.BlockSpec((columns, rows), lambda i: (0, i)),
             pl.BlockSpec((columns, lanes), const),
-            pl.BlockSpec((rows * tiles, 128), lambda i: (i, 0)),
+            pl.BlockSpec((2, rows * tiles, 128), lambda i: (0, i, 0)),
         ]
         + weight_specs(up, down, number),
         out_specs=(
-            pl.BlockSpec((rows * tiles, 128), lambda i: (i, 0)),
+            pl.BlockSpec((2, rows * tiles, 128), lambda i: (0, i, 0)),
             pl.BlockSpec((columns, lanes), const),
         ),
-        scratch_shapes=[pltpu.VMEM((columns, lanes), F32)] + wide_weights(up),
+        scratch_shapes=[pltpu.VMEM((2, columns // 2, lanes), F32)]
+        + wide_weights(up)
+        + [pltpu.VMEM((2, columns // 2, lanes), BF16)],
         cost_estimate=cost(
             4 * cells * columns * lanes + 16 * cells * lanes * up.shape[1],
             cells * (columns * 4 + lanes * 8),
         ),
         name="layer",
-    )(table, flipped, modes, grid, up, down)
+    )(table, flipped, modes, grid.reshape(2, cells * tiles, 128), up, down)
 
 
 def last_kernel(phase_ref, modes_ref, grid_ref, up_ref, down_ref, out_ref, up_wide_ref, down_wide_ref):
@@ -576,12 +644,14 @@
     spectral = lax.dot_general(
         phase_ref[...], modes_ref[...], (((0,), (0,)), ((), ())), preferred_element_type=F32
     )
-    for tile in range(tiles):
-        summed = (
-            grid_ref[pl.ds(tile, group * rows, stride=tiles), :]
-            + spectral[:, tile * 128 : (tile + 1) * 128]
-        )
-        result = mlp(summed, up_wide_ref, down_wide_ref).astype(BF16)
+    summed = [
+        grid_ref[pl.ds(tile, group * rows, stride=tiles), :]
+        + spectral[:, tile * 128 : (tile + 1) * 128]
+        for tile in range(tiles)
+    ]
+    results = mlp(summed, up_wide_ref, down_wide_ref)
+    for tile, result in enumerate(results):
+        result = result.astype(BF16)
         for source in range(group):
             out_ref[source, tile * rows : (tile + 1) * rows, :] = result[
                 source * rows : (source + 1) * rows, :
@@ -592,7 +662,7 @@
     columns, count = phases.shape
     lanes = modes.shape[1]
     tiles = lanes // 128
-    group = 4
+    group = 8
     rows = count // devices
     return pl.pallas_call(
         last_kernel,
@@ -637,6 +707,7 @@
 
     table, flipped = grid_tables(devices, modes_here)
     forward, inverse = depth_tables(devices, modes_here)
+    got, table, flipped = lax.optimization_barrier((got, table, flipped))
     here = got[:, -8:-6, 0 : pairs * lines : lines].astype(jnp.int32)
     rows = ((here[:, 0, :] * NY + here[:, 1, :]) * tiles).reshape(devices * pairs)
 
@@ -646,7 +717,7 @@
     modes = mix(modes, forward, inverse, spec_weight, 0, devices)
     modes = exchange(modes.reshape(devices, 2 * MX, lanes)).reshape(columns, lanes)
     grid, spectrum = layer(table, flipped, modes, grid, mlp_up, mlp_down, 0)
-    listed = gather(rows, grid, lines * tiles, devices)
+    listed = gather(rows, grid.reshape(-1, 128), lines * tiles, devices)
     modes = exchange(spectrum.reshape(devices, 2 * MX, lanes)).reshape(columns, lanes)
     modes = mix(modes, forward, inverse, spec_weight, 1, devices)
     modes = exchange(modes.reshape(devices, 2 * MX, lanes)).reshape(columns, lanes)

time: 203 us -> 174 us (0.86)
  blocking collectives: 94.8 us -> 60.5 us
  Pallas kernels: 89.1 us -> 68.1 us
  waiting for transfers between devices: 3.38 us -> 22.1 us
  starting transfers between devices: 7.9 us -> 15.2 us
    all_to_all x4 -> x3, blocking collectives: 94.8 us -> 60.5 us  [exchange(): lax.all_to_all(values, 'pen', split_axis=0, concat_axis=0, tiled=True)]
    all_to_all x2 -> x3, waiting for transfers between devices: 3.38 us -> 22.1 us  [exchange(): lax.all_to_all(values, 'pen', split_axis=0, concat_axis=0, tiled=True)]
    pallas_call x2, Pallas kernels: 40.5 us -> 23.6 us  [the longest x1 17 us: layer(): pl.pallas_call(layer_kernel, out_shape=(jax.ShapeDtypeStruct((2, cells *...]
    all_to_all x2 -> x3, starting transfers between devices: 7.9 us -> 15.2 us  [exchange(): lax.all_to_all(values, 'pen', split_axis=0, concat_axis=0, tiled=True)]
    unnamed x11 -> x13, local copies, waits for them, and re-layouts: 3.5 us -> 4.47 us
  transfers between devices with their start and end apart: 2 -> 3, of which waited for: 1 -> 3; matrix products, arithmetic and copies ran while one was open for 1% -> 1% of each run, Pallas kernels for 12% -> 11%
where the time goes in v2:
time: 174 us; the launch traced here: 173 us
  Pallas kernels  68.1 us (39%)
  blocking collectives  60.5 us (35%)
  waiting for transfers between devices  22.1 us (13%)
  starting transfers between devices  15.2 us (9%)
  local copies, waits for them, and re-layouts  5.42 us (3%)
    all_to_all x3, blocking collectives, exchange(): lax.all_to_all(values, 'pen', split_axis=0, concat_axis=0, tiled=True)  60.5 us
    all_to_all x3, waiting for transfers between devices, exchange(): lax.all_to_all(values, 'pen', split_axis=0, concat_axis=0, tiled=True)  22.1 us
    pallas_call x1, Pallas kernels, layer(): pl.pallas_call(layer_kernel, out_shape=(jax.ShapeDtypeStruct((2, cells *...  17 us
    all_to_all x3, starting transfers between devices, exchange(): lax.all_to_all(values, 'pen', split_axis=0, concat_axis=0, tiled=True)  15.2 us
    pallas_call x2, Pallas kernels, mix(): pl.pallas_call(functools.partial(mix_kernel, devices, number), out_shape=...  9.61 us
    pallas_call x1, Pallas kernels, scatter(): pl.pallas_call(scatter_kernel, out_shape=jax.ShapeDtypeStruct((NX * NY *...  6.76 us
    pallas_call x1, Pallas kernels, decode(): pl.pallas_call(decode_kernel, out_shape=jax.ShapeDtypeStruct((channels, p...  6.67 us
    pallas_call x1, Pallas kernels, grid_tables(): pl.pallas_call(table_kernel, out_shape=(jax.ShapeDtypeStruct((NX // 2 * N...  6.59 us
  transfers between devices with their start and end apart: 3, of which 3 were waited for; matrix products, arithmetic and copies ran while one was open for 1% of the time, Pallas kernels for 11%

profile of v2, /device:TPU:1, one launch (start us, length us, event | category | flops | bytes accessed | tf_op | source)
XLA Modules:
  0.0 172.9 jit_solution(14529235480629738782)
XLA Ops:
  0.0 0.1 pad.3.clone
  0.1 0.1 pad.2.clone
  0.2 0.7 and_select_fusion.1
  0.8 0.1 iota_add_fusion
  0.9 0.1 add.43
  1.1 0.1 broadcast_in_dim.2
  1.1 0.1 stack_reshape.4
  1.3 0.7 add_convert_fusion.spot_ref
  2.0 6.4 %encode.1 = bf16[16,264,128]{2,1,0:T(8,128)(2,1)} custom-call(bf16[64,2048]{1,0:T(8,128)(2,1)} %feature_ref.1, bf16[64,128,128]{2,1,0:T(8,128)(2,1)} %weight_ref.3, f32[8,128]{1,0:T(8,128)} %add_convert_fusion.spot_ref), custom_call_target="tpu_custom_call" | custom-call | flops 268435456 | bytes 2097152 | tf_op jit(solution)/shard_map/encode/pallas_call | solution.py:196
  8.4 7.3 %all-to-all-start = ((bf16[16,264,128]{2,1,0:T(8,128)(2,1)}), bf16[16,264,128]{2,1,0:T(8,128)(2,1)S(1)}, u32[]{:S(2)}, u32[]{:S(2)}) async-start(bf16[16,264,128]{2,1,0:T(8,128)(2,1)} %encode.1), calls=%async_computation | async-start | bytes 2162688 | tf_op jit(solution)/shard_map/all_to_all | solution.py:688
  15.7 6.6 %tables.1 = (bf16[4096,512]{1,0:T(8,128)(2,1)}, bf16[512,4096]{1,0:T(8,128)(2,1)}) custom-call(f32[64,512]{1,0:T(8,128)} %constant.53.clone.first_ref, f32[64,512]{1,0:T(8,128)} %constant.54.clone.second_ref, f32[64,512]{1,0:T(8,128)} %constant.55.clone.cos_ref, f32[64,512]{1,0:T(8,128)} %constant.56.clone.sin_ref), custom_call_target="tpu_custom_call" | custom-call | flops 8388608 | bytes 8388608 | tf_op jit(solution)/shard_map/tables/pallas_call | solution.py:136
  22.3 17.2 %all-to-all-done.got_ref = bf16[16,264,128]{2,1,0:T(8,128)(2,1)S(1)} async-done(((bf16[16,264,128]{2,1,0:T(8,128)(2,1)}), bf16[16,264,128]{2,1,0:T(8,128)(2,1)S(1)}, u32[]{:S(2)}, u32[]{:S(2)}) %all-to-all-start) | async-done | bytes 1081376 | tf_op jit(solution)/shard_map/all_to_all | solution.py:688
  39.5 0.0 copy-start
  39.5 1.0 copy-done
  40.5 3.7 %pair_spectrum.1 = (bf16[512,256]{1,0:T(8,128)(2,1)}, bf16[512,2048]{1,0:T(8,128)(2,1)}) custom-call(bf16[16,264,128]{2,1,0:T(8,128)(2,1)} %copy-done, bf16[64,128]{1,0:T(8,128)(2,1)} %constant.65.x_ref, bf16[64,64]{1,0:T(8,128)(2,1)} %constant.70.y_ref), custom_call_target="tpu_custom_call" | custom-call | flops 536870912 | bytes 3178496 | tf_op jit(solution)/shard_map/pair_spectrum/pallas_call | solution.py:308
  44.1 16.2 %all_to_all.30 = bf16[16,32,256]{2,1,0:T(8,128)(2,1)} all-to-all(bf16[16,32,256]{2,1,0:T(8,128)(2,1)} %bitcast.26), channel_id=1, replica_groups=mesh['groups'=2,'pen'=16] {'pen'}, dimensions={0} | all-to-all | bytes 524288 | tf_op jit(solution)/shard_map/all_to_all | solution.py:688
  60.4 0.0 copy-start.5
  60.4 0.0 copy-start.1
  60.4 4.8 %mix.2 = bf16[512,256]{1,0:T(8,128)(2,1)} custom-call(bf16[512,256]{1,0:T(8,128)(2,1)} %bitcast.22, bf16[128,64]{1,0:T(8,128)(2,1)} %constant.76.forward_ref, bf16[128,128]{1,0:T(8,128)(2,1)} %constant.82.inverse_ref, bf16[2,16,16,64,128]{4,3,2,1,0:T(8,128)(2,1)} %all_ref.3), custom_call_target="tpu_custom_call" | custom-call | flops 600000000 | bytes 4718592 | tf_op jit(solution)/shard_map/mix/pallas_call | solution.py:420
  65.2 3.9 %all-to-all-start.2 = ((bf16[16,32,256]{2,1,0:T(8,128)(2,1)}), bf16[16,32,256]{2,1,0:T(8,128)(2,1)S(1)}, u32[]{:S(2)}, u32[]{:S(2)}) async-start(bf16[16,32,256]{2,1,0:T(8,128)(2,1)} %bitcast.19), calls=%async_computation.2 | async-start | bytes 524288 | tf_op jit(solution)/shard_map/all_to_all | solution.py:688
  69.2 0.0 copy-done.5
  69.2 0.8 copy.18.up_ref
  69.9 0.0 copy-done.1
  69.9 0.4 slice.9
  70.3 0.1 mul.43.spot_ref
  70.4 6.8 %scatter.1 = f32[16384,128]{1,0:T(8,128)} custom-call(s32[1024]{0:T(1024)S(1)} %mul.43.spot_ref, bf16[16,264,128]{2,1,0:T(8,128)(2,1)S(1)} %copy-done.1), custom_call_target="tpu_custom_call" | custom-call | flops 1000000 | bytes 33554432 | tf_op jit(solution)/shard_map/scatter/pallas_call | solution.py:494
  77.2 1.6 all-to-all-done.2
  78.7 0.0 copy-start.3
  78.7 0.7 copy-done.3
  79.4 17.0 %layer.1 = (f32[2,8192,128]{2,1,0:T(8,128)}, bf16[512,256]{1,0:T(8,128)(2,1)}) custom-call(bf16[4096,512]{1,0:T(8,128)(2,1)} %get-tuple-element.18.table_ref, bf16[512,4096]{1,0:T(8,128)(2,1)} %get-tuple-element.19.flipped_ref, bf16[512,256]{1,0:T(8,128)(2,1)} %bitcast.23, f32[2,8192,128]{2,1,0:T(8,128)} %bitcast.18, bf16[2,256,64]{2,1,0:T(8,128)(2,1)} %copy.18.up_ref, ...), custom_call_target="tpu_custom_call" | custom-call | flops 6442450944 | bytes 16777216 | tf_op jit(solution)/shard_map/layer/pallas_call | solution.py:606
  96.4 14.2 %all_to_all.31 = bf16[16,32,256]{2,1,0:T(8,128)(2,1)} all-to-all(bf16[16,32,256]{2,1,0:T(8,128)(2,1)} %bitcast.25), channel_id=1, replica_groups=mesh['groups'=2,'pen'=16] {'pen'}, dimensions={0} | all-to-all | bytes 524288 | tf_op jit(solution)/shard_map/all_to_all | solution.py:688
  110.6 4.8 %mix.3 = bf16[512,256]{1,0:T(8,128)(2,1)} custom-call(bf16[512,256]{1,0:T(8,128)(2,1)} %bitcast.21, bf16[128,64]{1,0:T(8,128)(2,1)} %constant.76.forward_ref, bf16[128,128]{1,0:T(8,128)(2,1)} %constant.82.inverse_ref, bf16[2,16,16,64,128]{4,3,2,1,0:T(8,128)(2,1)} %all_ref.3), custom_call_target="tpu_custom_call" | custom-call | flops 600000000 | bytes 4718592 | tf_op jit(solution)/shard_map/mix/pallas_call | solution.py:420
  115.4 3.9 %all-to-all-start.4 = ((bf16[16,32,256]{2,1,0:T(8,128)(2,1)}), bf16[16,32,256]{2,1,0:T(8,128)(2,1)S(1)}, u32[]{:S(2)}, u32[]{:S(2)}) async-start(bf16[16,32,256]{2,1,0:T(8,128)(2,1)} %bitcast.20), calls=%async_computation.4 | async-start | bytes 524288 | tf_op jit(solution)/shard_map/all_to_all | solution.py:688
  119.4 4.9 %gather.1.grid_ref = f32[4096,128]{1,0:T(8,128)S(1)} custom-call(s32[1024]{0:T(1024)S(1)} %mul.43.spot_ref, f32[16384,128]{1,0:T(8,128)} %bitcast.17), custom_call_target="tpu_custom_call" | custom-call | flops 1000000 | bytes 16777216 | tf_op jit(solution)/shard_map/gather/pallas_call | solution.py:523
  124.2 0.0 copy-start.2
  124.2 1.3 copy-done.2
  125.6 3.4 %all-to-all-done.4 = bf16[16,32,256]{2,1,0:T(8,128)(2,1)S(1)} async-done(((bf16[16,32,256]{2,1,0:T(8,128)(2,1)}), bf16[16,32,256]{2,1,0:T(8,128)(2,1)S(1)}, u32[]{:S(2)}, u32[]{:S(2)}) %all-to-all-start.4) | async-done | bytes 262176 | tf_op jit(solution)/shard_map/all_to_all | solution.py:688
  128.9 0.0 copy-start.4
  128.9 0.7 copy-done.4
  129.6 6.5 %last_layer.1 = bf16[16,256,128]{2,1,0:T(8,128)(2,1)} custom-call(bf16[512,2048]{1,0:T(8,128)(2,1)} %get-tuple-element.17.phase_ref, bf16[512,256]{1,0:T(8,128)(2,1)} %bitcast.24, f32[4096,128]{1,0:T(8,128)} %copy-done.2, bf16[2,256,64]{2,1,0:T(8,128)(2,1)} %copy.18.up_ref, bf16[2,64,256]{2,1,0:T(8,128)(2,1)} %down_ref.3), custom_call_target="tpu_custom_call" | custom-call | flops 2684354560 | bytes 5242880 | tf_op jit(solution)/shard_map/last_layer/pallas_call | solution.py:667
  136.2 30.1 %all_to_all.32.got_ref = bf16[16,256,128]{2,1,0:T(8,128)(2,1)} all-to-all(bf16[16,256,128]{2,1,0:T(8,128)(2,1)} %last_layer.1), channel_id=1, replica_groups=mesh['groups'=2,'pen'=16] {'pen'}, dimensions={0} | all-to-all | bytes 2097152 | tf_op jit(solution)/shard_map/all_to_all | solution.py:688
  166.2 6.7 %decode.1 = f32[64,2048]{1,0:T(8,128)} custom-call(bf16[16,256,128]{2,1,0:T(8,128)(2,1)} %all_to_all.32.got_ref, bf16[64,128,128]{2,1,0:T(8,128)(2,1)} %weight_ref.3), custom_call_target="tpu_custom_call" | custom-call | flops 268435456 | bytes 2097152 | tf_op jit(solution)/shard_map/decode/pallas_call | solution.py:247
  (5 shorter events, 0.1 us)
Async XLA Ops:
  8.4 31.1 %all-to-all-start = ((bf16[16,264,128]{2,1,0:T(8,128)(2,1)}), bf16[16,264,128]{2,1,0:T(8,128)(2,1)S(1)}, u32[]{:S(2)}, u32[]{:S(2)}) async-start(bf16[16,264,128]{2,1,0:T(8,128)(2,1)} %encode.1), calls=%async_computation | async-start | bytes 2162688 | tf_op jit(solution)/shard_map/all_to_all | solution.py:688
  39.5 1.0 copy-start
  60.4 8.8 %copy-start.5 = (bf16[2,256,64]{1,2,0:T(8,128)(2,1)S(1)}, bf16[2,256,64]{1,2,0:T(8,128)(2,1)}, u32[]{:S(2)}) copy-start(bf16[2,256,64]{1,2,0:T(8,128)(2,1)} %param.20) | copy-start | bytes 196612
  60.4 9.5 %copy-start.1 = (bf16[16,264,128]{2,1,0:T(8,128)(2,1)S(1)}, bf16[16,264,128]{2,1,0:T(8,128)(2,1)}, u32[]{:S(2)}) copy-start(bf16[16,264,128]{2,1,0:T(8,128)(2,1)} %copy-done) | copy-start | bytes 3244036
  65.2 13.5 %all-to-all-start.2 = ((bf16[16,32,256]{2,1,0:T(8,128)(2,1)}), bf16[16,32,256]{2,1,0:T(8,128)(2,1)S(1)}, u32[]{:S(2)}, u32[]{:S(2)}) async-start(bf16[16,32,256]{2,1,0:T(8,128)(2,1)} %bitcast.19), calls=%async_computation.2 | async-start | bytes 524288 | tf_op jit(solution)/shard_map/all_to_all | solution.py:688
  78.7 0.7 copy-start.3
  115.4 13.5 %all-to-all-start.4 = ((bf16[16,32,256]{2,1,0:T(8,128)(2,1)}), bf16[16,32,256]{2,1,0:T(8,128)(2,1)S(1)}, u32[]{:S(2)}, u32[]{:S(2)}) async-start(bf16[16,32,256]{2,1,0:T(8,128)(2,1)} %bitcast.20), calls=%async_computation.4 | async-start | bytes 524288 | tf_op jit(solution)/shard_map/all_to_all | solution.py:688
  124.2 1.3 copy-start.2
  128.9 0.7 copy-start.4

commit v3 on v2

--- a/solution.py
+++ b/solution.py
@@ -20,6 +20,7 @@
 GELU_K = math.sqrt(2.0 / math.pi)
 SCALE = 1.66575
 PAD = 8
+PARTS = 4
 
 F32 = jnp.float32
 BF16 = jnp.bfloat16
@@ -27,6 +28,22 @@
 
 def vmem_spec():
     return pl.BlockSpec(memory_space=pltpu.VMEM)
+
+
+def in_vmem(values):
+    return pltpu.with_memory_space_constraint(values, pltpu.VMEM)
+
+
+def in_hbm(values):
+    return pltpu.with_memory_space_constraint(values, pltpu.HBM)
+
+
+def any_spec():
+    return pl.BlockSpec(memory_space=pl.ANY)
+
+
+def limit(mebibytes):
+    return pltpu.CompilerParams(vmem_limit_bytes=mebibytes << 20)
 
 
 def cost(flops, size, transcendentals=0):
@@ -136,8 +153,8 @@
     return pl.pallas_call(
         table_kernel,
         out_shape=(
-            jax.ShapeDtypeStruct((NX // 2 * NY, columns), BF16),
-            jax.ShapeDtypeStruct((columns, NX // 2 * NY), BF16),
+            pltpu.HBM((NX // 2 * NY, columns), BF16),
+            pltpu.HBM((columns, NX // 2 * NY), BF16),
         ),
         grid=(NX // 2 // lines,),
         in_specs=[
@@ -151,17 +168,53 @@
             pl.BlockSpec((columns, rows), lambda i: (0, i)),
         ),
         cost_estimate=cost(4 * NX // 2 * NY * columns, 4 * NX // 2 * NY * columns),
+        compiler_params=limit(8),
         name="tables",
     )(first, second, y_cos, y_sin)
 
 
-def encode_kernel(feature_ref, weight_ref, spot_ref, out_ref, wide_ref):
+def copies_of(from_ref, to_ref, sem_ref):
+    step = from_ref.shape[0] // PARTS
+    return [
+        pltpu.make_async_copy(
+            from_ref.at[pl.ds(part * step, step)],
+            to_ref.at[pl.ds(part * step, step)],
+            sem_ref.at[part],
+        )
+        for part in range(PARTS)
+    ]
+
+
+def encode_kernel(
+    feature_hbm_ref, weight_hbm_ref, owner_ref, number_ref, out_ref, wide_ref, feature_ref,
+    weight_ref, sem_ref
+):
     devices = out_ref.shape[0]
     pairs, block = weight_ref.shape[0], weight_ref.shape[1]
+    points = pairs // NBR
     lines = block // NZ
     tiles = NZ // devices // 2
     rows = tiles * pairs * lines
+    copies = copies_of(weight_hbm_ref, weight_ref, sem_ref)
+    first_copy = pltpu.make_async_copy(feature_hbm_ref, feature_ref, sem_ref.at[PARTS])
+    for copy in [first_copy] + copies:
+        copy.start()
     lane = lax.broadcasted_iota(jnp.int32, (devices, 128), 1)
+    strip = NY // lines
+    target = owner_ref[...] * (NX * strip // devices) + number_ref[...]
+    y_at = (target % strip) * lines
+    spots = jnp.concatenate(
+        [
+            jnp.concatenate([target // strip] * lines, axis=1),
+            jnp.concatenate([y_at + line for line in range(lines)], axis=1),
+            jnp.zeros((6, 128), jnp.int32),
+        ],
+        axis=0,
+    )
+    spots = spots.astype(F32).astype(BF16)
+    for device in range(devices):
+        out_ref[device, rows : rows + 8, :] = spots
+    first_copy.wait()
 
     def one(point, carry):
         features = feature_ref[:, pl.ds(pl.multiple_of(point * block, block), block)]
@@ -175,7 +228,7 @@
                 for tile in range(tiles):
                     first = line * NZ + 2 * tile * devices
                     wide_ref[
-                        pl.ds((tile * pairs + pair) * lines + line, devices, stride=rows + PAD), :
+                        pl.ds((tile * lines + line) * pairs + pair, devices, stride=rows + PAD), :
                     ] = jnp.where(
                         lane < 64,
                         turned[first : first + devices],
@@ -183,28 +236,40 @@
                     )
         return carry
 
-    lax.fori_loop(0, pairs // NBR, one, 0)
+    for part, copy in enumerate(copies):
+        copy.wait()
+        lax.fori_loop(
+            part * points // PARTS, (part + 1) * points // PARTS, one, 0, unroll=2
+        )
     for device in range(devices):
         base = device * (rows + PAD)
         out_ref[device, 0:rows, :] = wide_ref[base : base + rows, :].astype(BF16)
-        out_ref[device, rows : rows + 8, :] = spot_ref[...].astype(BF16)
-
-
-def encode(features, weights, spots, devices):
+
+
+def encode(features, weights, owners, numbers, devices):
     pairs, block = weights.shape[0], weights.shape[1]
     rows = NZ // devices // 2 * pairs * (block // NZ)
     return pl.pallas_call(
         encode_kernel,
         out_shape=jax.ShapeDtypeStruct((devices, rows + 8, 128), BF16),
-        in_specs=[vmem_spec()] * 3,
+        in_specs=[any_spec()] * 2 + [vmem_spec()] * 2,
         out_specs=vmem_spec(),
-        scratch_shapes=[pltpu.VMEM((devices * (rows + PAD), 128), F32)],
+        scratch_shapes=[
+            pltpu.VMEM((devices * (rows + PAD), 128), F32),
+            pltpu.VMEM(features.shape, BF16),
+            pltpu.VMEM(weights.shape, BF16),
+            pltpu.SemaphoreType.DMA((PARTS + 1,)),
+        ],
+        compiler_params=limit(10),
         cost_estimate=cost(4 * pairs * block * block * 64, pairs * block * block * 2),
         name="encode",
-    )(features, weights, spots)
-
-
-def decode_kernel(got_ref, weight_ref, out_ref, wide_ref):
+    )(in_hbm(features), in_hbm(weights), owners, numbers)
+
+
+def decode_kernel(got_ref, weight_hbm_ref, out_ref, wide_ref, weight_ref, sem_ref):
+    copies = copies_of(weight_hbm_ref, weight_ref, sem_ref)
+    for copy in copies:
+        copy.start()
     devices, rows, _ = got_ref.shape
     pairs, block = weight_ref.shape[0], weight_ref.shape[1]
     lines = block // NZ
@@ -222,7 +287,7 @@
             for line in range(lines):
                 for tile in range(tiles):
                     values = wide_ref[
-                        pl.ds((tile * pairs + pair) * lines + line, devices, stride=rows + PAD), :
+                        pl.ds((tile * lines + line) * pairs + pair, devices, stride=rows + PAD), :
                     ]
                     pieces.append(jnp.where(lane < 64, values, 0.0))
                     pieces.append(jnp.where(lane < 64, 0.0, values))
@@ -238,7 +303,12 @@
         )
         return carry
 
-    lax.fori_loop(0, pairs // NBR, one, 0)
+    points = pairs // NBR
+    for part, copy in enumerate(copies):
+        copy.wait()
+        lax.fori_loop(
+            part * points // PARTS, (part + 1) * points // PARTS, one, 0, unroll=2
+        )
 
 
 def decode(got, weights, channels):
@@ -247,32 +317,33 @@
     return pl.pallas_call(
         decode_kernel,
         out_shape=jax.ShapeDtypeStruct((channels, pairs // NBR * block), F32),
-        in_specs=[vmem_spec()] * 2,
+        in_specs=[vmem_spec(), any_spec()],
         out_specs=vmem_spec(),
-        scratch_shapes=[pltpu.VMEM((devices * (rows + PAD), 128), F32)],
+        scratch_shapes=[
+            pltpu.VMEM((devices * (rows + PAD), 128), F32),
+            pltpu.VMEM(weights.shape, BF16),
+            pltpu.SemaphoreType.DMA((PARTS,)),
+        ],
         cost_estimate=cost(4 * pairs * block * block * 64, pairs * block * block * 2),
+        compiler_params=limit(12),
         name="decode",
-    )(got, weights)
-
-
-def pair_spectrum_kernel(modes_here, got_ref, x_ref, y_ref, out_ref, phase_ref):
-    devices = got_ref.shape[0]
-    rows = got_ref.shape[1] - 8
-    tiles = out_ref.shape[1] // 128
-    lanes = rows // tiles
+    )(got, in_hbm(weights))
+
+
+def look_up(table_ref, count, spot):
+    every = lax.broadcasted_iota(jnp.int32, (count, spot.shape[1]), 0)
+    values = dot(table_ref[...], (every == spot).astype(F32).astype(BF16))
+    half = values.shape[0] // 2
+    return values[0:half] + values[half:]
+
+
+def fill_phases(modes_here, devices, spots, x_ref, y_ref, phase_ref):
     half = MX // 2
-    x_all = lax.broadcasted_iota(jnp.int32, (NX, lanes), 0)
-    y_all = lax.broadcasted_iota(jnp.int32, (NY, lanes), 0)
-
-    def look_up(table_ref, chosen):
-        values = dot(table_ref[...], chosen.astype(F32).astype(BF16))
-        count = values.shape[0] // 2
-        return values[0:count] + values[count:]
-
-    for source in range(devices):
-        spot = got_ref[source, rows : rows + 8, :].astype(F32)
-        x_turn = look_up(x_ref, x_all == spot[0:1, :].astype(jnp.int32))
-        y_turn = look_up(y_ref, y_all == spot[1:2, :].astype(jnp.int32))
+    for source, spot in enumerate(spots):
+        spot = spot.astype(F32)
+        x_turn = look_up(x_ref, NX, spot[0:1, :].astype(jnp.int32))
+        y_turn = look_up(y_ref, NY, spot[1:2, :].astype(jnp.int32))
+        lanes = spot.shape[1]
         place = slice(source * lanes, (source + 1) * lanes)
         for device in range(devices):
             row = (device * modes_here) // MZ
@@ -285,6 +356,19 @@
                 )
                 base = (2 * device + parity) * MX
                 phase_ref[base : base + MX, place] = both.astype(BF16)
+
+
+def pair_spectrum_kernel(
+    modes_here, got_ref, x_ref, y_ref, out_ref, phase_hbm_ref, phase_ref, sem_ref
+):
+    devices = got_ref.shape[0]
+    rows = got_ref.shape[1] - 8
+    tiles = out_ref.shape[1] // 128
+    lanes = rows // tiles
+    spots = [got_ref[source, rows : rows + 8, :] for source in range(devices)]
+    fill_phases(modes_here, devices, spots, x_ref, y_ref, phase_ref)
+    copy = pltpu.make_async_copy(phase_ref, phase_hbm_ref, sem_ref)
+    copy.start()
     values = jnp.concatenate(
         [
             jnp.concatenate(
@@ -299,9 +383,10 @@
         axis=1,
     )
     out_ref[...] = dot(phase_ref[...], values).astype(BF16)
-
-
-def pair_spectrum(got, modes_here, lanes):
+    copy.wait()
+
+
+def pair_spectrum(got, tables, modes_here, lanes):
     devices, rows, _ = got.shape
     count = devices * (rows - 8) // (lanes // 128)
     columns = devices * 2 * MX
@@ -309,13 +394,15 @@
         functools.partial(pair_spectrum_kernel, modes_here),
         out_shape=(
             jax.ShapeDtypeStruct((columns, lanes), BF16),
-            jax.ShapeDtypeStruct((columns, count), BF16),
+            pltpu.HBM((columns, count), BF16),
         ),
         in_specs=[vmem_spec()] * 3,
-        out_specs=(vmem_spec(), vmem_spec()),
+        out_specs=(vmem_spec(), any_spec()),
+        scratch_shapes=[pltpu.VMEM((columns, count), BF16), pltpu.SemaphoreType.DMA],
+        compiler_params=limit(10),
         cost_estimate=cost(2 * columns * count * lanes, got.size * 2 + columns * count * 2),
         name="pair_spectrum",
-    )(got, *lookup_tables())
+    )(got, *tables)
 
 
 def row_of(wave, part):
@@ -325,16 +412,18 @@
 
 
 def mix_kernel(
-    devices, number, got_ref, forward_ref, inverse_ref, all_ref, out_ref, wide_ref, back_ref,
-    weight_ref, sem_ref
+    devices, number, got_ref, forward_ref, inverse_ref, weight_hbm_ref, out_ref, wide_ref,
+    back_ref, weight_ref, sem_ref
 ):
     modes_here, _, channels, _ = weight_ref.shape
-    pieces_at = [slice(first, first + 4) for first in range(0, MX, 4)]
+    each = MX // PARTS
     copies = [
         pltpu.make_async_copy(
-            all_ref.at[number, :, place], weight_ref.at[:, place], sem_ref.at[index]
+            weight_hbm_ref.at[number, :, pl.ds(part * each, each)],
+            weight_ref.at[:, pl.ds(part * each, each)],
+            sem_ref.at[part],
         )
-        for index, place in enumerate(pieces_at)
+        for part in range(PARTS)
     ]
     for copy in copies:
         copy.start()
@@ -377,8 +466,8 @@
     mixed = []
     for wave in range(MX):
         pieces = []
-        if wave % 4 == 0:
-            copies[wave // 4].wait()
+        if wave % each == 0:
+            copies[wave // each].wait()
         for first in range(0, modes_here, group):
             now = spread[wave][2 * first : 2 * (first + group), :]
             left = jnp.concatenate(
@@ -420,18 +509,19 @@
     return pl.pallas_call(
         functools.partial(mix_kernel, devices, number),
         out_shape=jax.ShapeDtypeStruct((rows, lanes), BF16),
-        in_specs=[vmem_spec()] * 3 + [pl.BlockSpec(memory_space=pl.ANY)],
+        in_specs=[vmem_spec()] * 3 + [any_spec()],
         out_specs=vmem_spec(),
         scratch_shapes=[pltpu.VMEM((lanes // 128, rows, 128), F32)] * 2
-        + [pltpu.VMEM(weights.shape[1:], BF16), pltpu.SemaphoreType.DMA((4,))],
+        + [pltpu.VMEM(weights.shape[1:], BF16), pltpu.SemaphoreType.DMA((PARTS,))],
+        compiler_params=limit(12),
         cost_estimate=cost(6e8, weights.size + rows * lanes * 4),
         name="mix",
-    )(got, forward, inverse, weights)
+    )(got, forward, inverse, in_hbm(weights))
 
 
 def spread_weights(up_ref, down_ref, up_wide_ref, down_wide_ref):
-    hidden, channels = up_ref.shape[1:]
-    up = up_ref[0].T
+    channels, hidden = up_ref.shape[1:]
+    up = up_ref[0]
     down = (down_ref[0].astype(F32) * 0.5).astype(BF16).T
     up_wide_ref[...] = jnp.zeros_like(up_wide_ref)
     down_wide_ref[...] = jnp.zeros_like(down_wide_ref)
@@ -461,19 +551,21 @@
     return totals
 
 
-def scatter_kernel(spot_ref, got_ref, out_ref, wide_ref):
+def scatter_kernel(spot_ref, got_ref, out_hbm_ref, wide_ref, out_ref, sem_ref):
     devices, rows, _ = got_ref.shape
     rows = rows - 8
     pairs = spot_ref.shape[0] // devices
     size = rows // pairs
-    lines = size // TILES(out_ref)
     tiles = TILES(out_ref)
+    lines = size // tiles
     out_ref[...] = jnp.zeros_like(out_ref)
     for source in range(devices):
         for tile in range(tiles):
-            wide_ref[pl.ds(source * rows + tile, pairs * lines, stride=tiles), :] = got_ref[
-                source, tile * pairs * lines : (tile + 1) * pairs * lines, :
-            ].astype(F32)
+            for line in range(lines):
+                first = (tile * lines + line) * pairs
+                wide_ref[pl.ds(source * rows + line * tiles + tile, pairs, stride=size), :] = (
+                    got_ref[source, first : first + pairs, :].astype(F32)
+                )
 
     @pl.loop(0, devices)
     def _(source):
@@ -484,30 +576,41 @@
                 out_ref[pl.ds(base, size), :] + wide_ref[pl.ds(here, size), :]
             )
 
+    copy = pltpu.make_async_copy(out_ref, out_hbm_ref, sem_ref)
+    copy.start()
+    copy.wait()
+
 
 def TILES(ref):
     return ref.shape[0] // (NX * NY)
+
+
+def smem_spec():
+    return pl.BlockSpec(memory_space=pltpu.SMEM)
 
 
 def scatter(spots, got, tiles):
     devices, rows, _ = got.shape
     return pl.pallas_call(
         scatter_kernel,
-        out_shape=jax.ShapeDtypeStruct((NX * NY * tiles, 128), F32),
-        grid_spec=pltpu.PrefetchScalarGridSpec(
-            num_scalar_prefetch=1,
-            grid=(1,),
-            in_specs=[pl.BlockSpec(got.shape, lambda i, s: (0, 0, 0))],
-            out_specs=pl.BlockSpec((NX * NY * tiles, 128), lambda i, s: (0, 0)),
-            scratch_shapes=[pltpu.VMEM((devices * (rows - 8), 128), F32)],
-        ),
-        compiler_params=pltpu.CompilerParams(vmem_limit_bytes=48 * 1024 * 1024),
+        out_shape=pltpu.HBM((NX * NY * tiles, 128), F32),
+        in_specs=[smem_spec(), vmem_spec()],
+        out_specs=any_spec(),
+        scratch_shapes=[
+            pltpu.VMEM((devices * (rows - 8), 128), F32),
+            pltpu.VMEM((NX * NY * tiles, 128), F32),
+            pltpu.SemaphoreType.DMA,
+        ],
+        compiler_params=limit(14),
         cost_estimate=cost(1e6, NX * NY * tiles * 128 * 16),
         name="scatter",
     )(spots, got)
 
 
-def gather_kernel(size, devices, spot_ref, grid_ref, out_ref):
+def gather_kernel(size, devices, spot_ref, grid_hbm_ref, out_ref, grid_ref, sem_ref):
+    copy = pltpu.make_async_copy(grid_hbm_ref, grid_ref, sem_ref)
+    copy.start()
+    copy.wait()
     pairs = spot_ref.shape[0] // devices
 
     @pl.loop(0, devices)
@@ -522,17 +625,14 @@
     count = spots.shape[0]
     return pl.pallas_call(
         functools.partial(gather_kernel, size, devices),
-        out_shape=jax.ShapeDtypeStruct((count * size, 128), F32),
-        grid_spec=pltpu.PrefetchScalarGridSpec(
-            num_scalar_prefetch=1,
-            grid=(1,),
-            in_specs=[pl.BlockSpec(grid.shape, lambda i, s: (0, 0))],
-            out_specs=pl.BlockSpec((count * size, 128), lambda i, s: (0, 0)),
-        ),
-        compiler_params=pltpu.CompilerParams(vmem_limit_bytes=48 * 1024 * 1024),
+        out_shape=pltpu.VMEM((count * size, 128), F32),
+        in_specs=[smem_spec(), any_spec()],
+        out_specs=vmem_spec(),
+        scratch_shapes=[pltpu.VMEM(grid.shape, F32), pltpu.SemaphoreType.DMA],
+        compiler_params=limit(12),
         cost_estimate=cost(1e6, grid.size * 8),
         name="gather",
-    )(spots, grid)
+    )(spots, in_hbm(grid))
 
 
 def layer_kernel(
@@ -590,7 +690,7 @@
 
 
 def wide_weights(up):
-    hidden, channels = up.shape[1:]
+    channels, hidden = up.shape[1:]
     return [
         pltpu.VMEM((2 * channels, 2 * hidden), BF16),
         pltpu.VMEM((2 * hidden, 2 * channels), BF16),
@@ -606,7 +706,7 @@
     return pl.pallas_call(
         layer_kernel,
         out_shape=(
-            jax.ShapeDtypeStruct((2, cells * tiles, 128), F32),
+            pltpu.HBM((2, cells * tiles, 128), F32),
             jax.ShapeDtypeStruct((columns, lanes), BF16),
         ),
         grid=(cells // rows,),
@@ -625,14 +725,18 @@
         + wide_weights(up)
         + [pltpu.VMEM((2, columns // 2, lanes), BF16)],
         cost_estimate=cost(
-            4 * cells * columns * lanes + 16 * cells * lanes * up.shape[1],
+            4 * cells * columns * lanes + 16 * cells * lanes * up.shape[2],
             cells * (columns * 4 + lanes * 8),
         ),
+        compiler_params=limit(22),
         name="layer",
-    )(table, flipped, modes, grid.reshape(2, cells * tiles, 128), up, down)
-
-
-def last_kernel(phase_ref, modes_ref, grid_ref, up_ref, down_ref, out_ref, up_wide_ref, down_wide_ref):
+    )(
+        in_hbm(table), in_hbm(flipped), modes, in_hbm(grid.reshape(2, cells * tiles, 128)),
+        up, down,
+    )
+
+
+def last_kernel(lines, phase_ref, modes_ref, grid_ref, up_ref, down_ref, out_ref, up_wide_ref, down_wide_ref):
     group, rows, _ = out_ref.shape
     tiles = modes_ref.shape[1] // 128
     rows = rows // tiles
@@ -644,8 +748,19 @@
     spectral = lax.dot_general(
         phase_ref[...], modes_ref[...], (((0,), (0,)), ((), ())), preferred_element_type=F32
     )
+    size = tiles * lines
+    pairs = rows // lines
     summed = [
-        grid_ref[pl.ds(tile, group * rows, stride=tiles), :]
+        jnp.concatenate(
+            [
+                grid_ref[
+                    pl.ds(source * pairs * size + line * tiles + tile, pairs, stride=size), :
+                ]
+                for source in range(group)
+                for line in range(lines)
+            ],
+            axis=0,
+        )
         + spectral[:, tile * 128 : (tile + 1) * 128]
         for tile in range(tiles)
     ]
@@ -658,14 +773,14 @@
             ]
 
 
-def last_layer(phases, modes, grid, up, down, number, devices):
+def last_layer(phases, modes, grid, up, down, number, devices, lines):
     columns, count = phases.shape
     lanes = modes.shape[1]
     tiles = lanes // 128
     group = 8
     rows = count // devices
     return pl.pallas_call(
-        last_kernel,
+        functools.partial(last_kernel, lines),
         out_shape=jax.ShapeDtypeStruct((devices, rows * tiles, 128), BF16),
         grid=(devices // group,),
         in_specs=[
@@ -677,11 +792,12 @@
         out_specs=pl.BlockSpec((group, rows * tiles, 128), lambda i: (i, 0, 0)),
         scratch_shapes=wide_weights(up),
         cost_estimate=cost(
-            2 * count * columns * lanes + 16 * count * lanes * up.shape[1],
+            2 * count * columns * lanes + 16 * count * lanes * up.shape[2],
             count * (columns * 2 + lanes * 6),
         ),
+        compiler_params=limit(24),
         name="last_layer",
-    )(phases, modes, grid, up, down)
+    )(in_hbm(phases), modes, in_vmem(grid), up, down)
 
 
 def exchange(values):
@@ -698,30 +814,30 @@
     tiles = lanes // 128
     columns = devices * 2 * MX
 
-    target = pair_owner[:, 0] * (NX * NY // lines // devices) + pair_block
-    x_at = jnp.repeat(target // (NY // lines), lines)
-    y_at = (target % (NY // lines))[:, None] * lines + jnp.arange(lines, dtype=jnp.int32)
-    spots = jnp.stack([x_at, y_at.reshape(-1)] + [jnp.zeros_like(x_at)] * 6).astype(F32)
-
-    got = exchange(encode(point_feat, pair_kernel, spots, devices))
+    up = mlp_up.transpose(0, 2, 1)
+    send = encode(
+        point_feat, pair_kernel, pair_owner.reshape(1, pairs), pair_block.reshape(1, pairs), devices
+    )
+    got = exchange(send)
 
     table, flipped = grid_tables(devices, modes_here)
+    got, table, flipped = lax.optimization_barrier((got, table, flipped))
     forward, inverse = depth_tables(devices, modes_here)
-    got, table, flipped = lax.optimization_barrier((got, table, flipped))
-    here = got[:, -8:-6, 0 : pairs * lines : lines].astype(jnp.int32)
+    lookups = lookup_tables()
+    here = got[:, -8:-6, 0:pairs].astype(jnp.int32)
     rows = ((here[:, 0, :] * NY + here[:, 1, :]) * tiles).reshape(devices * pairs)
 
-    spectrum, phases = pair_spectrum(got, modes_here, lanes)
+    spectrum, phases = pair_spectrum(got, lookups, modes_here, lanes)
     grid = scatter(rows, got, tiles)
     modes = exchange(spectrum.reshape(devices, 2 * MX, lanes)).reshape(columns, lanes)
     modes = mix(modes, forward, inverse, spec_weight, 0, devices)
     modes = exchange(modes.reshape(devices, 2 * MX, lanes)).reshape(columns, lanes)
-    grid, spectrum = layer(table, flipped, modes, grid, mlp_up, mlp_down, 0)
+    grid, spectrum = layer(table, flipped, modes, grid, up, mlp_down, 0)
     listed = gather(rows, grid.reshape(-1, 128), lines * tiles, devices)
     modes = exchange(spectrum.reshape(devices, 2 * MX, lanes)).reshape(columns, lanes)
     modes = mix(modes, forward, inverse, spec_weight, 1, devices)
     modes = exchange(modes.reshape(devices, 2 * MX, lanes)).reshape(columns, lanes)
-    result = last_layer(phases, modes, listed, mlp_up, mlp_down, 1, devices)
+    result = last_layer(phases, modes, listed, up, mlp_down, 1, devices, lines)
     return decode(exchange(result), pair_kernel, channels)
 
 

time: 174 us -> 160 us (0.920)
  Pallas kernels: 68.1 us -> 59.1 us
  local copies, waits for them, and re-layouts: 5.42 us -> 1.43 us
  waiting for transfers between devices: 22.1 us -> 25.9 us
  blocking collectives: 60.5 us -> 57.2 us
    all_to_all x3, waiting for transfers between devices: 22.1 us -> 25.9 us  [exchange(): lax.all_to_all(values, 'pen', split_axis=0, concat_axis=0, tiled=True)]
    all_to_all x3, blocking collectives: 60.5 us -> 57.2 us  [exchange(): lax.all_to_all(values, 'pen', split_axis=0, concat_axis=0, tiled=True)]
    unnamed x13 -> x24, local copies, waits for them, and re-layouts: 4.47 us -> 1.36 us
    pallas_call x4, Pallas kernels: 36.9 us -> 34.1 us  [the longest x1 16.8 us: layer(): pl.pallas_call(layer_kernel, out_shape=(pltpu.HBM((2, cells * tiles, 128)...]
    pallas_call x1, Pallas kernels: 6.67 us -> 4.5 us  [decode(): pl.pallas_call(decode_kernel, out_shape=jax.ShapeDtypeStruct((channels, p...]
  transfers between devices with their start and end apart: 3 -> 3, of which waited for: 3 -> 3; matrix products, arithmetic and copies ran while one was open for 1% -> 0% of each run, Pallas kernels for 11% -> 11%
where the time goes in v3:
time: 160 us; the launch traced here: 159 us
  Pallas kernels  59.1 us (37%)
  blocking collectives  57.2 us (36%)
  waiting for transfers between devices  25.9 us (16%)
  starting transfers between devices  15.4 us (10%)
    all_to_all x3, blocking collectives, exchange(): lax.all_to_all(values, 'pen', split_axis=0, concat_axis=0, tiled=True)  57.2 us
    all_to_all x3, waiting for transfers between devices, exchange(): lax.all_to_all(values, 'pen', split_axis=0, concat_axis=0, tiled=True)  25.9 us
    pallas_call x1, Pallas kernels, layer(): pl.pallas_call(layer_kernel, out_shape=(pltpu.HBM((2, cells * tiles, 128)...  16.8 us
    all_to_all x3, starting transfers between devices, exchange(): lax.all_to_all(values, 'pen', split_axis=0, concat_axis=0, tiled=True)  15.4 us
    pallas_call x2, Pallas kernels, mix(): pl.pallas_call(functools.partial(mix_kernel, devices, number), out_shape=...  8.24 us
    pallas_call x1, Pallas kernels, scatter(): pl.pallas_call(scatter_kernel, out_shape=pltpu.HBM((NX * NY * tiles, 128)...  6.78 us
    pallas_call x1, Pallas kernels, last_layer(): pl.pallas_call(functools.partial(last_kernel, lines), out_shape=jax.Shape...  5.3 us
    pallas_call x1, Pallas kernels, grid_tables(): pl.pallas_call(table_kernel, out_shape=(pltpu.HBM((NX // 2 * NY, columns)...  5.21 us
  transfers between devices with their start and end apart: 3, of which 3 were waited for; matrix products, arithmetic and copies ran while one was open for 0% of the time, Pallas kernels for 11%

profile of v3, /device:TPU:1, one launch (start us, length us, event | category | flops | bytes accessed | tf_op | source)
XLA Modules:
  0.0 159.3 jit_solution(953997692918491355)
XLA Ops:
  0.0 0.0 copy-start.6
  0.0 0.7 copy-done.6
  0.7 0.0 copy-start.7
  0.7 0.7 copy-done.7
  1.3 0.0 copy-start.2
  1.3 0.0 copy-start.3
  1.3 0.0 copy-start.4
  1.3 0.0 copy-start.5
  1.3 4.9 %encode.1 = bf16[16,264,128]{2,1,0:T(8,128)(2,1)} custom-call(bf16[64,2048]{1,0:T(8,128)(2,1)} %feature_hbm_ref.1, bf16[64,128,128]{2,1,0:T(8,128)(2,1)} %weight_hbm_ref.7, s32[1,64]{1,0:T(1,128)S(1)} %bitcast.19, s32[1,64]{1,0:T(1,128)S(1)} %bitcast.20), custom_call_target="tpu_custom_call" | custom-call | flops 268435456 | bytes 2097152 | tf_op jit(solution)/shard_map/encode/pallas_call | solution.py:252
  6.2 0.0 copy-start.10
  6.2 0.0 copy-start.11
  6.3 0.0 copy-start
  6.3 0.0 copy-start.1
  6.3 7.5 %all-to-all-start = ((bf16[16,264,128]{2,1,0:T(8,128)(2,1)}), bf16[16,264,128]{2,1,0:T(8,128)(2,1)S(1)}, u32[]{:S(2)}, u32[]{:S(2)}) async-start(bf16[16,264,128]{2,1,0:T(8,128)(2,1)} %encode.1), calls=%async_computation | async-start | bytes 2162688 | tf_op jit(solution)/shard_map/all_to_all | solution.py:804
  13.8 0.0 copy-done.2
  13.8 0.0 copy-done.3
  13.8 0.0 copy-done.4
  13.8 0.0 copy-done.5
  13.8 5.2 %tables.1 = (bf16[4096,512]{1,0:T(8,128)(2,1)}, bf16[512,4096]{1,0:T(8,128)(2,1)}) custom-call(f32[64,512]{1,0:T(8,128)S(1)} %copy-done.5, f32[64,512]{1,0:T(8,128)S(1)} %copy-done.4, f32[64,512]{1,0:T(8,128)S(1)} %copy-done.3, f32[64,512]{1,0:T(8,128)S(1)} %copy-done.2), custom_call_target="tpu_custom_call" | custom-call | flops 8388608 | bytes 8388608 | tf_op jit(solution)/shard_map/tables/pallas_call | solution.py:153
  19.0 18.5 %all-to-all-done.got_ref = bf16[16,264,128]{2,1,0:T(8,128)(2,1)S(1)} async-done(((bf16[16,264,128]{2,1,0:T(8,128)(2,1)}), bf16[16,264,128]{2,1,0:T(8,128)(2,1)S(1)}, u32[]{:S(2)}, u32[]{:S(2)}) %all-to-all-start) | async-done | bytes 1081376 | tf_op jit(solution)/shard_map/all_to_all | solution.py:804
  37.5 0.0 copy-done.10
  37.5 0.0 copy-done.11
  37.5 2.4 %pair_spectrum.1 = (bf16[512,256]{1,0:T(8,128)(2,1)S(1)}, bf16[512,2048]{1,0:T(8,128)(2,1)}) custom-call(bf16[16,264,128]{2,1,0:T(8,128)(2,1)S(1)} %all-to-all-done.got_ref, bf16[64,128]{1,0:T(8,128)(2,1)S(1)} %copy-done.11, bf16[64,64]{1,0:T(8,128)(2,1)S(1)} %copy-done.10), custom_call_target="tpu_custom_call" | custom-call | flops 536870912 | bytes 3178496 | tf_op jit(solution)/shard_map/pair_spectrum/pallas_call | solution.py:393
  40.0 15.9 %all_to_all.30 = bf16[16,32,256]{2,1,0:T(8,128)(2,1)S(1)} all-to-all(bf16[16,32,256]{2,1,0:T(8,128)(2,1)S(1)} %bitcast.18), channel_id=1, replica_groups=mesh['groups'=2,'pen'=16] {'pen'}, dimensions={0} | all-to-all | bytes 524288 | tf_op jit(solution)/shard_map/all_to_all | solution.py:804
  55.9 0.0 copy-done
  55.9 0.0 copy-done.1
  55.9 4.2 %mix.2 = bf16[512,256]{1,0:T(8,128)(2,1)} custom-call(bf16[512,256]{1,0:T(8,128)(2,1)S(1)} %bitcast.14, bf16[128,64]{1,0:T(8,128)(2,1)S(1)} %copy-done.1, bf16[128,128]{1,0:T(8,128)(2,1)S(1)} %copy-done, bf16[2,16,16,64,128]{4,3,2,1,0:T(8,128)(2,1)} %weight_hbm_ref.6), custom_call_target="tpu_custom_call" | custom-call | flops 600000000 | bytes 4718592 | tf_op jit(solution)/shard_map/mix/pallas_call | solution.py:509
  60.1 3.9 %all-to-all-start.2 = ((bf16[16,32,256]{2,1,0:T(8,128)(2,1)}), bf16[16,32,256]{2,1,0:T(8,128)(2,1)S(1)}, u32[]{:S(2)}, u32[]{:S(2)}) async-start(bf16[16,32,256]{2,1,0:T(8,128)(2,1)} %bitcast.4), calls=%async_computation.2 | async-start | bytes 524288 | tf_op jit(solution)/shard_map/all_to_all | solution.py:804
  64.1 0.1 mul.22.spot_ref
  64.2 0.0 copy-start.8
  64.2 0.0 copy-start.9
  64.2 6.8 %scatter.1 = f32[16384,128]{1,0:T(8,128)} custom-call(s32[1024]{0:T(1024)S(1)} %mul.22.spot_ref, bf16[16,264,128]{2,1,0:T(8,128)(2,1)S(1)} %all-to-all-done.got_ref), custom_call_target="tpu_custom_call" | custom-call | flops 1000000 | bytes 33554432 | tf_op jit(solution)/shard_map/scatter/pallas_call | solution.py:594
  71.0 2.7 %all-to-all-done.2 = bf16[16,32,256]{2,1,0:T(8,128)(2,1)S(1)} async-done(((bf16[16,32,256]{2,1,0:T(8,128)(2,1)}), bf16[16,32,256]{2,1,0:T(8,128)(2,1)S(1)}, u32[]{:S(2)}, u32[]{:S(2)}) %all-to-all-start.2) | async-done | bytes 262176 | tf_op jit(solution)/shard_map/all_to_all | solution.py:804
  73.6 0.0 copy-done.8
  73.6 0.0 copy-done.9
  73.6 16.8 %layer.1 = (f32[2,8192,128]{2,1,0:T(8,128)}, bf16[512,256]{1,0:T(8,128)(2,1)S(1)}) custom-call(bf16[4096,512]{1,0:T(8,128)(2,1)} %get-tuple-element.18.table_ref, bf16[512,4096]{1,0:T(8,128)(2,1)} %get-tuple-element.19.flipped_ref, bf16[512,256]{1,0:T(8,128)(2,1)S(1)} %bitcast.15, f32[2,8192,128]{2,1,0:T(8,128)} %bitcast.24, ...), custom_call_target="tpu_custom_call" | custom-call | flops 6442450944 | bytes 16777216 | tf_op jit(solution)/shard_map/layer/pallas_call | solution.py:706
  90.5 12.8 %all_to_all.31 = bf16[16,32,256]{2,1,0:T(8,128)(2,1)S(1)} all-to-all(bf16[16,32,256]{2,1,0:T(8,128)(2,1)S(1)} %bitcast.17), channel_id=1, replica_groups=mesh['groups'=2,'pen'=16] {'pen'}, dimensions={0} | all-to-all | bytes 524288 | tf_op jit(solution)/shard_map/all_to_all | solution.py:804
  103.2 4.1 %mix.3 = bf16[512,256]{1,0:T(8,128)(2,1)} custom-call(bf16[512,256]{1,0:T(8,128)(2,1)S(1)} %bitcast.13, bf16[128,64]{1,0:T(8,128)(2,1)S(1)} %copy-done.1, bf16[128,128]{1,0:T(8,128)(2,1)S(1)} %copy-done, bf16[2,16,16,64,128]{4,3,2,1,0:T(8,128)(2,1)} %weight_hbm_ref.6), custom_call_target="tpu_custom_call" | custom-call | flops 600000000 | bytes 4718592 | tf_op jit(solution)/shard_map/mix/pallas_call | solution.py:509
  107.3 3.9 %all-to-all-start.4 = ((bf16[16,32,256]{2,1,0:T(8,128)(2,1)}), bf16[16,32,256]{2,1,0:T(8,128)(2,1)S(1)}, u32[]{:S(2)}, u32[]{:S(2)}) async-start(bf16[16,32,256]{2,1,0:T(8,128)(2,1)} %bitcast.10), calls=%async_computation.4 | async-start | bytes 524288 | tf_op jit(solution)/shard_map/all_to_all | solution.py:804
  111.2 4.9 %gather.1.grid_ref = f32[4096,128]{1,0:T(8,128)S(1)} custom-call(s32[1024]{0:T(1024)S(1)} %mul.22.spot_ref, f32[16384,128]{1,0:T(8,128)} %bitcast.23), custom_call_target="tpu_custom_call" | custom-call | flops 1000000 | bytes 16777216 | tf_op jit(solution)/shard_map/gather/pallas_call | solution.py:626
  116.1 4.7 %all-to-all-done.4 = bf16[16,32,256]{2,1,0:T(8,128)(2,1)S(1)} async-done(((bf16[16,32,256]{2,1,0:T(8,128)(2,1)}), bf16[16,32,256]{2,1,0:T(8,128)(2,1)S(1)}, u32[]{:S(2)}, u32[]{:S(2)}) %all-to-all-start.4) | async-done | bytes 262176 | tf_op jit(solution)/shard_map/all_to_all | solution.py:804
  120.8 5.3 %last_layer.1 = bf16[16,256,128]{2,1,0:T(8,128)(2,1)S(1)} custom-call(bf16[512,2048]{1,0:T(8,128)(2,1)} %get-tuple-element.17.phase_ref, bf16[512,256]{1,0:T(8,128)(2,1)S(1)} %bitcast.16, f32[4096,128]{1,0:T(8,128)S(1)} %gather.1.grid_ref, bf16[2,64,256]{2,1,0:T(8,128)(2,1)S(1)} %bitcast.22, bf16[2,64,256]{2,1,0:T(8,128)(2,1)S(1)} %copy-done.9), custom_call_target="tpu_custom_call" | custom-call | flops 2684354560 | bytes 5242880 | tf_op jit(solution)/shard_map/last_layer/pallas_call | solution.py:782
  126.1 28.5 %all_to_all.32.got_ref = bf16[16,256,128]{2,1,0:T(8,128)(2,1)S(1)} all-to-all(bf16[16,256,128]{2,1,0:T(8,128)(2,1)S(1)} %last_layer.1), channel_id=1, replica_groups=mesh['groups'=2,'pen'=16] {'pen'}, dimensions={0} | all-to-all | bytes 2097152 | tf_op jit(solution)/shard_map/all_to_all | solution.py:804
  154.7 4.5 %decode.1 = f32[64,2048]{1,0:T(8,128)} custom-call(bf16[16,256,128]{2,1,0:T(8,128)(2,1)S(1)} %all_to_all.32.got_ref, bf16[64,128,128]{2,1,0:T(8,128)(2,1)} %weight_hbm_ref.7), custom_call_target="tpu_custom_call" | custom-call | flops 268435456 | bytes 2097152 | tf_op jit(solution)/shard_map/decode/pallas_call | solution.py:317
  (2 shorter events, 0.0 us)
Async XLA Ops:
  0.0 0.7 copy-start.6
  0.7 0.7 copy-start.7
  1.3 12.5 %copy-start.2 = (f32[64,512]{1,0:T(8,128)S(1)}, f32[64,512]{1,0:T(8,128)}, u32[]{:S(2)}) copy-start(f32[64,512]{1,0:T(8,128)} %constant.23.clone.sin_ref) | copy-start | bytes 393220
  1.3 12.5 %copy-start.3 = (f32[64,512]{1,0:T(8,128)S(1)}, f32[64,512]{1,0:T(8,128)}, u32[]{:S(2)}) copy-start(f32[64,512]{1,0:T(8,128)} %constant.22.clone.cos_ref) | copy-start | bytes 393220
  1.3 12.5 %copy-start.4 = (f32[64,512]{1,0:T(8,128)S(1)}, f32[64,512]{1,0:T(8,128)}, u32[]{:S(2)}) copy-start(f32[64,512]{1,0:T(8,128)} %constant.21.clone.second_ref) | copy-start | bytes 393220
  1.3 12.5 %copy-start.5 = (f32[64,512]{1,0:T(8,128)S(1)}, f32[64,512]{1,0:T(8,128)}, u32[]{:S(2)}) copy-start(f32[64,512]{1,0:T(8,128)} %constant.20.clone.first_ref) | copy-start | bytes 393220
  6.2 31.3 %copy-start.10 = (bf16[64,64]{1,0:T(8,128)(2,1)S(1)}, bf16[64,64]{1,0:T(8,128)(2,1)}, u32[]{:S(2)}) copy-start(bf16[64,64]{1,0:T(8,128)(2,1)} %constant.37.y_ref) | copy-start | bytes 24580
  6.2 31.3 %copy-start.11 = (bf16[64,128]{1,0:T(8,128)(2,1)S(1)}, bf16[64,128]{1,0:T(8,128)(2,1)}, u32[]{:S(2)}) copy-start(bf16[64,128]{1,0:T(8,128)(2,1)} %constant.32.x_ref) | copy-start | bytes 49156
  6.3 49.6 %copy-start = (bf16[128,128]{1,0:T(8,128)(2,1)S(1)}, bf16[128,128]{1,0:T(8,128)(2,1)}, u32[]{:S(2)}) copy-start(bf16[128,128]{1,0:T(8,128)(2,1)} %constant.49.inverse_ref) | copy-start | bytes 98308
  6.3 49.6 %copy-start.1 = (bf16[128,64]{1,0:T(8,128)(2,1)S(1)}, bf16[128,64]{1,0:T(8,128)(2,1)}, u32[]{:S(2)}) copy-start(bf16[128,64]{1,0:T(8,128)(2,1)} %constant.43.forward_ref) | copy-start | bytes 49156
  6.3 31.2 %all-to-all-start = ((bf16[16,264,128]{2,1,0:T(8,128)(2,1)}), bf16[16,264,128]{2,1,0:T(8,128)(2,1)S(1)}, u32[]{:S(2)}, u32[]{:S(2)}) async-start(bf16[16,264,128]{2,1,0:T(8,128)(2,1)} %encode.1), calls=%async_computation | async-start | bytes 2162688 | tf_op jit(solution)/shard_map/all_to_all | solution.py:804
  60.1 13.5 %all-to-all-start.2 = ((bf16[16,32,256]{2,1,0:T(8,128)(2,1)}), bf16[16,32,256]{2,1,0:T(8,128)(2,1)S(1)}, u32[]{:S(2)}, u32[]{:S(2)}) async-start(bf16[16,32,256]{2,1,0:T(8,128)(2,1)} %bitcast.4), calls=%async_computation.2 | async-start | bytes 524288 | tf_op jit(solution)/shard_map/all_to_all | solution.py:804
  64.2 9.5 %copy-start.8 = (bf16[2,256,64]{1,2,0:T(8,128)(2,1)S(1)}, bf16[2,256,64]{1,2,0:T(8,128)(2,1)}, u32[]{:S(2)}) copy-start(bf16[2,256,64]{1,2,0:T(8,128)(2,1)} %param.20) | copy-start | bytes 196612
  64.2 9.5 %copy-start.9 = (bf16[2,64,256]{2,1,0:T(8,128)(2,1)S(1)}, bf16[2,64,256]{2,1,0:T(8,128)(2,1)}, u32[]{:S(2)}) copy-start(bf16[2,64,256]{2,1,0:T(8,128)(2,1)} %down_ref.3) | copy-start | bytes 196612
  107.3 13.5 %all-to-all-start.4 = ((bf16[16,32,256]{2,1,0:T(8,128)(2,1)}), bf16[16,32,256]{2,1,0:T(8,128)(2,1)S(1)}, u32[]{:S(2)}, u32[]{:S(2)}) async-start(bf16[16,32,256]{2,1,0:T(8,128)(2,1)} %bitcast.10), calls=%async_computation.4 | async-start | bytes 524288 | tf_op jit(solution)/shard_map/all_to_all | solution.py:804

commit v4 on v3

--- a/solution.py
+++ b/solution.py
@@ -20,7 +20,9 @@
 GELU_K = math.sqrt(2.0 / math.pi)
 SCALE = 1.66575
 PAD = 8
+PITCH = 2 * MX + PAD
 PARTS = 4
+LONG_PARTS = 2
 
 F32 = jnp.float32
 BF16 = jnp.bfloat16
@@ -128,7 +130,11 @@
         table = jnp.asarray(table.astype(np.float32))
         chosen.append(table[0] if table.shape[0] == 1 else table[which])
     forward, inverse = chosen
-    return jnp.concatenate(split(forward), axis=1), jnp.concatenate(split(inverse), axis=1)
+    high, low = split(inverse)
+    return (
+        jnp.concatenate(split(forward), axis=1),
+        jnp.concatenate([high, low, high], axis=1),
+    )
 
 
 def table_kernel(first_ref, second_ref, cos_ref, sin_ref, table_ref, flipped_ref):
@@ -174,20 +180,20 @@
 
 
 def copies_of(from_ref, to_ref, sem_ref):
-    step = from_ref.shape[0] // PARTS
+    step = from_ref.shape[0] // LONG_PARTS
     return [
         pltpu.make_async_copy(
             from_ref.at[pl.ds(part * step, step)],
             to_ref.at[pl.ds(part * step, step)],
             sem_ref.at[part],
         )
-        for part in range(PARTS)
+        for part in range(LONG_PARTS)
     ]
 
 
 def encode_kernel(
-    feature_hbm_ref, weight_hbm_ref, owner_ref, number_ref, out_ref, wide_ref, feature_ref,
-    weight_ref, sem_ref
+    feature_hbm_ref, weight_hbm_ref, owner_hbm_ref, number_hbm_ref, out_hbm_ref, wide_ref,
+    feature_ref, weight_ref, owner_ref, number_ref, out_ref, sem_ref, out_sem_ref
 ):
     devices = out_ref.shape[0]
     pairs, block = weight_ref.shape[0], weight_ref.shape[1]
@@ -196,9 +202,20 @@
     tiles = NZ // devices // 2
     rows = tiles * pairs * lines
     copies = copies_of(weight_hbm_ref, weight_ref, sem_ref)
-    first_copy = pltpu.make_async_copy(feature_hbm_ref, feature_ref, sem_ref.at[PARTS])
-    for copy in [first_copy] + copies:
+    small = [
+        pltpu.make_async_copy(from_ref, to_ref, sem_ref.at[LONG_PARTS + place])
+        for place, (from_ref, to_ref) in enumerate(
+            (
+                (owner_hbm_ref, owner_ref),
+                (number_hbm_ref, number_ref),
+                (feature_hbm_ref, feature_ref),
+            )
+        )
+    ]
+    for copy in small + copies:
         copy.start()
+    for copy in small[0:2]:
+        copy.wait()
     lane = lax.broadcasted_iota(jnp.int32, (devices, 128), 1)
     strip = NY // lines
     target = owner_ref[...] * (NX * strip // devices) + number_ref[...]
@@ -214,7 +231,7 @@
     spots = spots.astype(F32).astype(BF16)
     for device in range(devices):
         out_ref[device, rows : rows + 8, :] = spots
-    first_copy.wait()
+    small[2].wait()
 
     def one(point, carry):
         features = feature_ref[:, pl.ds(pl.multiple_of(point * block, block), block)]
@@ -239,11 +256,20 @@
     for part, copy in enumerate(copies):
         copy.wait()
         lax.fori_loop(
-            part * points // PARTS, (part + 1) * points // PARTS, one, 0, unroll=2
+            part * points // LONG_PARTS, (part + 1) * points // LONG_PARTS, one, 0, unroll=points // LONG_PARTS
         )
+    results = []
     for device in range(devices):
         base = device * (rows + PAD)
         out_ref[device, 0:rows, :] = wide_ref[base : base + rows, :].astype(BF16)
+        results.append(
+            pltpu.make_async_copy(
+                out_ref.at[device], out_hbm_ref.at[device], out_sem_ref.at[device]
+            )
+        )
+        results[-1].start()
+    for result in results:
+        result.wait()
 
 
 def encode(features, weights, owners, numbers, devices):
@@ -251,22 +277,28 @@
     rows = NZ // devices // 2 * pairs * (block // NZ)
     return pl.pallas_call(
         encode_kernel,
-        out_shape=jax.ShapeDtypeStruct((devices, rows + 8, 128), BF16),
-        in_specs=[any_spec()] * 2 + [vmem_spec()] * 2,
-        out_specs=vmem_spec(),
+        out_shape=pltpu.HBM((devices, rows + 8, 128), BF16),
+        in_specs=[any_spec()] * 4,
+        out_specs=any_spec(),
         scratch_shapes=[
             pltpu.VMEM((devices * (rows + PAD), 128), F32),
             pltpu.VMEM(features.shape, BF16),
             pltpu.VMEM(weights.shape, BF16),
-            pltpu.SemaphoreType.DMA((PARTS + 1,)),
+            pltpu.VMEM(owners.shape, jnp.int32),
+            pltpu.VMEM(numbers.shape, jnp.int32),
+            pltpu.VMEM((devices, rows + 8, 128), BF16),
+            pltpu.SemaphoreType.DMA((LONG_PARTS + 3,)),
+            pltpu.SemaphoreType.DMA((devices,)),
         ],
         compiler_params=limit(10),
         cost_estimate=cost(4 * pairs * block * block * 64, pairs * block * block * 2),
         name="encode",
-    )(in_hbm(features), in_hbm(weights), owners, numbers)
-
-
-def decode_kernel(got_ref, weight_hbm_ref, out_ref, wide_ref, weight_ref, sem_ref):
+    )(in_hbm(features), in_hbm(weights), in_hbm(owners), in_hbm(numbers))
+
+
+def decode_kernel(
+    got_ref, weight_hbm_ref, out_hbm_ref, wide_ref, weight_ref, out_ref, sem_ref, out_sem_ref
+):
     copies = copies_of(weight_hbm_ref, weight_ref, sem_ref)
     for copy in copies:
         copy.start()
@@ -304,11 +336,21 @@
         return carry
 
     points = pairs // NBR
+    results = []
     for part, copy in enumerate(copies):
         copy.wait()
         lax.fori_loop(
-            part * points // PARTS, (part + 1) * points // PARTS, one, 0, unroll=2
+            part * points // LONG_PARTS, (part + 1) * points // LONG_PARTS, one, 0, unroll=points // LONG_PARTS
         )
+        place = pl.ds(part * points // LONG_PARTS * block, points // LONG_PARTS * block)
+        results.append(
+            pltpu.make_async_copy(
+                out_ref.at[:, place], out_hbm_ref.at[:, place], out_sem_ref.at[part]
+            )
+        )
+        results[-1].start()
+    for result in results:
+        result.wait()
 
 
 def decode(got, weights, channels):
@@ -316,13 +358,15 @@
     pairs, block = weights.shape[0], weights.shape[1]
     return pl.pallas_call(
         decode_kernel,
-        out_shape=jax.ShapeDtypeStruct((channels, pairs // NBR * block), F32),
+        out_shape=pltpu.HBM((channels, pairs // NBR * block), F32),
         in_specs=[vmem_spec(), any_spec()],
-        out_specs=vmem_spec(),
+        out_specs=any_spec(),
         scratch_shapes=[
             pltpu.VMEM((devices * (rows + PAD), 128), F32),
             pltpu.VMEM(weights.shape, BF16),
-            pltpu.SemaphoreType.DMA((PARTS,)),
+            pltpu.VMEM((channels, pairs // NBR * block), F32),
+            pltpu.SemaphoreType.DMA((LONG_PARTS,)),
+            pltpu.SemaphoreType.DMA((LONG_PARTS,)),
         ],
         cost_estimate=cost(4 * pairs * block * block * 64, pairs * block * block * 2),
         compiler_params=limit(12),
@@ -359,7 +403,7 @@
 
 
 def pair_spectrum_kernel(
-    modes_here, got_ref, x_ref, y_ref, out_ref, phase_hbm_ref, phase_ref, sem_ref
+    modes_here, got_ref, x_ref, y_ref, out_ref, phase_ref
 ):
     devices = got_ref.shape[0]
     rows = got_ref.shape[1] - 8
@@ -367,8 +411,6 @@
     lanes = rows // tiles
     spots = [got_ref[source, rows : rows + 8, :] for source in range(devices)]
     fill_phases(modes_here, devices, spots, x_ref, y_ref, phase_ref)
-    copy = pltpu.make_async_copy(phase_ref, phase_hbm_ref, sem_ref)
-    copy.start()
     values = jnp.concatenate(
         [
             jnp.concatenate(
@@ -383,7 +425,6 @@
         axis=1,
     )
     out_ref[...] = dot(phase_ref[...], values).astype(BF16)
-    copy.wait()
 
 
 def pair_spectrum(got, tables, modes_here, lanes):
@@ -392,16 +433,43 @@
     columns = devices * 2 * MX
     return pl.pallas_call(
         functools.partial(pair_spectrum_kernel, modes_here),
-        out_shape=(
-            jax.ShapeDtypeStruct((columns, lanes), BF16),
-            pltpu.HBM((columns, count), BF16),
-        ),
+        out_shape=jax.ShapeDtypeStruct((columns, lanes), BF16),
         in_specs=[vmem_spec()] * 3,
-        out_specs=(vmem_spec(), any_spec()),
-        scratch_shapes=[pltpu.VMEM((columns, count), BF16), pltpu.SemaphoreType.DMA],
+        out_specs=vmem_spec(),
+        scratch_shapes=[pltpu.VMEM((columns, count), BF16)],
         compiler_params=limit(10),
         cost_estimate=cost(2 * columns * count * lanes, got.size * 2 + columns * count * 2),
         name="pair_spectrum",
+    )(got, *tables)
+
+
+def phase_kernel(modes_here, got_ref, x_ref, y_ref, out_hbm_ref, phase_ref, out_ref, sem_ref):
+    devices = got_ref.shape[0]
+    rows = got_ref.shape[1] - 8
+    spots = [got_ref[source, rows : rows + 8, :] for source in range(devices)]
+    fill_phases(modes_here, devices, spots, x_ref, y_ref, phase_ref)
+    out_ref[...] = phase_ref[...].T
+    copy = pltpu.make_async_copy(out_ref, out_hbm_ref, sem_ref)
+    copy.start()
+    copy.wait()
+
+
+def pair_phases(got, tables, modes_here, lanes):
+    devices, rows, _ = got.shape
+    shape = (devices * 2 * MX, devices * (rows - 8) // (lanes // 128))
+    return pl.pallas_call(
+        functools.partial(phase_kernel, modes_here),
+        out_shape=pltpu.HBM(shape[::-1], BF16),
+        in_specs=[vmem_spec()] * 3,
+        out_specs=any_spec(),
+        scratch_shapes=[
+            pltpu.VMEM(shape, BF16),
+            pltpu.VMEM(shape[::-1], BF16),
+            pltpu.SemaphoreType.DMA,
+        ],
+        compiler_params=limit((4 * shape[0] * shape[1] >> 20) + 6),
+        cost_estimate=cost(1e6, got.size * 2 + shape[0] * shape[1] * 2),
+        name="pair_phases",
     )(got, *tables)
 
 
@@ -431,7 +499,10 @@
     tiles = got_ref.shape[1] // 128
     group = 8
     for tile in range(tiles):
-        wide_ref[tile] = got_ref[:, tile * 128 : (tile + 1) * 128].astype(F32)
+        for device in range(devices):
+            wide_ref[tile, device * PITCH : device * PITCH + 2 * MX, :] = got_ref[
+                device * 2 * MX : (device + 1) * 2 * MX, tile * 128 : (tile + 1) * 128
+            ].astype(F32)
     lane = lax.broadcasted_iota(jnp.int32, (2 * modes_here, 128), 1)
     row = lax.broadcasted_iota(jnp.int32, (2 * group, 128), 0)
     lane_small = lax.broadcasted_iota(jnp.int32, (2 * group, 128), 1)
@@ -444,7 +515,7 @@
             [
                 jnp.concatenate(
                     [
-                        wide_ref[tile, pl.ds(row_of(wave, part), devices, stride=2 * MX), :]
+                        wide_ref[tile, pl.ds(row_of(wave, part), devices, stride=PITCH), :]
                         for part in range(2)
                     ],
                     axis=0,
@@ -487,21 +558,21 @@
     for wave in range(MX):
         stacked = jnp.concatenate([mixed[wave], pltpu.roll(mixed[wave], 64, 1)], axis=0)
         upper, lower = split(stacked)
-        count = upper.shape[0]
-        planes = dot(inverse, jnp.concatenate([upper, upper], axis=0)) + dot(
-            inverse[:, 0:count], lower
-        )
+        planes = dot(inverse, jnp.concatenate([upper, upper, lower], axis=0))
         size = 2 * devices
         for tile in range(tiles):
             even = planes[2 * tile * size : (2 * tile + 1) * size, :]
             odd = planes[(2 * tile + 1) * size : (2 * tile + 2) * size, :]
             both = jnp.where(lane_back < 64, even, pltpu.roll(odd, 64, 1))
             for part in range(2):
-                back_ref[tile, pl.ds(row_of(wave, part), devices, stride=2 * MX), :] = both[
+                back_ref[tile, pl.ds(row_of(wave, part), devices, stride=PITCH), :] = both[
                     part * devices : (part + 1) * devices
                 ]
     for tile in range(tiles):
-        out_ref[:, tile * 128 : (tile + 1) * 128] = back_ref[tile].astype(BF16)
+        for device in range(devices):
+            out_ref[
+                device * 2 * MX : (device + 1) * 2 * MX, tile * 128 : (tile + 1) * 128
+            ] = back_ref[tile, device * PITCH : device * PITCH + 2 * MX, :].astype(BF16)
 
 
 def mix(got, forward, inverse, weights, number, devices):
@@ -511,7 +582,7 @@
         out_shape=jax.ShapeDtypeStruct((rows, lanes), BF16),
         in_specs=[vmem_spec()] * 3 + [any_spec()],
         out_specs=vmem_spec(),
-        scratch_shapes=[pltpu.VMEM((lanes // 128, rows, 128), F32)] * 2
+        scratch_shapes=[pltpu.VMEM((lanes // 128, devices * PITCH, 128), F32)] * 2
         + [pltpu.VMEM(weights.shape[1:], BF16), pltpu.SemaphoreType.DMA((PARTS,))],
         compiler_params=limit(12),
         cost_estimate=cost(6e8, weights.size + rows * lanes * 4),
@@ -745,9 +816,7 @@
     def _():
         spread_weights(up_ref, down_ref, up_wide_ref, down_wide_ref)
 
-    spectral = lax.dot_general(
-        phase_ref[...], modes_ref[...], (((0,), (0,)), ((), ())), preferred_element_type=F32
-    )
+    spectral = dot(phase_ref[...], modes_ref[...])
     size = tiles * lines
     pairs = rows // lines
     summed = [
@@ -774,7 +843,7 @@
 
 
 def last_layer(phases, modes, grid, up, down, number, devices, lines):
-    columns, count = phases.shape
+    count, columns = phases.shape
     lanes = modes.shape[1]
     tiles = lanes // 128
     group = 8
@@ -784,7 +853,7 @@
         out_shape=jax.ShapeDtypeStruct((devices, rows * tiles, 128), BF16),
         grid=(devices // group,),
         in_specs=[
-            pl.BlockSpec((columns, group * rows), lambda i: (0, i)),
+            pl.BlockSpec((group * rows, columns), lambda i: (i, 0)),
             pl.BlockSpec((columns, lanes), lambda i: (0, 0)),
             pl.BlockSpec((group * rows * tiles, 128), lambda i: (i, 0)),
         ]
@@ -827,7 +896,8 @@
     here = got[:, -8:-6, 0:pairs].astype(jnp.int32)
     rows = ((here[:, 0, :] * NY + here[:, 1, :]) * tiles).reshape(devices * pairs)
 
-    spectrum, phases = pair_spectrum(got, lookups, modes_here, lanes)
+    spectrum = pair_spectrum(got, lookups, modes_here, lanes)
+    phases = pair_phases(got, lookups, modes_here, lanes)
     grid = scatter(rows, got, tiles)
     modes = exchange(spectrum.reshape(devices, 2 * MX, lanes)).reshape(columns, lanes)
     modes = mix(modes, forward, inverse, spec_weight, 0, devices)

time: 160 us -> 156 us (0.975)
  waiting for transfers between devices: 25.9 us -> 23.1 us
    all_to_all x3, waiting for transfers between devices: 25.9 us -> 23.1 us  [exchange(): lax.all_to_all(values, 'pen', split_axis=0, concat_axis=0, tiled=True)]
    pallas_call x2 -> x3, Pallas kernels: 9.41 us -> 10.8 us  [the longest x1 4.34 us: encode(): pl.pallas_call(encode_kernel, out_shape=pltpu.HBM((devices, rows + 8, 128...]
  transfers between devices with their start and end apart: 3 -> 3, of which waited for: 3 -> 3; matrix products, arithmetic and copies ran while one was open for 0% -> 0% of each run, Pallas kernels for 11% -> 13%
where the time goes in v4:
time: 156 us
  Pallas kernels  58.8 us (38%)
  blocking collectives  57.9 us (37%)
  waiting for transfers between devices  23.1 us (15%)
  starting transfers between devices  15.3 us (10%)
    all_to_all x3, blocking collectives, exchange(): lax.all_to_all(values, 'pen', split_axis=0, concat_axis=0, tiled=True)  57.9 us
    all_to_all x3, waiting for transfers between devices, exchange(): lax.all_to_all(values, 'pen', split_axis=0, concat_axis=0, tiled=True)  23.1 us
    pallas_call x1, Pallas kernels, layer(): pl.pallas_call(layer_kernel, out_shape=(pltpu.HBM((2, cells * tiles, 128)...  16.8 us
    all_to_all x3, starting transfers between devices, exchange(): lax.all_to_all(values, 'pen', split_axis=0, concat_axis=0, tiled=True)  15.3 us
    pallas_call x2, Pallas kernels, mix(): pl.pallas_call(functools.partial(mix_kernel, devices, number), out_shape=...  7.7 us
    pallas_call x1, Pallas kernels, scatter(): pl.pallas_call(scatter_kernel, out_shape=pltpu.HBM((NX * NY * tiles, 128)...  6.78 us
    pallas_call x1, Pallas kernels, last_layer(): pl.pallas_call(functools.partial(last_kernel, lines), out_shape=jax.Shape...  5.26 us
    pallas_call x1, Pallas kernels, grid_tables(): pl.pallas_call(table_kernel, out_shape=(pltpu.HBM((NX // 2 * NY, columns)...  5.24 us
  transfers between devices with their start and end apart: 3, of which 3 were waited for; matrix products, arithmetic and copies ran while one was open for 0% of the time, Pallas kernels for 13%

profile of v4, /device:TPU:1, one launch (start us, length us, event | category | flops | bytes accessed | tf_op | source)
XLA Modules:
  0.0 155.6 jit_solution(13796143257905973560)
XLA Ops:
  0.0 0.0 copy-start.2
  0.0 0.0 copy-start.3
  0.0 0.0 copy-start.4
  0.0 0.0 copy-start.5
  0.0 4.3 %encode.1 = bf16[16,264,128]{2,1,0:T(8,128)(2,1)} custom-call(bf16[64,2048]{1,0:T(8,128)(2,1)} %feature_hbm_ref.1, bf16[64,128,128]{2,1,0:T(8,128)(2,1)} %weight_hbm_ref.7, s32[1,64]{1,0:T(1,128)} %bitcast.23, s32[1,64]{1,0:T(1,128)} %bitcast.24), custom_call_target="tpu_custom_call" | custom-call | flops 268435456 | bytes 2097152 | tf_op jit(solution)/shard_map/encode/pallas_call | solution.py:278
  4.4 0.0 copy-start.6
  4.4 0.0 copy-start.7
  4.4 0.0 copy-start
  4.4 0.0 copy-start.1
  4.4 7.5 %all-to-all-start = ((bf16[16,264,128]{2,1,0:T(8,128)(2,1)}), bf16[16,264,128]{2,1,0:T(8,128)(2,1)S(1)}, u32[]{:S(2)}, u32[]{:S(2)}) async-start(bf16[16,264,128]{2,1,0:T(8,128)(2,1)} %encode.1), calls=%async_computation | async-start | bytes 2162688 | tf_op jit(solution)/shard_map/all_to_all | solution.py:873
  11.9 0.0 copy-done.2
  11.9 0.0 copy-done.3
  11.9 0.0 copy-done.4
  11.9 0.0 copy-done.5
  11.9 5.2 %tables.1 = (bf16[4096,512]{1,0:T(8,128)(2,1)}, bf16[512,4096]{1,0:T(8,128)(2,1)}) custom-call(f32[64,512]{1,0:T(8,128)S(1)} %copy-done.2, f32[64,512]{1,0:T(8,128)S(1)} %copy-done.3, f32[64,512]{1,0:T(8,128)S(1)} %copy-done.4, f32[64,512]{1,0:T(8,128)S(1)} %copy-done.5), custom_call_target="tpu_custom_call" | custom-call | flops 8388608 | bytes 8388608 | tf_op jit(solution)/shard_map/tables/pallas_call | solution.py:159
  17.2 18.5 %all-to-all-done.got_ref = bf16[16,264,128]{2,1,0:T(8,128)(2,1)S(1)} async-done(((bf16[16,264,128]{2,1,0:T(8,128)(2,1)}), bf16[16,264,128]{2,1,0:T(8,128)(2,1)S(1)}, u32[]{:S(2)}, u32[]{:S(2)}) %all-to-all-start) | async-done | bytes 1081376 | tf_op jit(solution)/shard_map/all_to_all | solution.py:873
  35.7 0.0 copy-done.6
  35.7 0.0 copy-done.7
  35.7 1.3 pair_spectrum.1
  37.0 15.9 %all_to_all.30 = bf16[16,32,256]{2,1,0:T(8,128)(2,1)S(1)} all-to-all(bf16[16,32,256]{2,1,0:T(8,128)(2,1)S(1)} %bitcast.18), channel_id=1, replica_groups=mesh['groups'=2,'pen'=16] {'pen'}, dimensions={0} | all-to-all | bytes 524288 | tf_op jit(solution)/shard_map/all_to_all | solution.py:873
  52.9 0.0 copy-done
  52.9 0.0 copy-done.1
  52.9 4.0 %mix.2 = bf16[512,256]{1,0:T(8,128)(2,1)} custom-call(bf16[512,256]{1,0:T(8,128)(2,1)S(1)} %bitcast.14, bf16[128,64]{1,0:T(8,128)(2,1)S(1)} %copy-done.1, bf16[128,192]{1,0:T(8,128)(2,1)S(1)} %copy-done, bf16[2,16,16,64,128]{4,3,2,1,0:T(8,128)(2,1)} %weight_hbm_ref.6), custom_call_target="tpu_custom_call" | custom-call | flops 600000000 | bytes 4718592 | tf_op jit(solution)/shard_map/mix/pallas_call | solution.py:580
  56.9 3.9 %all-to-all-start.2 = ((bf16[16,32,256]{2,1,0:T(8,128)(2,1)}), bf16[16,32,256]{2,1,0:T(8,128)(2,1)S(1)}, u32[]{:S(2)}, u32[]{:S(2)}) async-start(bf16[16,32,256]{2,1,0:T(8,128)(2,1)} %bitcast.4), calls=%async_computation.2 | async-start | bytes 524288 | tf_op jit(solution)/shard_map/all_to_all | solution.py:873
  60.9 0.1 mul.22.spot_ref
  61.0 0.0 copy-start.8
  61.0 0.0 copy-start.9
  61.0 6.8 %scatter.1 = f32[16384,128]{1,0:T(8,128)} custom-call(s32[1024]{0:T(1024)S(1)} %mul.22.spot_ref, bf16[16,264,128]{2,1,0:T(8,128)(2,1)S(1)} %all-to-all-done.got_ref), custom_call_target="tpu_custom_call" | custom-call | flops 1000000 | bytes 33554432 | tf_op jit(solution)/shard_map/scatter/pallas_call | solution.py:665
  67.7 2.7 %all-to-all-done.2 = bf16[16,32,256]{2,1,0:T(8,128)(2,1)S(1)} async-done(((bf16[16,32,256]{2,1,0:T(8,128)(2,1)}), bf16[16,32,256]{2,1,0:T(8,128)(2,1)S(1)}, u32[]{:S(2)}, u32[]{:S(2)}) %all-to-all-start.2) | async-done | bytes 262176 | tf_op jit(solution)/shard_map/all_to_all | solution.py:873
  70.4 0.0 copy-done.8
  70.4 0.0 copy-done.9
  70.4 16.8 %layer.1 = (f32[2,8192,128]{2,1,0:T(8,128)}, bf16[512,256]{1,0:T(8,128)(2,1)S(1)}) custom-call(bf16[4096,512]{1,0:T(8,128)(2,1)} %get-tuple-element.15.table_ref, bf16[512,4096]{1,0:T(8,128)(2,1)} %get-tuple-element.16.flipped_ref, bf16[512,256]{1,0:T(8,128)(2,1)S(1)} %bitcast.15, f32[2,8192,128]{2,1,0:T(8,128)} %bitcast.22, ...), custom_call_target="tpu_custom_call" | custom-call | flops 6442450944 | bytes 16777216 | tf_op jit(solution)/shard_map/layer/pallas_call | solution.py:777
  87.2 12.8 %all_to_all.31 = bf16[16,32,256]{2,1,0:T(8,128)(2,1)S(1)} all-to-all(bf16[16,32,256]{2,1,0:T(8,128)(2,1)S(1)} %bitcast.17), channel_id=1, replica_groups=mesh['groups'=2,'pen'=16] {'pen'}, dimensions={0} | all-to-all | bytes 524288 | tf_op jit(solution)/shard_map/all_to_all | solution.py:873
  100.0 3.7 %mix.3 = bf16[512,256]{1,0:T(8,128)(2,1)} custom-call(bf16[512,256]{1,0:T(8,128)(2,1)S(1)} %bitcast.13, bf16[128,64]{1,0:T(8,128)(2,1)S(1)} %copy-done.1, bf16[128,192]{1,0:T(8,128)(2,1)S(1)} %copy-done, bf16[2,16,16,64,128]{4,3,2,1,0:T(8,128)(2,1)} %weight_hbm_ref.6), custom_call_target="tpu_custom_call" | custom-call | flops 600000000 | bytes 4718592 | tf_op jit(solution)/shard_map/mix/pallas_call | solution.py:580
  103.8 3.9 %all-to-all-start.4 = ((bf16[16,32,256]{2,1,0:T(8,128)(2,1)}), bf16[16,32,256]{2,1,0:T(8,128)(2,1)S(1)}, u32[]{:S(2)}, u32[]{:S(2)}) async-start(bf16[16,32,256]{2,1,0:T(8,128)(2,1)} %bitcast.10), calls=%async_computation.4 | async-start | bytes 524288 | tf_op jit(solution)/shard_map/all_to_all | solution.py:873
  107.7 2.7 %pair_phases.1.phase_ref = bf16[2048,512]{1,0:T(8,128)(2,1)} custom-call(bf16[16,264,128]{2,1,0:T(8,128)(2,1)S(1)} %all-to-all-done.got_ref, bf16[64,128]{1,0:T(8,128)(2,1)S(1)} %copy-done.6, bf16[64,64]{1,0:T(8,128)(2,1)S(1)} %copy-done.7), custom_call_target="tpu_custom_call" | custom-call | flops 1000000 | bytes 3178496 | tf_op jit(solution)/shard_map/pair_phases/pallas_call | solution.py:460
  110.4 4.9 %gather.1.grid_ref = f32[4096,128]{1,0:T(8,128)S(1)} custom-call(s32[1024]{0:T(1024)S(1)} %mul.22.spot_ref, f32[16384,128]{1,0:T(8,128)} %bitcast.21), custom_call_target="tpu_custom_call" | custom-call | flops 1000000 | bytes 16777216 | tf_op jit(solution)/shard_map/gather/pallas_call | solution.py:697
  115.3 2.0 %all-to-all-done.4 = bf16[16,32,256]{2,1,0:T(8,128)(2,1)S(1)} async-done(((bf16[16,32,256]{2,1,0:T(8,128)(2,1)}), bf16[16,32,256]{2,1,0:T(8,128)(2,1)S(1)}, u32[]{:S(2)}, u32[]{:S(2)}) %all-to-all-start.4) | async-done | bytes 262176 | tf_op jit(solution)/shard_map/all_to_all | solution.py:873
  117.3 5.3 %last_layer.1 = bf16[16,256,128]{2,1,0:T(8,128)(2,1)S(1)} custom-call(bf16[2048,512]{1,0:T(8,128)(2,1)} %pair_phases.1.phase_ref, bf16[512,256]{1,0:T(8,128)(2,1)S(1)} %bitcast.16, f32[4096,128]{1,0:T(8,128)S(1)} %gather.1.grid_ref, bf16[2,64,256]{2,1,0:T(8,128)(2,1)S(1)} %bitcast.20, bf16[2,64,256]{2,1,0:T(8,128)(2,1)S(1)} %copy-done.9), custom_call_target="tpu_custom_call" | custom-call | flops 2684354560 | bytes 5242880 | tf_op jit(solution)/shard_map/last_layer/pallas_call | solution.py:851
  122.5 29.2 %all_to_all.32.got_ref = bf16[16,256,128]{2,1,0:T(8,128)(2,1)S(1)} all-to-all(bf16[16,256,128]{2,1,0:T(8,128)(2,1)S(1)} %last_layer.1), channel_id=1, replica_groups=mesh['groups'=2,'pen'=16] {'pen'}, dimensions={0} | all-to-all | bytes 2097152 | tf_op jit(solution)/shard_map/all_to_all | solution.py:873
  151.7 3.7 %decode.1 = f32[64,2048]{1,0:T(8,128)} custom-call(bf16[16,256,128]{2,1,0:T(8,128)(2,1)S(1)} %all_to_all.32.got_ref, bf16[64,128,128]{2,1,0:T(8,128)(2,1)} %weight_hbm_ref.7), custom_call_target="tpu_custom_call" | custom-call | flops 268435456 | bytes 2097152 | tf_op jit(solution)/shard_map/decode/pallas_call | solution.py:359
  (2 shorter events, 0.0 us)
Async XLA Ops:
  0.0 11.9 %copy-start.2 = (f32[64,512]{1,0:T(8,128)S(1)}, f32[64,512]{1,0:T(8,128)}, u32[]{:S(2)}) copy-start(f32[64,512]{1,0:T(8,128)} %constant.20.clone.first_ref) | copy-start | bytes 393220
  0.0 11.9 %copy-start.3 = (f32[64,512]{1,0:T(8,128)S(1)}, f32[64,512]{1,0:T(8,128)}, u32[]{:S(2)}) copy-start(f32[64,512]{1,0:T(8,128)} %constant.21.clone.second_ref) | copy-start | bytes 393220
  0.0 11.9 %copy-start.4 = (f32[64,512]{1,0:T(8,128)S(1)}, f32[64,512]{1,0:T(8,128)}, u32[]{:S(2)}) copy-start(f32[64,512]{1,0:T(8,128)} %constant.22.clone.cos_ref) | copy-start | bytes 393220
  0.0 11.9 %copy-start.5 = (f32[64,512]{1,0:T(8,128)S(1)}, f32[64,512]{1,0:T(8,128)}, u32[]{:S(2)}) copy-start(f32[64,512]{1,0:T(8,128)} %constant.23.clone.sin_ref) | copy-start | bytes 393220
  4.4 31.3 %copy-start.6 = (bf16[64,128]{1,0:T(8,128)(2,1)S(1)}, bf16[64,128]{1,0:T(8,128)(2,1)}, u32[]{:S(2)}) copy-start(bf16[64,128]{1,0:T(8,128)(2,1)} %constant.32.x_ref) | copy-start | bytes 49156
  4.4 31.3 %copy-start.7 = (bf16[64,64]{1,0:T(8,128)(2,1)S(1)}, bf16[64,64]{1,0:T(8,128)(2,1)}, u32[]{:S(2)}) copy-start(bf16[64,64]{1,0:T(8,128)(2,1)} %constant.37.y_ref) | copy-start | bytes 24580
  4.4 48.5 %copy-start = (bf16[128,192]{1,0:T(8,128)(2,1)S(1)}, bf16[128,192]{1,0:T(8,128)(2,1)}, u32[]{:S(2)}) copy-start(bf16[128,192]{1,0:T(8,128)(2,1)} %constant.49.inverse_ref) | copy-start | bytes 147460
  4.4 48.5 %copy-start.1 = (bf16[128,64]{1,0:T(8,128)(2,1)S(1)}, bf16[128,64]{1,0:T(8,128)(2,1)}, u32[]{:S(2)}) copy-start(bf16[128,64]{1,0:T(8,128)(2,1)} %constant.43.forward_ref) | copy-start | bytes 49156
  4.4 31.2 %all-to-all-start = ((bf16[16,264,128]{2,1,0:T(8,128)(2,1)}), bf16[16,264,128]{2,1,0:T(8,128)(2,1)S(1)}, u32[]{:S(2)}, u32[]{:S(2)}) async-start(bf16[16,264,128]{2,1,0:T(8,128)(2,1)} %encode.1), calls=%async_computation | async-start | bytes 2162688 | tf_op jit(solution)/shard_map/all_to_all | solution.py:873
  56.9 13.5 %all-to-all-start.2 = ((bf16[16,32,256]{2,1,0:T(8,128)(2,1)}), bf16[16,32,256]{2,1,0:T(8,128)(2,1)S(1)}, u32[]{:S(2)}, u32[]{:S(2)}) async-start(bf16[16,32,256]{2,1,0:T(8,128)(2,1)} %bitcast.4), calls=%async_computation.2 | async-start | bytes 524288 | tf_op jit(solution)/shard_map/all_to_all | solution.py:873
  61.0 9.5 %copy-start.8 = (bf16[2,256,64]{1,2,0:T(8,128)(2,1)S(1)}, bf16[2,256,64]{1,2,0:T(8,128)(2,1)}, u32[]{:S(2)}) copy-start(bf16[2,256,64]{1,2,0:T(8,128)(2,1)} %param.20) | copy-start | bytes 196612
  61.0 9.5 %copy-start.9 = (bf16[2,64,256]{2,1,0:T(8,128)(2,1)S(1)}, bf16[2,64,256]{2,1,0:T(8,128)(2,1)}, u32[]{:S(2)}) copy-start(bf16[2,64,256]{2,1,0:T(8,128)(2,1)} %down_ref.3) | copy-start | bytes 196612
  103.8 13.5 %all-to-all-start.4 = ((bf16[16,32,256]{2,1,0:T(8,128)(2,1)}), bf16[16,32,256]{2,1,0:T(8,128)(2,1)S(1)}, u32[]{:S(2)}, u32[]{:S(2)}) async-start(bf16[16,32,256]{2,1,0:T(8,128)(2,1)} %bitcast.10), calls=%async_computation.4 | async-start | bytes 524288 | tf_op jit(solution)/shard_map/all_to_all | solution.py:873

commit v5 on v4

--- a/solution.py
+++ b/solution.py
@@ -9,13 +9,13 @@
 from jax.experimental.pallas import tpu as pltpu
 from jax.sharding import PartitionSpec as P
 
+
 NX = 128
 NY = 64
 NZ = 64
 MX = 16
 MY = 16
 MZ = 16
-LAYERS = 2
 NBR = 4
 GELU_K = math.sqrt(2.0 / math.pi)
 SCALE = 1.66575
@@ -312,10 +312,9 @@
         wide_ref[base : base + rows, :] = got_ref[device].astype(F32)
 
     def one(point, carry):
-        total = None
+        pieces = []
         for near in range(NBR):
             pair = point * NBR + near
-            pieces = []
             for line in range(lines):
                 for tile in range(tiles):
                     values = wide_ref[
@@ -323,16 +322,12 @@
                     ]
                     pieces.append(jnp.where(lane < 64, values, 0.0))
                     pieces.append(jnp.where(lane < 64, 0.0, values))
-            part = lax.dot_general(
-                jnp.concatenate(pieces, axis=0).astype(BF16),
-                weight_ref[pair],
-                (((0,), (1,)), ((), ())),
-                preferred_element_type=F32,
-            )
-            total = part if total is None else total + part
-        out_ref[:, pl.ds(pl.multiple_of(point * block, block), block)] = (
-            total[0:64, :] + total[64:128, :]
+        total = dot(
+            jnp.concatenate([weight_ref[point * NBR + near] for near in range(NBR)], axis=1),
+            jnp.concatenate(pieces, axis=0).astype(BF16),
         )
+        total = (total + pltpu.roll(total, 64, 1)).T
+        out_ref[:, pl.ds(pl.multiple_of(point * block, block), block)] = total[0:64, :]
         return carry
 
     points = pairs // NBR
@@ -495,7 +490,6 @@
     ]
     for copy in copies:
         copy.start()
-    local = got_ref.shape[1] // channels
     tiles = got_ref.shape[1] // 128
     group = 8
     for tile in range(tiles):
@@ -873,7 +867,7 @@
     return lax.all_to_all(values, "pen", split_axis=0, concat_axis=0, tiled=True)
 
 
-def per_device(point_feat, pair_kernel, pair_owner, pair_block, spec_weight, mlp_up, mlp_down):
+def forward_pass(point_feat, pair_kernel, pair_owner, pair_block, spec_weight, mlp_up, mlp_down):
     devices = lax.axis_size("pen")
     pairs, block = pair_kernel.shape[0], pair_kernel.shape[1]
     channels = point_feat.shape[0]
@@ -923,5 +917,5 @@
     )
     out_specs = P(None, ("groups", "pen"))
     return jax.shard_map(
-        per_device, mesh=mesh, in_specs=in_specs, out_specs=out_specs, check_vma=False
+        forward_pass, mesh=mesh, in_specs=in_specs, out_specs=out_specs, check_vma=False
     )

time: 156 us -> 156 us (level)
  no operation moved by 1% of the time
where the time goes in v5:
time: 156 us; the launch traced here: 155 us
  Pallas kernels  58.4 us (37%)
  blocking collectives  57.9 us (37%)
  waiting for transfers between devices  23.1 us (15%)
  starting transfers between devices  15.3 us (10%)
    all_to_all x3, blocking collectives, exchange(): lax.all_to_all(values, 'pen', split_axis=0, concat_axis=0, tiled=True)  57.9 us
    all_to_all x3, waiting for transfers between devices, exchange(): lax.all_to_all(values, 'pen', split_axis=0, concat_axis=0, tiled=True)  23.1 us
    pallas_call x1, Pallas kernels, layer(): pl.pallas_call(layer_kernel, out_shape=(pltpu.HBM((2, cells * tiles, 128)...  16.8 us
    all_to_all x3, starting transfers between devices, exchange(): lax.all_to_all(values, 'pen', split_axis=0, concat_axis=0, tiled=True)  15.3 us
    pallas_call x2, Pallas kernels, mix(): pl.pallas_call(functools.partial(mix_kernel, devices, number), out_shape=...  7.7 us
    pallas_call x1, Pallas kernels, scatter(): pl.pallas_call(scatter_kernel, out_shape=pltpu.HBM((NX * NY * tiles, 128)...  6.78 us
    pallas_call x1, Pallas kernels, last_layer(): pl.pallas_call(functools.partial(last_kernel, lines), out_shape=jax.Shape...  5.26 us
    pallas_call x1, Pallas kernels, grid_tables(): pl.pallas_call(table_kernel, out_shape=(pltpu.HBM((NX // 2 * NY, columns)...  5.24 us
  transfers between devices with their start and end apart: 3, of which 3 were waited for; matrix products, arithmetic and copies ran while one was open for 0% of the time, Pallas kernels for 13%

profile of v5, /device:TPU:1, one launch (start us, length us, event | category | flops | bytes accessed | tf_op | source)
XLA Modules:
  0.0 155.2 jit_solution(251448892355598290)
XLA Ops:
  0.0 0.0 copy-start.2
  0.0 0.0 copy-start.3
  0.0 0.0 copy-start.4
  0.0 0.0 copy-start.5
  0.0 4.3 %encode.1 = bf16[16,264,128]{2,1,0:T(8,128)(2,1)} custom-call(bf16[64,2048]{1,0:T(8,128)(2,1)} %feature_hbm_ref.1, bf16[64,128,128]{2,1,0:T(8,128)(2,1)} %weight_hbm_ref.7, s32[1,64]{1,0:T(1,128)} %bitcast.23, s32[1,64]{1,0:T(1,128)} %bitcast.24), custom_call_target="tpu_custom_call" | custom-call | flops 268435456 | bytes 2097152 | tf_op jit(solution)/shard_map/encode/pallas_call | solution.py:278
  4.4 0.0 copy-start.6
  4.4 0.0 copy-start.7
  4.4 0.0 copy-start
  4.4 0.0 copy-start.1
  4.4 7.5 %all-to-all-start = ((bf16[16,264,128]{2,1,0:T(8,128)(2,1)}), bf16[16,264,128]{2,1,0:T(8,128)(2,1)S(1)}, u32[]{:S(2)}, u32[]{:S(2)}) async-start(bf16[16,264,128]{2,1,0:T(8,128)(2,1)} %encode.1), calls=%async_computation | async-start | bytes 2162688 | tf_op jit(solution)/shard_map/all_to_all | solution.py:867
  11.9 0.0 copy-done.2
  11.9 0.0 copy-done.3
  11.9 0.0 copy-done.4
  11.9 0.0 copy-done.5
  11.9 5.2 %tables.1 = (bf16[4096,512]{1,0:T(8,128)(2,1)}, bf16[512,4096]{1,0:T(8,128)(2,1)}) custom-call(f32[64,512]{1,0:T(8,128)S(1)} %copy-done.2, f32[64,512]{1,0:T(8,128)S(1)} %copy-done.3, f32[64,512]{1,0:T(8,128)S(1)} %copy-done.4, f32[64,512]{1,0:T(8,128)S(1)} %copy-done.5), custom_call_target="tpu_custom_call" | custom-call | flops 8388608 | bytes 8388608 | tf_op jit(solution)/shard_map/tables/pallas_call | solution.py:159
  17.2 18.5 %all-to-all-done.got_ref = bf16[16,264,128]{2,1,0:T(8,128)(2,1)S(1)} async-done(((bf16[16,264,128]{2,1,0:T(8,128)(2,1)}), bf16[16,264,128]{2,1,0:T(8,128)(2,1)S(1)}, u32[]{:S(2)}, u32[]{:S(2)}) %all-to-all-start) | async-done | bytes 1081376 | tf_op jit(solution)/shard_map/all_to_all | solution.py:867
  35.7 0.0 copy-done.6
  35.7 0.0 copy-done.7
  35.7 1.3 pair_spectrum.1
  37.0 15.9 %all_to_all.30 = bf16[16,32,256]{2,1,0:T(8,128)(2,1)S(1)} all-to-all(bf16[16,32,256]{2,1,0:T(8,128)(2,1)S(1)} %bitcast.18), channel_id=1, replica_groups=mesh['groups'=2,'pen'=16] {'pen'}, dimensions={0} | all-to-all | bytes 524288 | tf_op jit(solution)/shard_map/all_to_all | solution.py:867
  52.9 0.0 copy-done
  52.9 0.0 copy-done.1
  52.9 4.0 %mix.2 = bf16[512,256]{1,0:T(8,128)(2,1)} custom-call(bf16[512,256]{1,0:T(8,128)(2,1)S(1)} %bitcast.14, bf16[128,64]{1,0:T(8,128)(2,1)S(1)} %copy-done.1, bf16[128,192]{1,0:T(8,128)(2,1)S(1)} %copy-done, bf16[2,16,16,64,128]{4,3,2,1,0:T(8,128)(2,1)} %weight_hbm_ref.6), custom_call_target="tpu_custom_call" | custom-call | flops 600000000 | bytes 4718592 | tf_op jit(solution)/shard_map/mix/pallas_call | solution.py:574
  56.9 3.9 %all-to-all-start.2 = ((bf16[16,32,256]{2,1,0:T(8,128)(2,1)}), bf16[16,32,256]{2,1,0:T(8,128)(2,1)S(1)}, u32[]{:S(2)}, u32[]{:S(2)}) async-start(bf16[16,32,256]{2,1,0:T(8,128)(2,1)} %bitcast.4), calls=%async_computation.2 | async-start | bytes 524288 | tf_op jit(solution)/shard_map/all_to_all | solution.py:867
  60.9 0.1 mul.22.spot_ref
  61.0 0.0 copy-start.8
  61.0 0.0 copy-start.9
  61.0 6.8 %scatter.1 = f32[16384,128]{1,0:T(8,128)} custom-call(s32[1024]{0:T(1024)S(1)} %mul.22.spot_ref, bf16[16,264,128]{2,1,0:T(8,128)(2,1)S(1)} %all-to-all-done.got_ref), custom_call_target="tpu_custom_call" | custom-call | flops 1000000 | bytes 33554432 | tf_op jit(solution)/shard_map/scatter/pallas_call | solution.py:659
  67.7 2.7 %all-to-all-done.2 = bf16[16,32,256]{2,1,0:T(8,128)(2,1)S(1)} async-done(((bf16[16,32,256]{2,1,0:T(8,128)(2,1)}), bf16[16,32,256]{2,1,0:T(8,128)(2,1)S(1)}, u32[]{:S(2)}, u32[]{:S(2)}) %all-to-all-start.2) | async-done | bytes 262176 | tf_op jit(solution)/shard_map/all_to_all | solution.py:867
  70.4 0.0 copy-done.8
  70.4 0.0 copy-done.9
  70.4 16.8 %layer.1 = (f32[2,8192,128]{2,1,0:T(8,128)}, bf16[512,256]{1,0:T(8,128)(2,1)S(1)}) custom-call(bf16[4096,512]{1,0:T(8,128)(2,1)} %get-tuple-element.15.table_ref, bf16[512,4096]{1,0:T(8,128)(2,1)} %get-tuple-element.16.flipped_ref, bf16[512,256]{1,0:T(8,128)(2,1)S(1)} %bitcast.15, f32[2,8192,128]{2,1,0:T(8,128)} %bitcast.22, ...), custom_call_target="tpu_custom_call" | custom-call | flops 6442450944 | bytes 16777216 | tf_op jit(solution)/shard_map/layer/pallas_call | solution.py:771
  87.2 12.8 %all_to_all.31 = bf16[16,32,256]{2,1,0:T(8,128)(2,1)S(1)} all-to-all(bf16[16,32,256]{2,1,0:T(8,128)(2,1)S(1)} %bitcast.17), channel_id=1, replica_groups=mesh['groups'=2,'pen'=16] {'pen'}, dimensions={0} | all-to-all | bytes 524288 | tf_op jit(solution)/shard_map/all_to_all | solution.py:867
  100.0 3.7 %mix.3 = bf16[512,256]{1,0:T(8,128)(2,1)} custom-call(bf16[512,256]{1,0:T(8,128)(2,1)S(1)} %bitcast.13, bf16[128,64]{1,0:T(8,128)(2,1)S(1)} %copy-done.1, bf16[128,192]{1,0:T(8,128)(2,1)S(1)} %copy-done, bf16[2,16,16,64,128]{4,3,2,1,0:T(8,128)(2,1)} %weight_hbm_ref.6), custom_call_target="tpu_custom_call" | custom-call | flops 600000000 | bytes 4718592 | tf_op jit(solution)/shard_map/mix/pallas_call | solution.py:574
  103.8 3.9 %all-to-all-start.4 = ((bf16[16,32,256]{2,1,0:T(8,128)(2,1)}), bf16[16,32,256]{2,1,0:T(8,128)(2,1)S(1)}, u32[]{:S(2)}, u32[]{:S(2)}) async-start(bf16[16,32,256]{2,1,0:T(8,128)(2,1)} %bitcast.10), calls=%async_computation.4 | async-start | bytes 524288 | tf_op jit(solution)/shard_map/all_to_all | solution.py:867
  107.7 2.7 %pair_phases.1.phase_ref = bf16[2048,512]{1,0:T(8,128)(2,1)} custom-call(bf16[16,264,128]{2,1,0:T(8,128)(2,1)S(1)} %all-to-all-done.got_ref, bf16[64,128]{1,0:T(8,128)(2,1)S(1)} %copy-done.6, bf16[64,64]{1,0:T(8,128)(2,1)S(1)} %copy-done.7), custom_call_target="tpu_custom_call" | custom-call | flops 1000000 | bytes 3178496 | tf_op jit(solution)/shard_map/pair_phases/pallas_call | solution.py:455
  110.4 4.9 %gather.1.grid_ref = f32[4096,128]{1,0:T(8,128)S(1)} custom-call(s32[1024]{0:T(1024)S(1)} %mul.22.spot_ref, f32[16384,128]{1,0:T(8,128)} %bitcast.21), custom_call_target="tpu_custom_call" | custom-call | flops 1000000 | bytes 16777216 | tf_op jit(solution)/shard_map/gather/pallas_call | solution.py:691
  115.3 2.0 %all-to-all-done.4 = bf16[16,32,256]{2,1,0:T(8,128)(2,1)S(1)} async-done(((bf16[16,32,256]{2,1,0:T(8,128)(2,1)}), bf16[16,32,256]{2,1,0:T(8,128)(2,1)S(1)}, u32[]{:S(2)}, u32[]{:S(2)}) %all-to-all-start.4) | async-done | bytes 262176 | tf_op jit(solution)/shard_map/all_to_all | solution.py:867
  117.3 5.3 %last_layer.1 = bf16[16,256,128]{2,1,0:T(8,128)(2,1)S(1)} custom-call(bf16[2048,512]{1,0:T(8,128)(2,1)} %pair_phases.1.phase_ref, bf16[512,256]{1,0:T(8,128)(2,1)S(1)} %bitcast.16, f32[4096,128]{1,0:T(8,128)S(1)} %gather.1.grid_ref, bf16[2,64,256]{2,1,0:T(8,128)(2,1)S(1)} %bitcast.20, bf16[2,64,256]{2,1,0:T(8,128)(2,1)S(1)} %copy-done.9), custom_call_target="tpu_custom_call" | custom-call | flops 2684354560 | bytes 5242880 | tf_op jit(solution)/shard_map/last_layer/pallas_call | solution.py:845
  122.5 29.2 %all_to_all.32.got_ref = bf16[16,256,128]{2,1,0:T(8,128)(2,1)S(1)} all-to-all(bf16[16,256,128]{2,1,0:T(8,128)(2,1)S(1)} %last_layer.1), channel_id=1, replica_groups=mesh['groups'=2,'pen'=16] {'pen'}, dimensions={0} | all-to-all | bytes 2097152 | tf_op jit(solution)/shard_map/all_to_all | solution.py:867
  151.7 3.3 %decode.1 = f32[64,2048]{1,0:T(8,128)} custom-call(bf16[16,256,128]{2,1,0:T(8,128)(2,1)S(1)} %all_to_all.32.got_ref, bf16[64,128,128]{2,1,0:T(8,128)(2,1)} %weight_hbm_ref.7), custom_call_target="tpu_custom_call" | custom-call | flops 268435456 | bytes 2097152 | tf_op jit(solution)/shard_map/decode/pallas_call | solution.py:354
  (2 shorter events, 0.0 us)
Async XLA Ops:
  0.0 11.9 %copy-start.2 = (f32[64,512]{1,0:T(8,128)S(1)}, f32[64,512]{1,0:T(8,128)}, u32[]{:S(2)}) copy-start(f32[64,512]{1,0:T(8,128)} %constant.20.clone.first_ref) | copy-start | bytes 393220
  0.0 11.9 %copy-start.3 = (f32[64,512]{1,0:T(8,128)S(1)}, f32[64,512]{1,0:T(8,128)}, u32[]{:S(2)}) copy-start(f32[64,512]{1,0:T(8,128)} %constant.21.clone.second_ref) | copy-start | bytes 393220
  0.0 11.9 %copy-start.4 = (f32[64,512]{1,0:T(8,128)S(1)}, f32[64,512]{1,0:T(8,128)}, u32[]{:S(2)}) copy-start(f32[64,512]{1,0:T(8,128)} %constant.22.clone.cos_ref) | copy-start | bytes 393220
  0.0 11.9 %copy-start.5 = (f32[64,512]{1,0:T(8,128)S(1)}, f32[64,512]{1,0:T(8,128)}, u32[]{:S(2)}) copy-start(f32[64,512]{1,0:T(8,128)} %constant.23.clone.sin_ref) | copy-start | bytes 393220
  4.4 31.3 %copy-start.6 = (bf16[64,128]{1,0:T(8,128)(2,1)S(1)}, bf16[64,128]{1,0:T(8,128)(2,1)}, u32[]{:S(2)}) copy-start(bf16[64,128]{1,0:T(8,128)(2,1)} %constant.32.x_ref) | copy-start | bytes 49156
  4.4 31.3 %copy-start.7 = (bf16[64,64]{1,0:T(8,128)(2,1)S(1)}, bf16[64,64]{1,0:T(8,128)(2,1)}, u32[]{:S(2)}) copy-start(bf16[64,64]{1,0:T(8,128)(2,1)} %constant.37.y_ref) | copy-start | bytes 24580
  4.4 48.5 %copy-start = (bf16[128,192]{1,0:T(8,128)(2,1)S(1)}, bf16[128,192]{1,0:T(8,128)(2,1)}, u32[]{:S(2)}) copy-start(bf16[128,192]{1,0:T(8,128)(2,1)} %constant.49.inverse_ref) | copy-start | bytes 147460
  4.4 48.5 %copy-start.1 = (bf16[128,64]{1,0:T(8,128)(2,1)S(1)}, bf16[128,64]{1,0:T(8,128)(2,1)}, u32[]{:S(2)}) copy-start(bf16[128,64]{1,0:T(8,128)(2,1)} %constant.43.forward_ref) | copy-start | bytes 49156
  4.4 31.2 %all-to-all-start = ((bf16[16,264,128]{2,1,0:T(8,128)(2,1)}), bf16[16,264,128]{2,1,0:T(8,128)(2,1)S(1)}, u32[]{:S(2)}, u32[]{:S(2)}) async-start(bf16[16,264,128]{2,1,0:T(8,128)(2,1)} %encode.1), calls=%async_computation | async-start | bytes 2162688 | tf_op jit(solution)/shard_map/all_to_all | solution.py:867
  56.9 13.5 %all-to-all-start.2 = ((bf16[16,32,256]{2,1,0:T(8,128)(2,1)}), bf16[16,32,256]{2,1,0:T(8,128)(2,1)S(1)}, u32[]{:S(2)}, u32[]{:S(2)}) async-start(bf16[16,32,256]{2,1,0:T(8,128)(2,1)} %bitcast.4), calls=%async_computation.2 | async-start | bytes 524288 | tf_op jit(solution)/shard_map/all_to_all | solution.py:867
  61.0 9.5 %copy-start.8 = (bf16[2,256,64]{1,2,0:T(8,128)(2,1)S(1)}, bf16[2,256,64]{1,2,0:T(8,128)(2,1)}, u32[]{:S(2)}) copy-start(bf16[2,256,64]{1,2,0:T(8,128)(2,1)} %param.20) | copy-start | bytes 196612
  61.0 9.5 %copy-start.9 = (bf16[2,64,256]{2,1,0:T(8,128)(2,1)S(1)}, bf16[2,64,256]{2,1,0:T(8,128)(2,1)}, u32[]{:S(2)}) copy-start(bf16[2,64,256]{2,1,0:T(8,128)(2,1)} %down_ref.3) | copy-start | bytes 196612
  103.8 13.5 %all-to-all-start.4 = ((bf16[16,32,256]{2,1,0:T(8,128)(2,1)}), bf16[16,32,256]{2,1,0:T(8,128)(2,1)S(1)}, u32[]{:S(2)}, u32[]{:S(2)}) async-start(bf16[16,32,256]{2,1,0:T(8,128)(2,1)} %bitcast.10), calls=%async_computation.4 | async-start | bytes 524288 | tf_op jit(solution)/shard_map/all_to_all | solution.py:867

commit v6 on v5

--- a/solution.py
+++ b/solution.py
@@ -21,7 +21,7 @@
 SCALE = 1.66575
 PAD = 8
 PITCH = 2 * MX + PAD
-PARTS = 4
+PARTS = 2
 LONG_PARTS = 2
 
 F32 = jnp.float32
@@ -766,7 +766,7 @@
     cells, columns = table.shape
     lanes = modes.shape[1]
     tiles = lanes // 128
-    rows = 512
+    rows = 1024
     const = lambda i: (0, 0)
     return pl.pallas_call(
         layer_kernel,
@@ -793,7 +793,7 @@
             4 * cells * columns * lanes + 16 * cells * lanes * up.shape[2],
             cells * (columns * 4 + lanes * 8),
         ),
-        compiler_params=limit(22),
+        compiler_params=limit(42),
         name="layer",
     )(
         in_hbm(table), in_hbm(flipped), modes, in_hbm(grid.reshape(2, cells * tiles, 128)),

time: 156 us -> 155 us (level)
  no operation moved by 1% of the time
where the time goes in v6:
time: 155 us
  blocking collectives  57.9 us (37%)
  Pallas kernels  57.8 us (37%)
  waiting for transfers between devices  23.1 us (15%)
  starting transfers between devices  15.3 us (10%)
    all_to_all x3, blocking collectives, exchange(): lax.all_to_all(values, 'pen', split_axis=0, concat_axis=0, tiled=True)  57.9 us
    all_to_all x3, waiting for transfers between devices, exchange(): lax.all_to_all(values, 'pen', split_axis=0, concat_axis=0, tiled=True)  23.1 us
    pallas_call x1, Pallas kernels, layer(): pl.pallas_call(layer_kernel, out_shape=(pltpu.HBM((2, cells * tiles, 128)...  15.9 us
    all_to_all x3, starting transfers between devices, exchange(): lax.all_to_all(values, 'pen', split_axis=0, concat_axis=0, tiled=True)  15.3 us
    pallas_call x2, Pallas kernels, mix(): pl.pallas_call(functools.partial(mix_kernel, devices, number), out_shape=...  8.01 us
    pallas_call x1, Pallas kernels, scatter(): pl.pallas_call(scatter_kernel, out_shape=pltpu.HBM((NX * NY * tiles, 128)...  6.78 us
    pallas_call x1, Pallas kernels, last_layer(): pl.pallas_call(functools.partial(last_kernel, lines), out_shape=jax.Shape...  5.26 us
    pallas_call x1, Pallas kernels, grid_tables(): pl.pallas_call(table_kernel, out_shape=(pltpu.HBM((NX // 2 * NY, columns)...  5.24 us
  transfers between devices with their start and end apart: 3, of which 3 were waited for; matrix products, arithmetic and copies ran while one was open for 0% of the time, Pallas kernels for 13%

profile of v6, /device:TPU:1, one launch (start us, length us, event | category | flops | bytes accessed | tf_op | source)
XLA Modules:
  0.0 154.6 jit_solution(737189676363745983)
XLA Ops:
  0.0 0.0 copy-start.2
  0.0 0.0 copy-start.3
  0.0 0.0 copy-start.4
  0.0 0.0 copy-start.5
  0.0 4.3 %encode.1 = bf16[16,264,128]{2,1,0:T(8,128)(2,1)} custom-call(bf16[64,2048]{1,0:T(8,128)(2,1)} %feature_hbm_ref.1, bf16[64,128,128]{2,1,0:T(8,128)(2,1)} %weight_hbm_ref.7, s32[1,64]{1,0:T(1,128)} %bitcast.23, s32[1,64]{1,0:T(1,128)} %bitcast.24), custom_call_target="tpu_custom_call" | custom-call | flops 268435456 | bytes 2097152 | tf_op jit(solution)/shard_map/encode/pallas_call | solution.py:278
  4.4 0.0 copy-start.6
  4.4 0.0 copy-start.7
  4.4 0.0 copy-start
  4.4 0.0 copy-start.1
  4.4 7.5 %all-to-all-start = ((bf16[16,264,128]{2,1,0:T(8,128)(2,1)}), bf16[16,264,128]{2,1,0:T(8,128)(2,1)S(1)}, u32[]{:S(2)}, u32[]{:S(2)}) async-start(bf16[16,264,128]{2,1,0:T(8,128)(2,1)} %encode.1), calls=%async_computation | async-start | bytes 2162688 | tf_op jit(solution)/shard_map/all_to_all | solution.py:867
  11.9 0.0 copy-done.2
  11.9 0.0 copy-done.3
  11.9 0.0 copy-done.4
  11.9 0.0 copy-done.5
  11.9 5.2 %tables.1 = (bf16[4096,512]{1,0:T(8,128)(2,1)}, bf16[512,4096]{1,0:T(8,128)(2,1)}) custom-call(f32[64,512]{1,0:T(8,128)S(1)} %copy-done.2, f32[64,512]{1,0:T(8,128)S(1)} %copy-done.3, f32[64,512]{1,0:T(8,128)S(1)} %copy-done.4, f32[64,512]{1,0:T(8,128)S(1)} %copy-done.5), custom_call_target="tpu_custom_call" | custom-call | flops 8388608 | bytes 8388608 | tf_op jit(solution)/shard_map/tables/pallas_call | solution.py:159
  17.2 18.5 %all-to-all-done.got_ref = bf16[16,264,128]{2,1,0:T(8,128)(2,1)S(1)} async-done(((bf16[16,264,128]{2,1,0:T(8,128)(2,1)}), bf16[16,264,128]{2,1,0:T(8,128)(2,1)S(1)}, u32[]{:S(2)}, u32[]{:S(2)}) %all-to-all-start) | async-done | bytes 1081376 | tf_op jit(solution)/shard_map/all_to_all | solution.py:867
  35.7 0.0 copy-done.6
  35.7 0.0 copy-done.7
  35.7 1.3 pair_spectrum.1
  37.0 15.9 %all_to_all.30 = bf16[16,32,256]{2,1,0:T(8,128)(2,1)S(1)} all-to-all(bf16[16,32,256]{2,1,0:T(8,128)(2,1)S(1)} %bitcast.18), channel_id=1, replica_groups=mesh['groups'=2,'pen'=16] {'pen'}, dimensions={0} | all-to-all | bytes 524288 | tf_op jit(solution)/shard_map/all_to_all | solution.py:867
  52.9 0.0 copy-done
  52.9 0.0 copy-done.1
  52.9 4.1 %mix.2 = bf16[512,256]{1,0:T(8,128)(2,1)} custom-call(bf16[512,256]{1,0:T(8,128)(2,1)S(1)} %bitcast.14, bf16[128,64]{1,0:T(8,128)(2,1)S(1)} %copy-done.1, bf16[128,192]{1,0:T(8,128)(2,1)S(1)} %copy-done, bf16[2,16,16,64,128]{4,3,2,1,0:T(8,128)(2,1)} %weight_hbm_ref.6), custom_call_target="tpu_custom_call" | custom-call | flops 600000000 | bytes 4718592 | tf_op jit(solution)/shard_map/mix/pallas_call | solution.py:574
  57.1 3.9 %all-to-all-start.2 = ((bf16[16,32,256]{2,1,0:T(8,128)(2,1)}), bf16[16,32,256]{2,1,0:T(8,128)(2,1)S(1)}, u32[]{:S(2)}, u32[]{:S(2)}) async-start(bf16[16,32,256]{2,1,0:T(8,128)(2,1)} %bitcast.4), calls=%async_computation.2 | async-start | bytes 524288 | tf_op jit(solution)/shard_map/all_to_all | solution.py:867
  61.0 0.1 mul.22.spot_ref
  61.1 0.0 copy-start.8
  61.1 0.0 copy-start.9
  61.1 6.8 %scatter.1 = f32[16384,128]{1,0:T(8,128)} custom-call(s32[1024]{0:T(1024)S(1)} %mul.22.spot_ref, bf16[16,264,128]{2,1,0:T(8,128)(2,1)S(1)} %all-to-all-done.got_ref), custom_call_target="tpu_custom_call" | custom-call | flops 1000000 | bytes 33554432 | tf_op jit(solution)/shard_map/scatter/pallas_call | solution.py:659
  67.9 2.7 %all-to-all-done.2 = bf16[16,32,256]{2,1,0:T(8,128)(2,1)S(1)} async-done(((bf16[16,32,256]{2,1,0:T(8,128)(2,1)}), bf16[16,32,256]{2,1,0:T(8,128)(2,1)S(1)}, u32[]{:S(2)}, u32[]{:S(2)}) %all-to-all-start.2) | async-done | bytes 262176 | tf_op jit(solution)/shard_map/all_to_all | solution.py:867
  70.6 0.0 copy-done.8
  70.6 0.0 copy-done.9
  70.6 15.9 %layer.1 = (f32[2,8192,128]{2,1,0:T(8,128)}, bf16[512,256]{1,0:T(8,128)(2,1)S(1)}) custom-call(bf16[4096,512]{1,0:T(8,128)(2,1)} %get-tuple-element.15.table_ref, bf16[512,4096]{1,0:T(8,128)(2,1)} %get-tuple-element.16.flipped_ref, bf16[512,256]{1,0:T(8,128)(2,1)S(1)} %bitcast.15, f32[2,8192,128]{2,1,0:T(8,128)} %bitcast.22, ...), custom_call_target="tpu_custom_call" | custom-call | flops 6442450944 | bytes 16777216 | tf_op jit(solution)/shard_map/layer/pallas_call | solution.py:771
  86.5 12.8 %all_to_all.31 = bf16[16,32,256]{2,1,0:T(8,128)(2,1)S(1)} all-to-all(bf16[16,32,256]{2,1,0:T(8,128)(2,1)S(1)} %bitcast.17), channel_id=1, replica_groups=mesh['groups'=2,'pen'=16] {'pen'}, dimensions={0} | all-to-all | bytes 524288 | tf_op jit(solution)/shard_map/all_to_all | solution.py:867
  99.2 3.9 %mix.3 = bf16[512,256]{1,0:T(8,128)(2,1)} custom-call(bf16[512,256]{1,0:T(8,128)(2,1)S(1)} %bitcast.13, bf16[128,64]{1,0:T(8,128)(2,1)S(1)} %copy-done.1, bf16[128,192]{1,0:T(8,128)(2,1)S(1)} %copy-done, bf16[2,16,16,64,128]{4,3,2,1,0:T(8,128)(2,1)} %weight_hbm_ref.6), custom_call_target="tpu_custom_call" | custom-call | flops 600000000 | bytes 4718592 | tf_op jit(solution)/shard_map/mix/pallas_call | solution.py:574
  103.1 3.9 %all-to-all-start.4 = ((bf16[16,32,256]{2,1,0:T(8,128)(2,1)}), bf16[16,32,256]{2,1,0:T(8,128)(2,1)S(1)}, u32[]{:S(2)}, u32[]{:S(2)}) async-start(bf16[16,32,256]{2,1,0:T(8,128)(2,1)} %bitcast.10), calls=%async_computation.4 | async-start | bytes 524288 | tf_op jit(solution)/shard_map/all_to_all | solution.py:867
  107.1 2.7 %pair_phases.1.phase_ref = bf16[2048,512]{1,0:T(8,128)(2,1)} custom-call(bf16[16,264,128]{2,1,0:T(8,128)(2,1)S(1)} %all-to-all-done.got_ref, bf16[64,128]{1,0:T(8,128)(2,1)S(1)} %copy-done.6, bf16[64,64]{1,0:T(8,128)(2,1)S(1)} %copy-done.7), custom_call_target="tpu_custom_call" | custom-call | flops 1000000 | bytes 3178496 | tf_op jit(solution)/shard_map/pair_phases/pallas_call | solution.py:455
  109.8 4.9 %gather.1.grid_ref = f32[4096,128]{1,0:T(8,128)S(1)} custom-call(s32[1024]{0:T(1024)S(1)} %mul.22.spot_ref, f32[16384,128]{1,0:T(8,128)} %bitcast.21), custom_call_target="tpu_custom_call" | custom-call | flops 1000000 | bytes 16777216 | tf_op jit(solution)/shard_map/gather/pallas_call | solution.py:691
  114.7 2.0 %all-to-all-done.4 = bf16[16,32,256]{2,1,0:T(8,128)(2,1)S(1)} async-done(((bf16[16,32,256]{2,1,0:T(8,128)(2,1)}), bf16[16,32,256]{2,1,0:T(8,128)(2,1)S(1)}, u32[]{:S(2)}, u32[]{:S(2)}) %all-to-all-start.4) | async-done | bytes 262176 | tf_op jit(solution)/shard_map/all_to_all | solution.py:867
  116.7 5.3 %last_layer.1 = bf16[16,256,128]{2,1,0:T(8,128)(2,1)S(1)} custom-call(bf16[2048,512]{1,0:T(8,128)(2,1)} %pair_phases.1.phase_ref, bf16[512,256]{1,0:T(8,128)(2,1)S(1)} %bitcast.16, f32[4096,128]{1,0:T(8,128)S(1)} %gather.1.grid_ref, bf16[2,64,256]{2,1,0:T(8,128)(2,1)S(1)} %bitcast.20, bf16[2,64,256]{2,1,0:T(8,128)(2,1)S(1)} %copy-done.9), custom_call_target="tpu_custom_call" | custom-call | flops 2684354560 | bytes 5242880 | tf_op jit(solution)/shard_map/last_layer/pallas_call | solution.py:845
  121.9 29.2 %all_to_all.32.got_ref = bf16[16,256,128]{2,1,0:T(8,128)(2,1)S(1)} all-to-all(bf16[16,256,128]{2,1,0:T(8,128)(2,1)S(1)} %last_layer.1), channel_id=1, replica_groups=mesh['groups'=2,'pen'=16] {'pen'}, dimensions={0} | all-to-all | bytes 2097152 | tf_op jit(solution)/shard_map/all_to_all | solution.py:867
  151.1 3.3 %decode.1 = f32[64,2048]{1,0:T(8,128)} custom-call(bf16[16,256,128]{2,1,0:T(8,128)(2,1)S(1)} %all_to_all.32.got_ref, bf16[64,128,128]{2,1,0:T(8,128)(2,1)} %weight_hbm_ref.7), custom_call_target="tpu_custom_call" | custom-call | flops 268435456 | bytes 2097152 | tf_op jit(solution)/shard_map/decode/pallas_call | solution.py:354
  (2 shorter events, 0.0 us)
Async XLA Ops:
  0.0 11.9 %copy-start.2 = (f32[64,512]{1,0:T(8,128)S(1)}, f32[64,512]{1,0:T(8,128)}, u32[]{:S(2)}) copy-start(f32[64,512]{1,0:T(8,128)} %constant.20.clone.first_ref) | copy-start | bytes 393220
  0.0 11.9 %copy-start.3 = (f32[64,512]{1,0:T(8,128)S(1)}, f32[64,512]{1,0:T(8,128)}, u32[]{:S(2)}) copy-start(f32[64,512]{1,0:T(8,128)} %constant.21.clone.second_ref) | copy-start | bytes 393220
  0.0 11.9 %copy-start.4 = (f32[64,512]{1,0:T(8,128)S(1)}, f32[64,512]{1,0:T(8,128)}, u32[]{:S(2)}) copy-start(f32[64,512]{1,0:T(8,128)} %constant.22.clone.cos_ref) | copy-start | bytes 393220
  0.0 11.9 %copy-start.5 = (f32[64,512]{1,0:T(8,128)S(1)}, f32[64,512]{1,0:T(8,128)}, u32[]{:S(2)}) copy-start(f32[64,512]{1,0:T(8,128)} %constant.23.clone.sin_ref) | copy-start | bytes 393220
  4.4 31.3 %copy-start.6 = (bf16[64,128]{1,0:T(8,128)(2,1)S(1)}, bf16[64,128]{1,0:T(8,128)(2,1)}, u32[]{:S(2)}) copy-start(bf16[64,128]{1,0:T(8,128)(2,1)} %constant.32.x_ref) | copy-start | bytes 49156
  4.4 31.3 %copy-start.7 = (bf16[64,64]{1,0:T(8,128)(2,1)S(1)}, bf16[64,64]{1,0:T(8,128)(2,1)}, u32[]{:S(2)}) copy-start(bf16[64,64]{1,0:T(8,128)(2,1)} %constant.37.y_ref) | copy-start | bytes 24580
  4.4 48.5 %copy-start = (bf16[128,192]{1,0:T(8,128)(2,1)S(1)}, bf16[128,192]{1,0:T(8,128)(2,1)}, u32[]{:S(2)}) copy-start(bf16[128,192]{1,0:T(8,128)(2,1)} %constant.49.inverse_ref) | copy-start | bytes 147460
  4.4 48.5 %copy-start.1 = (bf16[128,64]{1,0:T(8,128)(2,1)S(1)}, bf16[128,64]{1,0:T(8,128)(2,1)}, u32[]{:S(2)}) copy-start(bf16[128,64]{1,0:T(8,128)(2,1)} %constant.43.forward_ref) | copy-start | bytes 49156
  4.4 31.2 %all-to-all-start = ((bf16[16,264,128]{2,1,0:T(8,128)(2,1)}), bf16[16,264,128]{2,1,0:T(8,128)(2,1)S(1)}, u32[]{:S(2)}, u32[]{:S(2)}) async-start(bf16[16,264,128]{2,1,0:T(8,128)(2,1)} %encode.1), calls=%async_computation | async-start | bytes 2162688 | tf_op jit(solution)/shard_map/all_to_all | solution.py:867
  57.1 13.5 %all-to-all-start.2 = ((bf16[16,32,256]{2,1,0:T(8,128)(2,1)}), bf16[16,32,256]{2,1,0:T(8,128)(2,1)S(1)}, u32[]{:S(2)}, u32[]{:S(2)}) async-start(bf16[16,32,256]{2,1,0:T(8,128)(2,1)} %bitcast.4), calls=%async_computation.2 | async-start | bytes 524288 | tf_op jit(solution)/shard_map/all_to_all | solution.py:867
  61.1 9.5 %copy-start.8 = (bf16[2,256,64]{1,2,0:T(8,128)(2,1)S(1)}, bf16[2,256,64]{1,2,0:T(8,128)(2,1)}, u32[]{:S(2)}) copy-start(bf16[2,256,64]{1,2,0:T(8,128)(2,1)} %param.20) | copy-start | bytes 196612
  61.1 9.5 %copy-start.9 = (bf16[2,64,256]{2,1,0:T(8,128)(2,1)S(1)}, bf16[2,64,256]{2,1,0:T(8,128)(2,1)}, u32[]{:S(2)}) copy-start(bf16[2,64,256]{2,1,0:T(8,128)(2,1)} %down_ref.3) | copy-start | bytes 196612
  103.1 13.5 %all-to-all-start.4 = ((bf16[16,32,256]{2,1,0:T(8,128)(2,1)}), bf16[16,32,256]{2,1,0:T(8,128)(2,1)S(1)}, u32[]{:S(2)}, u32[]{:S(2)}) async-start(bf16[16,32,256]{2,1,0:T(8,128)(2,1)} %bitcast.10), calls=%async_computation.4 | async-start | bytes 524288 | tf_op jit(solution)/shard_map/all_to_all | solution.py:867
